TPU v7x, 512 devices: a whole 4x8x8 slice. The times are simulated.
512 devices in a mesh: rep: 8 (over z_hi, core), ty: 16 (over z_lo, y), tx: 4 (over x).
Axes of the slice: x: 4, y: 8, z: 8 (z_hi: 4, z_lo: 2; z = z_hi * 2 + z_lo), core: 2. Of those that a mesh axis runs over, the one named last changes fastest.
Arguments:
- tokens: bfloat16 [8, 1024, 16, 512], P('rep', 'ty', 'tx'), may hold values from -160 to 160
- qkv_weight: bfloat16 [512, 1536], replicated, may hold values from -16 to 16
- cotangent: bfloat16 [8, 1024, 16, 512], P('rep', 'ty', 'tx'), may hold values from -6 to 6
Outputs:
- token_grad: bfloat16 [8, 1024, 16, 512], P('rep', 'ty', 'tx')
- weight_grad: float32 [512, 1536], P(('ty', 'tx'))
All inputs are finite; a program needn't handle non-finite values.
Results may differ from a plain program's by a relative error of at most 0.024.
Values may be sent and summed in bfloat16 or wider, within the bound.
A program may use at most 64 MiB of HBM per device.

v0:
```python
import jax
import jax.numpy as jnp
from jax import lax
from jax.sharding import PartitionSpec as P

HEADS = 16
HEAD_DIM = 32
GRID = 8


eps_norm = 1e-05


def normalize(values):
    center = values - jnp.mean(values, axis=-1, keepdims=True)
    inv_std = lax.rsqrt(jnp.mean(center * center, axis=-1, keepdims=True) + eps_norm)
    return (center * inv_std, inv_std)


def window_grads(window_x, window_g, qkv_weight):
    win_count, win_tokens, channels = window_x.shape
    standard, inv_std = normalize(window_x.astype(jnp.float32))
    normed = standard.astype(jnp.bfloat16).reshape(win_count * win_tokens, channels)
    projection = jnp.dot(normed, qkv_weight, preferred_element_type=jnp.float32)
    head_shape = (win_count, win_tokens, HEADS, HEAD_DIM)
    query_heads = (
        (projection[:, :channels] * HEAD_DIM ** (-0.5)).astype(jnp.bfloat16).reshape(head_shape)
    )
    key_heads = projection[:, channels : 2 * channels].astype(jnp.bfloat16).reshape(head_shape)
    value_heads = projection[:, 2 * channels :].astype(jnp.bfloat16).reshape(head_shape)
    scores = jnp.einsum(
        "wqne,wkne->wnqk", query_heads, key_heads, preferred_element_type=jnp.float32
    )
    peak_score = jnp.max(scores, axis=-1, keepdims=True)
    exponent = jnp.exp(scores - peak_score)
    attn_probs = exponent / jnp.sum(exponent, axis=-1, keepdims=True)
    probs_low = attn_probs.astype(jnp.bfloat16)
    grad_heads = window_g.reshape(head_shape)
    attn_grad = jnp.einsum(
        "wqne,wkne->wnqk", grad_heads, value_heads, preferred_element_type=jnp.float32
    )
    value_grad = jnp.einsum(
        "wnqk,wqne->wkne", probs_low, grad_heads, preferred_element_type=jnp.float32
    ).astype(jnp.bfloat16)
    score_grad = (
        attn_probs * (attn_grad - jnp.sum(attn_probs * attn_grad, axis=-1, keepdims=True))
    ).astype(jnp.bfloat16)
    query_grad = (
        jnp.einsum("wnqk,wkne->wqne", score_grad, key_heads, preferred_element_type=jnp.float32)
        * HEAD_DIM ** (-0.5)
    ).astype(jnp.bfloat16)
    key_grad = jnp.einsum(
        "wnqk,wqne->wkne", score_grad, query_heads, preferred_element_type=jnp.float32
    ).astype(jnp.bfloat16)
    flat_shape = (win_count * win_tokens, channels)
    proj_grad = jnp.concatenate(
        [
            query_grad.reshape(flat_shape),
            key_grad.reshape(flat_shape),
            value_grad.reshape(flat_shape),
        ],
        axis=1,
    )
    normed_grad = lax.dot_general(
        proj_grad, qkv_weight, (((1,), (1,)), ((), ())), preferred_element_type=jnp.float32
    )
    normed_grad = normed_grad.reshape(win_count, win_tokens, channels)
    weight_term = lax.dot_general(
        normed, proj_grad, (((0,), (0,)), ((), ())), preferred_element_type=jnp.float32
    )
    inner_term = (
        normed_grad
        - jnp.mean(normed_grad, axis=-1, keepdims=True)
        - standard * jnp.mean(normed_grad * standard, axis=-1, keepdims=True)
    )
    token_grad = (window_g.astype(jnp.float32) + inv_std * inner_term).astype(jnp.bfloat16)
    return (token_grad, weight_term)


def shards(tokens, qkv_weight, cotangent):
    rep_count = lax.axis_size("rep")
    row_tiles = lax.axis_size("ty")
    col_tiles = lax.axis_size("tx")
    tile_count = row_tiles * col_tiles
    tile_height = tokens.shape[1]
    tile_width = tokens.shape[2]
    channels = tokens.shape[3]
    stride_rows = row_tiles * tile_height // GRID
    stride_cols = col_tiles * tile_width // GRID
    block_rows = min(tile_height, stride_rows)
    fold_rows = stride_rows // block_rows
    col_groups = tile_width // stride_cols
    outer_rows = tile_height // block_rows
    inner_rows = block_rows // tile_count
    split_shape = (outer_rows, tile_count, inner_rows, tile_width, channels)
    grid_x, grid_g = (
        lax.all_to_all(
            tokens.reshape(split_shape), ("ty", "tx"), split_axis=1, concat_axis=1, tiled=True
        ),
        lax.all_to_all(
            cotangent.reshape(split_shape), ("ty", "tx"), split_axis=1, concat_axis=1, tiled=True
        ),
    )
    token_shape = (
        outer_rows,
        row_tiles // fold_rows,
        fold_rows,
        col_tiles,
        inner_rows,
        col_groups,
        stride_cols,
        channels,
    )
    win_count = fold_rows * inner_rows * stride_cols

    def to_windows(values):
        return (
            values.reshape(token_shape)
            .transpose(2, 4, 6, 1, 0, 3, 5, 7)
            .reshape(win_count, GRID * GRID, channels)
        )

    grad_windows, weight_term = window_grads(to_windows(grid_x), to_windows(grid_g), qkv_weight)
    back_shape = (
        fold_rows,
        inner_rows,
        stride_cols,
        row_tiles // fold_rows,
        outer_rows,
        col_tiles,
        col_groups,
        channels,
    )
    spread = grad_windows.reshape(back_shape).transpose(4, 3, 0, 5, 1, 6, 2, 7).reshape(split_shape)
    returned = lax.all_to_all(spread, ("ty", "tx"), split_axis=1, concat_axis=1, tiled=True)
    token_grad = returned.reshape(1, tile_height, tile_width, channels)
    partial_rows = lax.psum_scatter(weight_term, ("ty", "tx"), scatter_dimension=0, tiled=True)
    weight_grad = lax.psum(partial_rows, "rep")
    weight_grad = weight_grad / (rep_count * tile_count)
    return (token_grad, weight_grad)


def solution(mesh):
    placed = (P("rep", "ty", "tx", None), P(), P("rep", "ty", "tx", None))
    return jax.shard_map(
        shards,
        mesh=mesh,
        in_specs=placed,
        out_specs=(P("rep", "ty", "tx", None), P(("ty", "tx"), None)),
        check_vma=False,
    )
```

profile of v0, /device:TPU:64, one launch (start us, length us, event | category | flops | bytes accessed | tf_op | source)
XLA Modules:
  0.0 442.9 jit_solution(9360469959169387966)
XLA Ops:
  7.2 23.8 %all_to_all.15 = bf16[1,64,1,4,512]{4,3,2,0,1:T(4,128)(2,1)S(1)} all-to-all(bf16[1,64,1,4,512]{4,3,2,0,1:T(4,128)(2,1)} %bitcast.67), channel_id=1, replica_groups=mesh['rep'=8,'ty'=16,'tx'=4] {'ty','tx'}, dimensions={1} | all-to-all | bytes 524288 | tf_op jit(solution)/shard_map/all_to_all | solution.py:97
  31.0 6.1 %all-to-all-start = ((bf16[1,64,1,4,512]{4,3,2,0,1:T(4,128)(2,1)}), bf16[1,64,1,4,512]{4,3,2,0,1:T(4,128)(2,1)S(1)}, u32[]{:S(2)}, u32[]{:S(2)}) async-start(bf16[1,64,1,4,512]{4,3,2,0,1:T(4,128)(2,1)} %bitcast.68), calls=%async_computation | async-start | bytes 524288 | tf_op jit(solution)/shard_map/all_to_all | solution.py:100
  37.1 0.3 reshape.162
  37.4 0.4 fusion.27
  37.8 0.3 copy.89
  38.2 0.5 multiply_reduce_fusion.1
  38.9 9.4 %all-to-all-done = bf16[1,64,1,4,512]{4,3,2,0,1:T(4,128)(2,1)S(1)} async-done(((bf16[1,64,1,4,512]{4,3,2,0,1:T(4,128)(2,1)}), bf16[1,64,1,4,512]{4,3,2,0,1:T(4,128)(2,1)S(1)}, u32[]{:S(2)}, u32[]{:S(2)}) %all-to-all-start) | async-done | bytes 262176 | tf_op jit(solution)/shard_map/all_to_all | solution.py:100
  48.4 0.2 copy.90
  48.6 0.5 copy-done.1
  49.1 0.4 reshape.161
  49.5 1.5 reshape_reshape.3
  51.0 2.8 copy.45
  53.7 1.8 fusion.30
  55.5 0.7 fusion.29
  56.4 0.2 reshape.152
  56.6 1.1 copy.43
  57.7 1.1 reshape.154
  58.8 1.1 fusion.9
  59.9 0.8 copy.40
  60.7 2.0 reshape.153
  62.7 3.2 fusion.31
  66.0 2.5 fusion.6
  68.6 0.7 fusion.1
  69.3 0.7 fusion.3
  70.0 0.3 copy-done.2
  70.3 1.4 fusion.5
  71.7 1.2 fusion.7
  73.0 0.4 copy.54
  73.4 1.1 reshape.157
  74.4 1.4 copy.48
  75.9 1.0 reshape.155
  76.9 1.4 copy.51
  78.4 1.0 reshape.156
  79.4 1.0 constant_dynamic-update-slice_fusion.2
  80.4 1.0 constant_dynamic-update-slice_fusion.1
  81.4 1.0 constant_dynamic-update-slice_fusion
  82.3 2.4 fusion.23
  84.8 1.4 fusion.28
  86.2 0.2 div.40
  86.4 0.2 div.38
  86.5 1.4 reshape.158
  87.9 1.7 fusion.18
  89.6 0.3 copy.55
  90.0 17.0 %all_to_all.16 = bf16[1,64,1,4,512]{4,3,2,0,1:T(4,128)(2,1)S(1)} all-to-all(bf16[1,64,1,4,512]{4,3,2,0,1:T(4,128)(2,1)S(1)} %reshape.159), channel_id=1, replica_groups=mesh['rep'=8,'ty'=16,'tx'=4] {'ty','tx'}, dimensions={1} | all-to-all | bytes 524288 | tf_op jit(solution)/shard_map/all_to_all | solution.py:135
  107.0 298.6 %reduce-scatter.2.cloned.1.call-done = f32[8,1536]{1,0:T(8,128)} async-done(((f32[512,1536]{1,0:T(8,128)}), f32[8,1536]{1,0:T(8,128)}) %reduce-scatter.2.cloned.1.call-update) | async-done | bytes 49168 | tf_op jit(solution)/shard_map/reduce_scatter | solution.py:137
  405.6 29.2 %psum.7 = f32[8,1536]{1,0:T(8,128)S(1)} all-reduce(f32[8,1536]{1,0:T(8,128)} %reduce-scatter.2.cloned.1.call-done), channel_id=1, replica_groups=mesh['rep'=8,'ty'=16,'tx'=4] {'rep'}, use_global_device_ids=true, to_apply=%region_8.0 | all-reduce | flops 12288 | bytes 98304 | tf_op jit(solution)/shard_map/psum | solution.py:138
  434.7 0.6 broadcast_multiply_fusion.1
  435.4 0.7 copy.94
  (20 shorter events, 0.9 us)
Async XLA Ops:
  7.2 46.6 %copy-start = (bf16[512,1536]{1,0:T(8,128)(2,1)S(1)}, bf16[512,1536]{1,0:T(8,128)(2,1)}, u32[]{:S(2)}) copy-start(bf16[512,1536]{1,0:T(8,128)(2,1)} %param.4) | copy-start | bytes 4718596
  31.0 17.3 %all-to-all-start = ((bf16[1,64,1,4,512]{4,3,2,0,1:T(4,128)(2,1)}), bf16[1,64,1,4,512]{4,3,2,0,1:T(4,128)(2,1)S(1)}, u32[]{:S(2)}, u32[]{:S(2)}) async-start(bf16[1,64,1,4,512]{4,3,2,0,1:T(4,128)(2,1)} %bitcast.68), calls=%async_computation | async-start | bytes 524288 | tf_op jit(solution)/shard_map/all_to_all | solution.py:100
  37.0 368.5 %reduce-scatter.2.cloned.1.call-start = ((), (), s32[]{:S(2)}) async-start(), calls=%async_computation.4 | async-start | bytes 3194880 | tf_op jit(solution)/shard_map/reduce_scatter | solution.py:137
  48.4 0.7 copy-start.1
  66.0 2.5 copy-start.3
  66.0 2.5 copy-start.4
  66.0 2.6 copy-start.5
  69.3 1.0 copy-start.2
Sparse Core Ops, SparseCore 0:
  84.9 320.6 reduce-scatter.1
where the time goes:
time: 444 us; the launch traced here: 443 us
  waiting for transfers between devices  308 us (69%)
  blocking collectives  69.9 us (16%)
  local copies, waits for them, and re-layouts  24.9 us (6%)
  matrix products  14.6 us (3%)
  between operations  14.2 us (3%)
  starting transfers between devices  6.1 us (1%)
  other arithmetic  5.05 us (1%)
    reduce_scatter x1, waiting for transfers between devices, shards(): lax.psum_scatter(weight_term, ('ty', 'tx'), scatter_dimension=0, tiled=True)  299 us
    psum x1, blocking collectives, shards(): weight_grad = lax.psum(partial_rows, 'rep')  29.2 us
    all_to_all x1, blocking collectives, shards(): lax.all_to_all(tokens.reshape(split_shape), ('ty', 'tx'), split_axis=1, c...  23.8 us
    all_to_all x1, blocking collectives, shards(): lax.all_to_all(spread, ('ty', 'tx'), split_axis=1, concat_axis=1, tiled=T...  17 us
    all_to_all x1, waiting for transfers between devices, shards(): lax.all_to_all(cotangent.reshape(split_shape), ('ty', 'tx'), split_axis=1...  9.41 us
  transfers between devices with their start and end apart: 2, of which 2 were waited for; matrix products, arithmetic and copies ran while one was open for 2% of the time, Pallas kernels for 0%

commit v1 on v0

--- a/solution.py
+++ b/solution.py
@@ -134,7 +134,11 @@
     spread = grad_windows.reshape(back_shape).transpose(4, 3, 0, 5, 1, 6, 2, 7).reshape(split_shape)
     returned = lax.all_to_all(spread, ("ty", "tx"), split_axis=1, concat_axis=1, tiled=True)
     token_grad = returned.reshape(1, tile_height, tile_width, channels)
-    partial_rows = lax.psum_scatter(weight_term, ("ty", "tx"), scatter_dimension=0, tiled=True)
+    row_blocks = weight_term.reshape(tile_count, channels // tile_count, weight_term.shape[1])
+    gathered = lax.all_to_all(
+        row_blocks.astype(jnp.bfloat16), ("ty", "tx"), 0, 0, tiled=True
+    )
+    partial_rows = jnp.sum(gathered.astype(jnp.float32), axis=0)
     weight_grad = lax.psum(partial_rows, "rep")
     weight_grad = weight_grad / (rep_count * tile_count)
     return (token_grad, weight_grad)

time: 444 us -> 185 us (0.42)
  the two profiles are of different devices: /device:TPU:64 before, /device:TPU:8 now
where the time goes in v1:
time: 185 us; the launch traced here: 184 us
  waiting for transfers between devices  58.6 us (32%)
  blocking collectives  57.5 us (31%)
  local copies, waits for them, and re-layouts  31.3 us (17%)
  matrix products  14.8 us (8%)
  starting transfers between devices  14.7 us (8%)
  other arithmetic  5.9 us (3%)
    all_to_all x1, waiting for transfers between devices, shards(): lax.all_to_all(row_blocks.astype(jnp.bfloat16), ('ty', 'tx'), 0, 0, tiled...  37.9 us
    psum x1, blocking collectives, shards(): weight_grad = lax.psum(partial_rows, 'rep')  31.9 us
    all_to_all x1, blocking collectives, shards(): lax.all_to_all(tokens.reshape(split_shape), ('ty', 'tx'), split_axis=1, c...  25.6 us
    all_to_all x1, waiting for transfers between devices, shards(): lax.all_to_all(cotangent.reshape(split_shape), ('ty', 'tx'), split_axis=1...  10.6 us
    all_to_all x1, waiting for transfers between devices, shards(): lax.all_to_all(spread, ('ty', 'tx'), split_axis=1, concat_axis=1, tiled=T...  10.2 us
    another operation x2, local copies, waits for them, and re-layouts, window_grads(): grad_heads = window_g.reshape(head_shape)  5.44 us
    all_to_all x1, starting transfers between devices, shards(): lax.all_to_all(row_blocks.astype(jnp.bfloat16), ('ty', 'tx'), 0, 0, tiled...  4.94 us
    all_to_all x1, starting transfers between devices, shards(): lax.all_to_all(cotangent.reshape(split_shape), ('ty', 'tx'), split_axis=1...  4.92 us
  transfers between devices with their start and end apart: 3, of which 3 were waited for; matrix products, arithmetic and copies ran while one was open for 2% of the time, Pallas kernels for 0%

profile of v1, /device:TPU:8, one launch (start us, length us, event | category | flops | bytes accessed | tf_op | source)
XLA Modules:
  0.0 183.9 jit_solution(11110473066027474147)
XLA Ops:
  0.6 25.6 %all_to_all.20 = bf16[1,64,1,4,512]{4,3,2,0,1:T(4,128)(2,1)S(1)} all-to-all(bf16[1,64,1,4,512]{4,3,2,0,1:T(4,128)(2,1)} %bitcast.73), channel_id=1, replica_groups=mesh['rep'=8,'ty'=16,'tx'=4] {'ty','tx'}, dimensions={1} | all-to-all | bytes 524288 | tf_op jit(solution)/shard_map/all_to_all | solution.py:97
  26.3 4.9 %all-to-all-start = ((bf16[1,64,1,4,512]{4,3,2,0,1:T(4,128)(2,1)}), bf16[1,64,1,4,512]{4,3,2,0,1:T(4,128)(2,1)S(1)}, u32[]{:S(2)}, u32[]{:S(2)}) async-start(bf16[1,64,1,4,512]{4,3,2,0,1:T(4,128)(2,1)} %bitcast.74), calls=%async_computation | async-start | bytes 524288 | tf_op jit(solution)/shard_map/all_to_all | solution.py:100
  31.5 0.4 fusion.31
  31.9 0.3 copy.98
  32.3 0.5 multiply_reduce_fusion.1
  33.0 10.6 %all-to-all-done = bf16[1,64,1,4,512]{4,3,2,0,1:T(4,128)(2,1)S(1)} async-done(((bf16[1,64,1,4,512]{4,3,2,0,1:T(4,128)(2,1)}), bf16[1,64,1,4,512]{4,3,2,0,1:T(4,128)(2,1)S(1)}, u32[]{:S(2)}, u32[]{:S(2)}) %all-to-all-start) | async-done | bytes 262176 | tf_op jit(solution)/shard_map/all_to_all | solution.py:100
  43.7 0.9 copy.99
  44.6 0.4 reshape.163
  45.0 2.7 %reshape_reshape.3 = bf16[4,64,16,32]{3,2,1,0:T(8,128)(2,1)} reshape(bf16[2,1,2,8,1,4,2,512]{7,6,5,3,2,0,4,1:T(2,128)(2,1)} %bitcast.71) | data formatting | bytes 524288 | tf_op jit(solution)/shard_map/reshape;reshape | solution.py:38
  47.7 2.8 %copy.50 = bf16[4,64,16,32]{1,3,2,0:T(8,128)(2,1)} copy(bf16[4,64,16,32]{3,2,1,0:T(8,128)(2,1)} %reshape_reshape.3) | data formatting | bytes 524288 | tf_op jit(solution)/shard_map/reshape;reshape | solution.py:38
  50.4 1.8 fusion.34
  52.2 0.7 fusion.33
  53.0 1.1 copy.48
  54.0 1.1 reshape.156
  55.1 0.8 copy.44
  56.0 1.2 reshape.154
  57.2 1.8 fusion.10
  59.0 1.8 copy.45
  60.8 2.0 %reshape.155 = bf16[4,64,16,32]{1,0,3,2:T(4,128)(2,1)} reshape(bf16[256,512]{0,1:T(8,128)(2,1)} %copy.45) | data formatting | bytes 524288 | tf_op jit(solution)/shard_map/reshape | solution.py:27
  62.8 3.8 %fusion.35 = (f32[4,16,64]{2,1,0:T(8,128)}, f32[4,16,64,64]{2,3,1,0:T(8,128)}) fusion(bf16[4,64,16,32]{1,0,3,2:T(4,128)(2,1)S(1)} %reshape.154, bf16[4,64,16,32]{1,0,3,2:T(4,128)(2,1)} %reshape.155), kind=kOutput, calls=%fused_computation.52 | convolution fusion | flops 17301568 | bytes 1589248 | tf_op jit(solution)/shard_map/sub | solution.py:35
  66.6 2.5 %fusion.6 = bf16[4,64,16,32]{1,3,2,0:T(8,128)(2,1)S(1)} fusion(bf16[4,64,16,32]{1,3,2,0:T(8,128)(2,1)} %copy.50, f32[4,16,64,64]{2,3,1,0:T(8,128)} %get-tuple-element.10, f32[4,16,64]{2,1,0:T(8,128)} %get-tuple-element.9), kind=kOutput, calls=%fused_computation.14 | convolution fusion | flops 17432576 | bytes 1589248 | tf_op jit(solution)/shard_map/wnqk,wqne->wkne/dot_general | solution.py:42
  69.3 0.6 fusion.1
  69.9 0.7 fusion.3
  70.6 0.4 copy-done.1
  70.9 1.4 fusion.5
  72.4 1.2 fusion.7
  73.6 0.4 copy.59
  74.0 1.0 reshape.159
  75.1 1.8 copy.62
  76.9 1.4 copy.53
  78.3 1.0 reshape.157
  79.4 1.8 copy.60
  81.2 1.4 copy.56
  82.6 1.0 reshape.158
  83.7 1.8 copy.61
  85.5 1.7 fusion.19
  87.2 0.9 fusion.32
  88.0 0.3 reshape.160
  88.7 0.8 fusion.21
  89.8 0.8 reshape.161
  90.6 4.9 %all-to-all-start.2 = ((bf16[1,64,1,4,512]{4,3,2,0,1:T(4,128)(2,1)}), bf16[1,64,1,4,512]{4,3,2,0,1:T(4,128)(2,1)S(1)}, u32[]{:S(2)}, u32[]{:S(2)}) async-start(bf16[1,64,1,4,512]{4,3,2,0,1:T(4,128)(2,1)} %reshape.161), calls=%async_computation.2 | async-start | bytes 524288 | tf_op jit(solution)/shard_map/all_to_all | solution.py:135
  95.7 1.7 convolution_convert_fusion
  97.4 10.2 %all-to-all-done.2 = bf16[1,64,1,4,512]{4,3,2,0,1:T(4,128)(2,1)S(1)} async-done(((bf16[1,64,1,4,512]{4,3,2,0,1:T(4,128)(2,1)}), bf16[1,64,1,4,512]{4,3,2,0,1:T(4,128)(2,1)S(1)}, u32[]{:S(2)}, u32[]{:S(2)}) %all-to-all-start.2) | async-done | bytes 262176 | tf_op jit(solution)/shard_map/all_to_all | solution.py:135
  107.6 4.9 %all-to-all-start.3 = ((bf16[64,8,1536]{2,1,0:T(8,128)(2,1)}), bf16[64,8,1536]{2,1,0:T(8,128)(2,1)S(1)}, u32[]{:S(2)}, u32[]{:S(2)}) async-start(bf16[64,8,1536]{2,1,0:T(8,128)(2,1)} %convolution_convert_fusion), calls=%async_computation.3 | async-start | bytes 3145728 | tf_op jit(solution)/shard_map/all_to_all | solution.py:138
  112.5 37.9 %all-to-all-done.3 = bf16[64,8,1536]{2,1,0:T(8,128)(2,1)S(1)} async-done(((bf16[64,8,1536]{2,1,0:T(8,128)(2,1)}), bf16[64,8,1536]{2,1,0:T(8,128)(2,1)S(1)}, u32[]{:S(2)}, u32[]{:S(2)}) %all-to-all-start.3) | async-done | bytes 1572896 | tf_op jit(solution)/shard_map/all_to_all | solution.py:138
  150.6 31.9 %psum.7 = f32[8,1536]{1,0:T(8,128)S(1)} all-reduce(f32[8,1536]{1,0:T(8,128)S(1)} %convert_reduce_fusion), channel_id=1, replica_groups=mesh['rep'=8,'ty'=16,'tx'=4] {'rep'}, use_global_device_ids=true, to_apply=%region_8.0 | all-reduce | flops 12288 | bytes 98304 | tf_op jit(solution)/shard_map/psum | solution.py:142
  182.5 0.6 broadcast_multiply_fusion.1
  183.2 0.7 copy.101
  (31 shorter events, 1.8 us)
Async XLA Ops:
  0.6 49.8 %copy-start = (bf16[512,1536]{1,0:T(8,128)(2,1)S(1)}, bf16[512,1536]{1,0:T(8,128)(2,1)}, u32[]{:S(2)}) copy-start(bf16[512,1536]{1,0:T(8,128)(2,1)} %param.4) | copy-start | bytes 4718596
  26.3 17.4 %all-to-all-start = ((bf16[1,64,1,4,512]{4,3,2,0,1:T(4,128)(2,1)}), bf16[1,64,1,4,512]{4,3,2,0,1:T(4,128)(2,1)S(1)}, u32[]{:S(2)}, u32[]{:S(2)}) async-start(bf16[1,64,1,4,512]{4,3,2,0,1:T(4,128)(2,1)} %bitcast.74), calls=%async_computation | async-start | bytes 524288 | tf_op jit(solution)/shard_map/all_to_all | solution.py:100
  66.6 2.5 %copy-start.2 = (f32[4,16,64,64]{2,3,1,0:T(8,128)S(1)}, f32[4,16,64,64]{2,3,1,0:T(8,128)}, u32[]{:S(2)}) copy-start(f32[4,16,64,64]{2,3,1,0:T(8,128)} %get-tuple-element.10) | copy-start | bytes 3145732
  66.6 2.5 %copy-start.4 = (bf16[4,64,16,32]{1,3,2,0:T(8,128)(2,1)S(1)}, bf16[4,64,16,32]{1,3,2,0:T(8,128)(2,1)}, u32[]{:S(2)}) copy-start(bf16[4,64,16,32]{1,3,2,0:T(8,128)(2,1)} %copy.50) | copy-start | bytes 786436
  66.6 2.6 %copy-start.5 = (bf16[4,64,16,32]{1,0,3,2:T(4,128)(2,1)S(1)}, bf16[4,64,16,32]{1,0,3,2:T(4,128)(2,1)}, u32[]{:S(2)}) copy-start(bf16[4,64,16,32]{1,0,3,2:T(4,128)(2,1)} %reshape.156) | copy-start | bytes 786436
  66.6 2.6 %copy-start.9 = (f32[4,16,64]{2,1,0:T(8,128)S(1)}, f32[4,16,64]{2,1,0:T(8,128)}, u32[]{:S(2)}) copy-start(f32[4,16,64]{2,1,0:T(8,128)} %get-tuple-element.9) | copy-start | bytes 49156
  69.9 1.0 copy-start.1
  88.4 7.2 %copy-start.3 = (bf16[512,256]{0,1:T(8,128)(2,1)S(1)}, bf16[512,256]{0,1:T(8,128)(2,1)}, u32[]{:S(2)}) copy-start(bf16[512,256]{0,1:T(8,128)(2,1)} %get-tuple-element.6) | copy-start | bytes 786436
  89.5 6.2 %copy-start.6 = (bf16[256,512]{1,0:T(8,128)(2,1)S(1)}, bf16[256,512]{1,0:T(8,128)(2,1)}, u32[]{:S(2)}) copy-start(bf16[256,512]{1,0:T(8,128)(2,1)} %copy.62) | copy-start | bytes 786436
  89.5 6.2 %copy-start.7 = (bf16[256,512]{1,0:T(8,128)(2,1)S(1)}, bf16[256,512]{1,0:T(8,128)(2,1)}, u32[]{:S(2)}) copy-start(bf16[256,512]{1,0:T(8,128)(2,1)} %copy.60) | copy-start | bytes 786436
  89.5 6.2 %copy-start.8 = (bf16[256,512]{1,0:T(8,128)(2,1)S(1)}, bf16[256,512]{1,0:T(8,128)(2,1)}, u32[]{:S(2)}) copy-start(bf16[256,512]{1,0:T(8,128)(2,1)} %copy.61) | copy-start | bytes 786436
  90.6 17.0 %all-to-all-start.2 = ((bf16[1,64,1,4,512]{4,3,2,0,1:T(4,128)(2,1)}), bf16[1,64,1,4,512]{4,3,2,0,1:T(4,128)(2,1)S(1)}, u32[]{:S(2)}, u32[]{:S(2)}) async-start(bf16[1,64,1,4,512]{4,3,2,0,1:T(4,128)(2,1)} %reshape.161), calls=%async_computation.2 | async-start | bytes 524288 | tf_op jit(solution)/shard_map/all_to_all | solution.py:135
  107.6 42.8 %all-to-all-start.3 = ((bf16[64,8,1536]{2,1,0:T(8,128)(2,1)}), bf16[64,8,1536]{2,1,0:T(8,128)(2,1)S(1)}, u32[]{:S(2)}, u32[]{:S(2)}) async-start(bf16[64,8,1536]{2,1,0:T(8,128)(2,1)} %convolution_convert_fusion), calls=%async_computation.3 | async-start | bytes 3145728 | tf_op jit(solution)/shard_map/all_to_all | solution.py:138

commit v2 on v1

--- a/solution.py
+++ b/solution.py
@@ -1,6 +1,10 @@
+import functools
+
 import jax
 import jax.numpy as jnp
 from jax import lax
+from jax.experimental import pallas as pl
+from jax.experimental.pallas import tpu as pltpu
 from jax.sharding import PartitionSpec as P
 
 HEADS = 16
@@ -75,6 +79,58 @@
     )
     token_grad = (window_g.astype(jnp.float32) + inv_std * inner_term).astype(jnp.bfloat16)
     return (token_grad, weight_term)
+
+
+def rep_sum_kernel(rep_count, part_ref, out_ref, held, copy_sems, send_sems, recv_sems):
+    me = lax.axis_index("rep")
+    row = lax.axis_index("ty")
+    col = lax.axis_index("tx")
+    barrier = pltpu.get_barrier_semaphore()
+    for step in range(1, rep_count):
+        peer = lax.rem(me + step, rep_count)
+        pl.semaphore_signal(
+            barrier, inc=1, device_id=(peer, row, col), device_id_type=pl.DeviceIdType.MESH
+        )
+    pl.semaphore_wait(barrier, rep_count - 1)
+    own = pltpu.make_async_copy(part_ref, held.at[me], copy_sems.at[0])
+    own.start()
+    copies = []
+    for step in range(1, rep_count):
+        peer = lax.rem(me + step, rep_count)
+        copy = pltpu.make_async_remote_copy(
+            src_ref=part_ref,
+            dst_ref=held.at[me],
+            send_sem=send_sems.at[step],
+            recv_sem=recv_sems.at[step],
+            device_id=(peer, row, col),
+            device_id_type=pl.DeviceIdType.MESH,
+        )
+        copy.start()
+        copies.append(copy)
+    own.wait()
+    for copy in copies:
+        copy.wait()
+    total = held[0]
+    for source in range(1, rep_count):
+        total = total + held[source]
+    out_ref[...] = total
+
+
+def rep_sum(partial_rows):
+    rep_count = lax.axis_size("rep")
+    return pl.pallas_call(
+        functools.partial(rep_sum_kernel, rep_count),
+        out_shape=jax.ShapeDtypeStruct(partial_rows.shape, partial_rows.dtype),
+        in_specs=[pl.BlockSpec(memory_space=pltpu.VMEM)],
+        out_specs=pl.BlockSpec(memory_space=pltpu.VMEM),
+        scratch_shapes=[
+            pltpu.VMEM((rep_count,) + partial_rows.shape, partial_rows.dtype),
+            pltpu.SemaphoreType.DMA((1,)),
+            pltpu.SemaphoreType.DMA((rep_count,)),
+            pltpu.SemaphoreType.DMA((rep_count,)),
+        ],
+        compiler_params=pltpu.CompilerParams(collective_id=0, has_side_effects=True),
+    )(partial_rows)
 
 
 def shards(tokens, qkv_weight, cotangent):
@@ -139,7 +195,7 @@
         row_blocks.astype(jnp.bfloat16), ("ty", "tx"), 0, 0, tiled=True
     )
     partial_rows = jnp.sum(gathered.astype(jnp.float32), axis=0)
-    weight_grad = lax.psum(partial_rows, "rep")
+    weight_grad = rep_sum(partial_rows)
     weight_grad = weight_grad / (rep_count * tile_count)
     return (token_grad, weight_grad)
 

time: 185 us -> 177 us (0.957)
  the two profiles are of different devices: /device:TPU:8 before, /device:TPU:9 now
where the time goes in v2:
time: 177 us; the launch traced here: 175 us
  waiting for transfers between devices  54.7 us (31%)
  local copies, waits for them, and re-layouts  31.3 us (18%)
  Pallas kernels  26.1 us (15%)
  blocking collectives  23.8 us (13%)
  starting transfers between devices  16.5 us (9%)
  matrix products  14.8 us (8%)
  other arithmetic  7.32 us (4%)
    all_to_all x1, waiting for transfers between devices, shards(): lax.all_to_all(row_blocks.astype(jnp.bfloat16), ('ty', 'tx'), 0, 0, tiled...  36.5 us
    pallas_call x1, Pallas kernels, rep_sum(): pl.pallas_call(functools.partial(rep_sum_kernel, rep_count), out_shape=ja...  26.1 us
    all_to_all x1, blocking collectives, shards(): lax.all_to_all(tokens.reshape(split_shape), ('ty', 'tx'), split_axis=1, c...  23.8 us
    all_to_all x1, waiting for transfers between devices, shards(): lax.all_to_all(cotangent.reshape(split_shape), ('ty', 'tx'), split_axis=1...  9.12 us
    all_to_all x1, waiting for transfers between devices, shards(): lax.all_to_all(spread, ('ty', 'tx'), split_axis=1, concat_axis=1, tiled=T...  9.08 us
    all_to_all x1, starting transfers between devices, shards(): lax.all_to_all(spread, ('ty', 'tx'), split_axis=1, concat_axis=1, tiled=T...  6.09 us
    all_to_all x1, starting transfers between devices, shards(): lax.all_to_all(cotangent.reshape(split_shape), ('ty', 'tx'), split_axis=1...  5.5 us
    another operation x2, local copies, waits for them, and re-layouts, window_grads(): grad_heads = window_g.reshape(head_shape)  5.44 us
  transfers between devices with their start and end apart: 3, of which 3 were waited for; matrix products, arithmetic and copies ran while one was open for 2% of the time, Pallas kernels for 0%

profile of v2, /device:TPU:9, one launch (start us, length us, event | category | flops | bytes accessed | tf_op | source)
XLA Modules:
  0.0 175.5 jit_solution(14786663867328237837)
XLA Ops:
  0.6 23.8 %all_to_all.20 = bf16[1,64,1,4,512]{4,3,2,0,1:T(4,128)(2,1)S(1)} all-to-all(bf16[1,64,1,4,512]{4,3,2,0,1:T(4,128)(2,1)} %bitcast.73), channel_id=1, replica_groups=mesh['rep'=8,'ty'=16,'tx'=4] {'ty','tx'}, dimensions={1} | all-to-all | bytes 524288 | tf_op jit(solution)/shard_map/all_to_all | solution.py:153
  24.4 5.5 %all-to-all-start = ((bf16[1,64,1,4,512]{4,3,2,0,1:T(4,128)(2,1)}), bf16[1,64,1,4,512]{4,3,2,0,1:T(4,128)(2,1)S(1)}, u32[]{:S(2)}, u32[]{:S(2)}) async-start(bf16[1,64,1,4,512]{4,3,2,0,1:T(4,128)(2,1)} %bitcast.74), calls=%async_computation | async-start | bytes 524288 | tf_op jit(solution)/shard_map/all_to_all | solution.py:156
  30.2 0.4 fusion.31
  31.1 0.5 multiply_reduce_fusion.1
  31.8 9.1 %all-to-all-done = bf16[1,64,1,4,512]{4,3,2,0,1:T(4,128)(2,1)S(1)} async-done(((bf16[1,64,1,4,512]{4,3,2,0,1:T(4,128)(2,1)}), bf16[1,64,1,4,512]{4,3,2,0,1:T(4,128)(2,1)S(1)}, u32[]{:S(2)}, u32[]{:S(2)}) %all-to-all-start) | async-done | bytes 262176 | tf_op jit(solution)/shard_map/all_to_all | solution.py:156
  41.0 0.9 copy.99
  41.9 0.4 reshape.163
  42.2 2.7 %reshape_reshape.3 = bf16[4,64,16,32]{3,2,1,0:T(8,128)(2,1)} reshape(bf16[2,1,2,8,1,4,2,512]{7,6,5,3,2,0,4,1:T(2,128)(2,1)} %bitcast.71) | data formatting | bytes 524288 | tf_op jit(solution)/shard_map/reshape;reshape | solution.py:42
  44.9 2.8 %copy.50 = bf16[4,64,16,32]{1,3,2,0:T(8,128)(2,1)} copy(bf16[4,64,16,32]{3,2,1,0:T(8,128)(2,1)} %reshape_reshape.3) | data formatting | bytes 524288 | tf_op jit(solution)/shard_map/reshape;reshape | solution.py:42
  47.7 1.8 %fusion.34 = (bf16[256,1536]{1,0:T(8,128)(2,1)S(1)}, f32[256,1536]{1,0:T(8,128)}) fusion(bf16[512,1536]{1,0:T(8,128)(2,1)S(1)} %copy-done, f32[256,512]{1,0:T(8,128)S(1)} %reshape.163, f32[256]{0:T(256)S(1)} %rsqrt.13, f32[256]{0:T(256)S(1)} %div.34), kind=kOutput, calls=%fused_computation.51 | convolution fusion | flops 403439616 | bytes 4458496 | tf_op jit(solution)/shard_map/dot_general | solution.py:28
  49.5 0.7 fusion.33
  50.2 1.1 copy.48
  51.3 1.1 reshape.156
  52.3 0.8 copy.44
  53.2 1.2 reshape.154
  54.4 1.8 %fusion.10 = bf16[256,512]{1,0:T(8,128)(2,1)} fusion(f32[256,1536]{1,0:T(8,128)} %get-tuple-element.8), kind=kLoop, calls=%fused_computation.21 | loop fusion | flops 262144 | bytes 786432 | tf_op jit(solution)/shard_map/convert_element_type | solution.py:31
  56.2 1.8 %copy.45 = bf16[256,512]{0,1:T(8,128)(2,1)} copy(bf16[256,512]{1,0:T(8,128)(2,1)} %fusion.10) | data formatting | bytes 524288 | tf_op jit(solution)/shard_map/convert_element_type | solution.py:31
  58.0 2.0 %reshape.155 = bf16[4,64,16,32]{1,0,3,2:T(4,128)(2,1)} reshape(bf16[256,512]{0,1:T(8,128)(2,1)} %copy.45) | data formatting | bytes 524288 | tf_op jit(solution)/shard_map/reshape | solution.py:31
  60.0 3.8 %fusion.35 = (f32[4,16,64]{2,1,0:T(8,128)}, f32[4,16,64,64]{2,3,1,0:T(8,128)}) fusion(bf16[4,64,16,32]{1,0,3,2:T(4,128)(2,1)S(1)} %reshape.154, bf16[4,64,16,32]{1,0,3,2:T(4,128)(2,1)} %reshape.155), kind=kOutput, calls=%fused_computation.52 | convolution fusion | flops 17301568 | bytes 1589248 | tf_op jit(solution)/shard_map/sub | solution.py:39
  63.9 2.5 %fusion.6 = bf16[4,64,16,32]{1,3,2,0:T(8,128)(2,1)S(1)} fusion(bf16[4,64,16,32]{1,3,2,0:T(8,128)(2,1)} %copy.50, f32[4,16,64,64]{2,3,1,0:T(8,128)} %get-tuple-element.10, f32[4,16,64]{2,1,0:T(8,128)} %get-tuple-element.9), kind=kOutput, calls=%fused_computation.14 | convolution fusion | flops 17432576 | bytes 1589248 | tf_op jit(solution)/shard_map/wnqk,wqne->wkne/dot_general | solution.py:46
  66.5 0.6 fusion.1
  67.1 0.7 fusion.3
  67.8 0.4 copy-done.1
  68.2 1.4 fusion.5
  69.6 1.2 fusion.7
  70.9 0.4 copy.59
  71.3 1.0 reshape.159
  72.3 1.8 %copy.62 = bf16[256,512]{1,0:T(8,128)(2,1)} copy(bf16[256,512]{0,1:T(8,128)(2,1)} %reshape.159) | data formatting | bytes 524288 | tf_op jit(solution)/shard_map/reshape | solution.py:64
  74.1 1.4 copy.53
  75.6 1.0 reshape.157
  76.6 1.8 %copy.60 = bf16[256,512]{1,0:T(8,128)(2,1)} copy(bf16[256,512]{0,1:T(8,128)(2,1)} %reshape.157) | data formatting | bytes 524288 | tf_op jit(solution)/shard_map/reshape | solution.py:62
  78.4 1.4 copy.56
  79.9 1.0 reshape.158
  80.9 1.8 %copy.61 = bf16[256,512]{1,0:T(8,128)(2,1)} copy(bf16[256,512]{0,1:T(8,128)(2,1)} %reshape.158) | data formatting | bytes 524288 | tf_op jit(solution)/shard_map/reshape | solution.py:63
  82.7 1.7 fusion.19
  84.4 0.9 fusion.32
  85.3 0.3 reshape.160
  86.0 0.8 fusion.21
  87.0 0.8 reshape.161
  87.8 6.1 %all-to-all-start.2 = ((bf16[1,64,1,4,512]{4,3,2,0,1:T(4,128)(2,1)}), bf16[1,64,1,4,512]{4,3,2,0,1:T(4,128)(2,1)S(1)}, u32[]{:S(2)}, u32[]{:S(2)}) async-start(bf16[1,64,1,4,512]{4,3,2,0,1:T(4,128)(2,1)} %reshape.161), calls=%async_computation.2 | async-start | bytes 524288 | tf_op jit(solution)/shard_map/all_to_all | solution.py:191
  94.1 1.7 convolution_convert_fusion
  95.8 9.1 %all-to-all-done.2 = bf16[1,64,1,4,512]{4,3,2,0,1:T(4,128)(2,1)S(1)} async-done(((bf16[1,64,1,4,512]{4,3,2,0,1:T(4,128)(2,1)}), bf16[1,64,1,4,512]{4,3,2,0,1:T(4,128)(2,1)S(1)}, u32[]{:S(2)}, u32[]{:S(2)}) %all-to-all-start.2) | async-done | bytes 262176 | tf_op jit(solution)/shard_map/all_to_all | solution.py:191
  104.9 4.9 %all-to-all-start.3 = ((bf16[64,8,1536]{2,1,0:T(8,128)(2,1)}), bf16[64,8,1536]{2,1,0:T(8,128)(2,1)S(1)}, u32[]{:S(2)}, u32[]{:S(2)}) async-start(bf16[64,8,1536]{2,1,0:T(8,128)(2,1)} %convolution_convert_fusion), calls=%async_computation.3 | async-start | bytes 3145728 | tf_op jit(solution)/shard_map/all_to_all | solution.py:194
  109.9 36.5 %all-to-all-done.3 = bf16[64,8,1536]{2,1,0:T(8,128)(2,1)S(1)} async-done(((bf16[64,8,1536]{2,1,0:T(8,128)(2,1)}), bf16[64,8,1536]{2,1,0:T(8,128)(2,1)S(1)}, u32[]{:S(2)}, u32[]{:S(2)}) %all-to-all-start.3) | async-done | bytes 1572896 | tf_op jit(solution)/shard_map/all_to_all | solution.py:194
  146.4 0.9 convert_reduce_fusion.part_ref
  147.2 26.1 %shard_map.50 = f32[8,1536]{1,0:T(8,128)} custom-call(f32[8,1536]{1,0:T(8,128)} %convert_reduce_fusion.part_ref), custom_call_target="tpu_custom_call" | custom-call | tf_op jit(solution)/shard_map/pallas_call | solution.py:121
  173.3 1.4 broadcast_multiply_fusion.1
  174.8 0.7 copy.101
  (31 shorter events, 1.9 us)
Async XLA Ops:
  0.6 47.1 %copy-start = (bf16[512,1536]{1,0:T(8,128)(2,1)S(1)}, bf16[512,1536]{1,0:T(8,128)(2,1)}, u32[]{:S(2)}) copy-start(bf16[512,1536]{1,0:T(8,128)(2,1)} %param.4) | copy-start | bytes 4718596
  24.4 16.4 %all-to-all-start = ((bf16[1,64,1,4,512]{4,3,2,0,1:T(4,128)(2,1)}), bf16[1,64,1,4,512]{4,3,2,0,1:T(4,128)(2,1)S(1)}, u32[]{:S(2)}, u32[]{:S(2)}) async-start(bf16[1,64,1,4,512]{4,3,2,0,1:T(4,128)(2,1)} %bitcast.74), calls=%async_computation | async-start | bytes 524288 | tf_op jit(solution)/shard_map/all_to_all | solution.py:156
  63.9 2.5 %copy-start.2 = (f32[4,16,64,64]{2,3,1,0:T(8,128)S(1)}, f32[4,16,64,64]{2,3,1,0:T(8,128)}, u32[]{:S(2)}) copy-start(f32[4,16,64,64]{2,3,1,0:T(8,128)} %get-tuple-element.10) | copy-start | bytes 3145732
  63.9 2.5 %copy-start.4 = (bf16[4,64,16,32]{1,3,2,0:T(8,128)(2,1)S(1)}, bf16[4,64,16,32]{1,3,2,0:T(8,128)(2,1)}, u32[]{:S(2)}) copy-start(bf16[4,64,16,32]{1,3,2,0:T(8,128)(2,1)} %copy.50) | copy-start | bytes 786436
  63.9 2.6 %copy-start.5 = (bf16[4,64,16,32]{1,0,3,2:T(4,128)(2,1)S(1)}, bf16[4,64,16,32]{1,0,3,2:T(4,128)(2,1)}, u32[]{:S(2)}) copy-start(bf16[4,64,16,32]{1,0,3,2:T(4,128)(2,1)} %reshape.156) | copy-start | bytes 786436
  63.9 2.6 %copy-start.9 = (f32[4,16,64]{2,1,0:T(8,128)S(1)}, f32[4,16,64]{2,1,0:T(8,128)}, u32[]{:S(2)}) copy-start(f32[4,16,64]{2,1,0:T(8,128)} %get-tuple-element.9) | copy-start | bytes 49156
  67.1 1.0 copy-start.1
  85.6 8.3 %copy-start.3 = (bf16[512,256]{0,1:T(8,128)(2,1)S(1)}, bf16[512,256]{0,1:T(8,128)(2,1)}, u32[]{:S(2)}) copy-start(bf16[512,256]{0,1:T(8,128)(2,1)} %get-tuple-element.6) | copy-start | bytes 786436
  86.7 7.4 %copy-start.6 = (bf16[256,512]{1,0:T(8,128)(2,1)S(1)}, bf16[256,512]{1,0:T(8,128)(2,1)}, u32[]{:S(2)}) copy-start(bf16[256,512]{1,0:T(8,128)(2,1)} %copy.62) | copy-start | bytes 786436
  86.7 7.4 %copy-start.7 = (bf16[256,512]{1,0:T(8,128)(2,1)S(1)}, bf16[256,512]{1,0:T(8,128)(2,1)}, u32[]{:S(2)}) copy-start(bf16[256,512]{1,0:T(8,128)(2,1)} %copy.60) | copy-start | bytes 786436
  86.7 7.4 %copy-start.8 = (bf16[256,512]{1,0:T(8,128)(2,1)S(1)}, bf16[256,512]{1,0:T(8,128)(2,1)}, u32[]{:S(2)}) copy-start(bf16[256,512]{1,0:T(8,128)(2,1)} %copy.61) | copy-start | bytes 786436
  87.8 17.1 %all-to-all-start.2 = ((bf16[1,64,1,4,512]{4,3,2,0,1:T(4,128)(2,1)}), bf16[1,64,1,4,512]{4,3,2,0,1:T(4,128)(2,1)S(1)}, u32[]{:S(2)}, u32[]{:S(2)}) async-start(bf16[1,64,1,4,512]{4,3,2,0,1:T(4,128)(2,1)} %reshape.161), calls=%async_computation.2 | async-start | bytes 524288 | tf_op jit(solution)/shard_map/all_to_all | solution.py:191
  104.9 41.4 %all-to-all-start.3 = ((bf16[64,8,1536]{2,1,0:T(8,128)(2,1)}), bf16[64,8,1536]{2,1,0:T(8,128)(2,1)S(1)}, u32[]{:S(2)}, u32[]{:S(2)}) async-start(bf16[64,8,1536]{2,1,0:T(8,128)(2,1)} %convolution_convert_fusion), calls=%async_computation.3 | async-start | bytes 3145728 | tf_op jit(solution)/shard_map/all_to_all | solution.py:194

commit v3 on v0

--- a/solution.py
+++ b/solution.py
@@ -1,6 +1,10 @@
+import functools
+
 import jax
 import jax.numpy as jnp
 from jax import lax
+from jax.experimental import pallas as pl
+from jax.experimental.pallas import tpu as pltpu
 from jax.sharding import PartitionSpec as P
 
 HEADS = 16
@@ -75,6 +79,112 @@
     )
     token_grad = (window_g.astype(jnp.float32) + inv_std * inner_term).astype(jnp.bfloat16)
     return (token_grad, weight_term)
+
+
+def weight_sum_kernel(rep_count, tile_count, col_tiles, blocks_ref, out_ref, arrived,
+                      partial, held, send_sems, recv_sems, rep_send_sems, rep_recv_sems):
+    me = lax.axis_index("rep")
+    row = lax.axis_index("ty")
+    col = lax.axis_index("tx")
+    tile = row * col_tiles + col
+    barrier = pltpu.get_barrier_semaphore()
+
+    def tile_peer(step):
+        peer = lax.rem(tile + step, tile_count)
+        return (me, peer // col_tiles, lax.rem(peer, col_tiles))
+
+    def rep_peer(step):
+        return (lax.rem(me + step, rep_count), row, col)
+
+    @pl.loop(1, tile_count)
+    def _(step):
+        pl.semaphore_signal(barrier, inc=1, device_id=tile_peer(step),
+                            device_id_type=pl.DeviceIdType.MESH)
+
+    @pl.loop(1, rep_count)
+    def _(step):
+        pl.semaphore_signal(barrier, inc=1, device_id=rep_peer(step),
+                            device_id_type=pl.DeviceIdType.MESH)
+
+    pl.semaphore_wait(barrier, tile_count + rep_count - 2)
+
+    def tile_copy(step):
+        peer = lax.rem(tile + step, tile_count)
+        return pltpu.make_async_remote_copy(
+            src_ref=blocks_ref.at[peer],
+            dst_ref=arrived.at[tile],
+            send_sem=send_sems.at[step],
+            recv_sem=recv_sems.at[step],
+            device_id=tile_peer(step),
+            device_id_type=pl.DeviceIdType.MESH,
+        )
+
+    own = pltpu.make_async_copy(blocks_ref.at[tile], arrived.at[tile], send_sems.at[0])
+    own.start()
+
+    @pl.loop(1, tile_count)
+    def _(step):
+        tile_copy(step).start()
+
+    own.wait()
+
+    @pl.loop(1, tile_count)
+    def _(step):
+        tile_copy(step).wait()
+
+    def add_source(source, total):
+        return total + arrived[source].astype(jnp.float32)
+
+    partial[...] = lax.fori_loop(
+        0, tile_count, add_source, jnp.zeros(partial.shape, jnp.float32)
+    )
+    held[me] = partial[...]
+
+    def rep_copy(step):
+        return pltpu.make_async_remote_copy(
+            src_ref=partial,
+            dst_ref=held.at[me],
+            send_sem=rep_send_sems.at[step],
+            recv_sem=rep_recv_sems.at[step],
+            device_id=rep_peer(step),
+            device_id_type=pl.DeviceIdType.MESH,
+        )
+
+    @pl.loop(1, rep_count)
+    def _(step):
+        rep_copy(step).start()
+
+    @pl.loop(1, rep_count)
+    def _(step):
+        rep_copy(step).wait()
+
+    total = held[0]
+    for source in range(1, rep_count):
+        total = total + held[source]
+    out_ref[...] = total
+
+
+def weight_sum(row_blocks):
+    rep_count = lax.axis_size("rep")
+    col_tiles = lax.axis_size("tx")
+    tile_count = row_blocks.shape[0]
+    block_shape = row_blocks.shape[1:]
+    return pl.pallas_call(
+        functools.partial(weight_sum_kernel, rep_count, tile_count, col_tiles),
+        out_shape=jax.ShapeDtypeStruct(block_shape, jnp.float32),
+        in_specs=[pl.BlockSpec(memory_space=pltpu.VMEM)],
+        out_specs=pl.BlockSpec(memory_space=pltpu.VMEM),
+        scratch_shapes=[
+            pltpu.VMEM(row_blocks.shape, row_blocks.dtype),
+            pltpu.VMEM(block_shape, jnp.float32),
+            pltpu.VMEM((rep_count,) + block_shape, jnp.float32),
+            pltpu.SemaphoreType.DMA((tile_count,)),
+            pltpu.SemaphoreType.DMA((tile_count,)),
+            pltpu.SemaphoreType.DMA((rep_count,)),
+            pltpu.SemaphoreType.DMA((rep_count,)),
+        ],
+        compiler_params=pltpu.CompilerParams(collective_id=0, has_side_effects=True),
+    )(row_blocks)
 
 
 def shards(tokens, qkv_weight, cotangent):
@@ -134,8 +244,8 @@
     spread = grad_windows.reshape(back_shape).transpose(4, 3, 0, 5, 1, 6, 2, 7).reshape(split_shape)
     returned = lax.all_to_all(spread, ("ty", "tx"), split_axis=1, concat_axis=1, tiled=True)
     token_grad = returned.reshape(1, tile_height, tile_width, channels)
-    partial_rows = lax.psum_scatter(weight_term, ("ty", "tx"), scatter_dimension=0, tiled=True)
-    weight_grad = lax.psum(partial_rows, "rep")
+    row_blocks = weight_term.reshape(tile_count, channels // tile_count, weight_term.shape[1])
+    weight_grad = weight_sum(row_blocks.astype(jnp.bfloat16))
     weight_grad = weight_grad / (rep_count * tile_count)
     return (token_grad, weight_grad)
 

time: 444 us -> 167 us (0.38)
  the two profiles are of different devices: /device:TPU:64 before, /device:TPU:1 now
where the time goes in v3:
time: 167 us; the launch traced here: 166 us
  Pallas kernels  67 us (40%)
  local copies, waits for them, and re-layouts  31.3 us (19%)
  blocking collectives  23.9 us (14%)
  matrix products  14.8 us (9%)
  starting transfers between devices  12.8 us (8%)
  waiting for transfers between devices  8.89 us (5%)
  other arithmetic  6.45 us (4%)
    pallas_call x1, Pallas kernels, weight_sum(): pl.pallas_call(functools.partial(weight_sum_kernel, rep_count, tile_count...  67 us
    all_to_all x1, blocking collectives, shards(): lax.all_to_all(tokens.reshape(split_shape), ('ty', 'tx'), split_axis=1, c...  23.9 us
    all_to_all x1, waiting for transfers between devices, shards(): lax.all_to_all(cotangent.reshape(split_shape), ('ty', 'tx'), split_axis=1...  8.89 us
    all_to_all x1, starting transfers between devices, shards(): lax.all_to_all(cotangent.reshape(split_shape), ('ty', 'tx'), split_axis=1...  6.53 us
    all_to_all x1, starting transfers between devices, shards(): lax.all_to_all(spread, ('ty', 'tx'), split_axis=1, concat_axis=1, tiled=T...  6.32 us
    another operation x2, local copies, waits for them, and re-layouts, window_grads(): grad_heads = window_g.reshape(head_shape)  5.44 us
    sub x1, matrix products, window_grads(): exponent = jnp.exp(scores - peak_score)  3.83 us
  transfers between devices with their start and end apart: 2, of which 1 were waited for; matrix products, arithmetic and copies ran while one was open for 3% of the time, Pallas kernels for 40%

profile of v3, /device:TPU:1, one launch (start us, length us, event | category | flops | bytes accessed | tf_op | source)
XLA Modules:
  0.0 166.1 jit_solution(7775001244971467701)
XLA Ops:
  0.6 23.9 %all_to_all.15 = bf16[1,64,1,4,512]{4,3,2,0,1:T(4,128)(2,1)S(1)} all-to-all(bf16[1,64,1,4,512]{4,3,2,0,1:T(4,128)(2,1)} %bitcast.73), channel_id=1, replica_groups=mesh['rep'=8,'ty'=16,'tx'=4] {'ty','tx'}, dimensions={1} | all-to-all | bytes 524288 | tf_op jit(solution)/shard_map/all_to_all | solution.py:207
  24.5 6.5 %all-to-all-start = ((bf16[1,64,1,4,512]{4,3,2,0,1:T(4,128)(2,1)}), bf16[1,64,1,4,512]{4,3,2,0,1:T(4,128)(2,1)S(1)}, u32[]{:S(2)}, u32[]{:S(2)}) async-start(bf16[1,64,1,4,512]{4,3,2,0,1:T(4,128)(2,1)} %bitcast.74), calls=%async_computation | async-start | bytes 524288 | tf_op jit(solution)/shard_map/all_to_all | solution.py:210
  31.0 0.3 reshape.164
  31.3 0.4 fusion.31
  31.7 0.3 copy.98
  32.2 0.5 multiply_reduce_fusion.1
  32.9 8.9 %all-to-all-done = bf16[1,64,1,4,512]{4,3,2,0,1:T(4,128)(2,1)S(1)} async-done(((bf16[1,64,1,4,512]{4,3,2,0,1:T(4,128)(2,1)}), bf16[1,64,1,4,512]{4,3,2,0,1:T(4,128)(2,1)S(1)}, u32[]{:S(2)}, u32[]{:S(2)}) %all-to-all-start) | async-done | bytes 262176 | tf_op jit(solution)/shard_map/all_to_all | solution.py:210
  41.9 0.9 copy.99
  42.8 0.4 reshape.163
  43.1 2.7 %reshape_reshape.3 = bf16[4,64,16,32]{3,2,1,0:T(8,128)(2,1)} reshape(bf16[2,1,2,8,1,4,2,512]{7,6,5,3,2,0,4,1:T(2,128)(2,1)} %bitcast.71) | data formatting | bytes 524288 | tf_op jit(solution)/shard_map/reshape;reshape | solution.py:42
  45.8 2.8 %copy.50 = bf16[4,64,16,32]{1,3,2,0:T(8,128)(2,1)} copy(bf16[4,64,16,32]{3,2,1,0:T(8,128)(2,1)} %reshape_reshape.3) | data formatting | bytes 524288 | tf_op jit(solution)/shard_map/reshape;reshape | solution.py:42
  48.6 1.8 %fusion.34 = (bf16[256,1536]{1,0:T(8,128)(2,1)S(1)}, f32[256,1536]{1,0:T(8,128)}) fusion(bf16[512,1536]{1,0:T(8,128)(2,1)S(1)} %copy-done, f32[256,512]{1,0:T(8,128)S(1)} %reshape.163, f32[256]{0:T(256)S(1)} %rsqrt.13, f32[256]{0:T(256)S(1)} %div.34), kind=kOutput, calls=%fused_computation.50 | convolution fusion | flops 403439616 | bytes 4458496 | tf_op jit(solution)/shard_map/dot_general | solution.py:28
  50.3 0.7 fusion.33
  51.1 1.1 copy.48
  52.2 1.1 reshape.156
  53.2 0.8 copy.44
  54.1 1.2 reshape.154
  55.3 1.8 %fusion.10 = bf16[256,512]{1,0:T(8,128)(2,1)} fusion(f32[256,1536]{1,0:T(8,128)} %get-tuple-element.8), kind=kLoop, calls=%fused_computation.20 | loop fusion | flops 262144 | bytes 786432 | tf_op jit(solution)/shard_map/convert_element_type | solution.py:31
  57.1 1.8 %copy.45 = bf16[256,512]{0,1:T(8,128)(2,1)} copy(bf16[256,512]{1,0:T(8,128)(2,1)} %fusion.10) | data formatting | bytes 524288 | tf_op jit(solution)/shard_map/convert_element_type | solution.py:31
  58.9 2.0 %reshape.155 = bf16[4,64,16,32]{1,0,3,2:T(4,128)(2,1)} reshape(bf16[256,512]{0,1:T(8,128)(2,1)} %copy.45) | data formatting | bytes 524288 | tf_op jit(solution)/shard_map/reshape | solution.py:31
  60.9 3.8 %fusion.35 = (f32[4,16,64]{2,1,0:T(8,128)}, f32[4,16,64,64]{2,3,1,0:T(8,128)}) fusion(bf16[4,64,16,32]{1,0,3,2:T(4,128)(2,1)S(1)} %reshape.154, bf16[4,64,16,32]{1,0,3,2:T(4,128)(2,1)} %reshape.155), kind=kOutput, calls=%fused_computation.51 | convolution fusion | flops 17301568 | bytes 1589248 | tf_op jit(solution)/shard_map/sub | solution.py:39
  64.7 2.5 %fusion.6 = bf16[4,64,16,32]{1,3,2,0:T(8,128)(2,1)S(1)} fusion(bf16[4,64,16,32]{1,3,2,0:T(8,128)(2,1)} %copy.50, f32[4,16,64,64]{2,3,1,0:T(8,128)} %get-tuple-element.10, f32[4,16,64]{2,1,0:T(8,128)} %get-tuple-element.9), kind=kOutput, calls=%fused_computation.13 | convolution fusion | flops 17432576 | bytes 1589248 | tf_op jit(solution)/shard_map/wnqk,wqne->wkne/dot_general | solution.py:46
  67.4 0.6 fusion.1
  68.0 0.7 fusion.3
  68.7 0.4 copy-done.1
  69.1 1.4 fusion.5
  70.5 1.2 fusion.7
  71.7 0.4 copy.59
  72.2 1.0 reshape.159
  73.2 1.8 %copy.62 = bf16[256,512]{1,0:T(8,128)(2,1)} copy(bf16[256,512]{0,1:T(8,128)(2,1)} %reshape.159) | data formatting | bytes 524288 | tf_op jit(solution)/shard_map/reshape | solution.py:64
  75.0 1.4 copy.53
  76.5 1.0 reshape.157
  77.5 1.8 %copy.60 = bf16[256,512]{1,0:T(8,128)(2,1)} copy(bf16[256,512]{0,1:T(8,128)(2,1)} %reshape.157) | data formatting | bytes 524288 | tf_op jit(solution)/shard_map/reshape | solution.py:62
  79.3 1.4 copy.56
  80.8 1.0 reshape.158
  81.8 1.8 %copy.61 = bf16[256,512]{1,0:T(8,128)(2,1)} copy(bf16[256,512]{0,1:T(8,128)(2,1)} %reshape.158) | data formatting | bytes 524288 | tf_op jit(solution)/shard_map/reshape | solution.py:63
  83.6 1.7 %fusion.19 = f32[256,512]{1,0:T(8,128)S(1)} fusion(bf16[512,1536]{1,0:T(8,128)(2,1)S(1)} %copy-done, bf16[256,512]{1,0:T(8,128)(2,1)} %copy.62, bf16[256,512]{1,0:T(8,128)(2,1)} %copy.61, bf16[256,512]{1,0:T(8,128)(2,1)} %copy.60), kind=kOutput, calls=%fused_computation.34 | convolution fusion | flops 405012480 | bytes 2883584 | tf_op jit(solution)/shard_map/dot_general | solution.py:68
  85.3 0.9 fusion.32
  86.2 0.3 reshape.160
  86.7 0.2 div.38
  86.8 0.8 fusion.21
  87.6 0.3 copy.63
  87.9 0.8 reshape.161
  88.7 6.3 %all-to-all-start.2 = ((bf16[1,64,1,4,512]{4,3,2,0,1:T(4,128)(2,1)}), bf16[1,64,1,4,512]{4,3,2,0,1:T(4,128)(2,1)S(1)}, u32[]{:S(2)}, u32[]{:S(2)}) async-start(bf16[1,64,1,4,512]{4,3,2,0,1:T(4,128)(2,1)} %reshape.161), calls=%async_computation.2 | async-start | bytes 524288 | tf_op jit(solution)/shard_map/all_to_all | solution.py:245
  95.2 1.7 %convolution_convert_fusion.blocks_ref = bf16[64,8,1536]{2,1,0:T(8,128)(2,1)} fusion(bf16[256,512]{1,0:T(8,128)(2,1)S(1)} %copy-done.6, bf16[256,512]{1,0:T(8,128)(2,1)S(1)} %copy-done.8, bf16[256,512]{1,0:T(8,128)(2,1)S(1)} %copy-done.7, bf16[512,256]{1,0:T(8,128)(2,1)S(1)} %copy.64), kind=kOutput, calls=%fused_computation.1 | convolution fusion | flops 405798912 | bytes 2621440 | tf_op jit(solution)/shard_map/dot_general | solution.py:72
  97.0 67.0 %shard_map.50 = f32[8,1536]{1,0:T(8,128)} custom-call(bf16[64,8,1536]{2,1,0:T(8,128)(2,1)} %convolution_convert_fusion.blocks_ref), custom_call_target="tpu_custom_call" | custom-call | tf_op jit(solution)/shard_map/pallas_call | solution.py:172
  164.0 1.4 broadcast_multiply_fusion.1
  165.4 0.7 copy.101
  (28 shorter events, 0.9 us)
Async XLA Ops:
  0.6 47.9 %copy-start = (bf16[512,1536]{1,0:T(8,128)(2,1)S(1)}, bf16[512,1536]{1,0:T(8,128)(2,1)}, u32[]{:S(2)}) copy-start(bf16[512,1536]{1,0:T(8,128)(2,1)} %param.4) | copy-start | bytes 4718596
  24.5 17.3 %all-to-all-start = ((bf16[1,64,1,4,512]{4,3,2,0,1:T(4,128)(2,1)}), bf16[1,64,1,4,512]{4,3,2,0,1:T(4,128)(2,1)S(1)}, u32[]{:S(2)}, u32[]{:S(2)}) async-start(bf16[1,64,1,4,512]{4,3,2,0,1:T(4,128)(2,1)} %bitcast.74), calls=%async_computation | async-start | bytes 524288 | tf_op jit(solution)/shard_map/all_to_all | solution.py:210
  64.7 2.5 %copy-start.2 = (f32[4,16,64,64]{2,3,1,0:T(8,128)S(1)}, f32[4,16,64,64]{2,3,1,0:T(8,128)}, u32[]{:S(2)}) copy-start(f32[4,16,64,64]{2,3,1,0:T(8,128)} %get-tuple-element.10) | copy-start | bytes 3145732
  64.7 2.5 %copy-start.4 = (bf16[4,64,16,32]{1,3,2,0:T(8,128)(2,1)S(1)}, bf16[4,64,16,32]{1,3,2,0:T(8,128)(2,1)}, u32[]{:S(2)}) copy-start(bf16[4,64,16,32]{1,3,2,0:T(8,128)(2,1)} %copy.50) | copy-start | bytes 786436
  64.7 2.6 %copy-start.5 = (bf16[4,64,16,32]{1,0,3,2:T(4,128)(2,1)S(1)}, bf16[4,64,16,32]{1,0,3,2:T(4,128)(2,1)}, u32[]{:S(2)}) copy-start(bf16[4,64,16,32]{1,0,3,2:T(4,128)(2,1)} %reshape.156) | copy-start | bytes 786436
  64.7 2.6 %copy-start.9 = (f32[4,16,64]{2,1,0:T(8,128)S(1)}, f32[4,16,64]{2,1,0:T(8,128)}, u32[]{:S(2)}) copy-start(f32[4,16,64]{2,1,0:T(8,128)} %get-tuple-element.9) | copy-start | bytes 49156
  68.0 1.0 copy-start.1
  86.5 8.6 %copy-start.3 = (bf16[512,256]{0,1:T(8,128)(2,1)S(1)}, bf16[512,256]{0,1:T(8,128)(2,1)}, u32[]{:S(2)}) copy-start(bf16[512,256]{0,1:T(8,128)(2,1)} %get-tuple-element.6) | copy-start | bytes 786436
  87.6 7.6 %copy-start.6 = (bf16[256,512]{1,0:T(8,128)(2,1)S(1)}, bf16[256,512]{1,0:T(8,128)(2,1)}, u32[]{:S(2)}) copy-start(bf16[256,512]{1,0:T(8,128)(2,1)} %copy.62) | copy-start | bytes 786436
  87.6 7.6 %copy-start.7 = (bf16[256,512]{1,0:T(8,128)(2,1)S(1)}, bf16[256,512]{1,0:T(8,128)(2,1)}, u32[]{:S(2)}) copy-start(bf16[256,512]{1,0:T(8,128)(2,1)} %copy.60) | copy-start | bytes 786436
  87.6 7.6 %copy-start.8 = (bf16[256,512]{1,0:T(8,128)(2,1)S(1)}, bf16[256,512]{1,0:T(8,128)(2,1)}, u32[]{:S(2)}) copy-start(bf16[256,512]{1,0:T(8,128)(2,1)} %copy.61) | copy-start | bytes 786436
  88.7 76.7 %all-to-all-start.2 = ((bf16[1,64,1,4,512]{4,3,2,0,1:T(4,128)(2,1)}), bf16[1,64,1,4,512]{4,3,2,0,1:T(4,128)(2,1)S(1)}, u32[]{:S(2)}, u32[]{:S(2)}) async-start(bf16[1,64,1,4,512]{4,3,2,0,1:T(4,128)(2,1)} %reshape.161), calls=%async_computation.2 | async-start | bytes 524288 | tf_op jit(solution)/shard_map/all_to_all | solution.py:245

commit v4 on v3

--- a/solution.py
+++ b/solution.py
@@ -26,35 +26,40 @@
     standard, inv_std = normalize(window_x.astype(jnp.float32))
     normed = standard.astype(jnp.bfloat16).reshape(win_count * win_tokens, channels)
     projection = jnp.dot(normed, qkv_weight, preferred_element_type=jnp.float32)
-    head_shape = (win_count, win_tokens, HEADS, HEAD_DIM)
-    query_heads = (
-        (projection[:, :channels] * HEAD_DIM ** (-0.5)).astype(jnp.bfloat16).reshape(head_shape)
-    )
-    key_heads = projection[:, channels : 2 * channels].astype(jnp.bfloat16).reshape(head_shape)
-    value_heads = projection[:, 2 * channels :].astype(jnp.bfloat16).reshape(head_shape)
-    scores = jnp.einsum(
-        "wqne,wkne->wnqk", query_heads, key_heads, preferred_element_type=jnp.float32
-    )
+    flat_shape = (win_count, win_tokens, channels)
+    query = (projection[:, :channels] * HEAD_DIM ** (-0.5)).astype(jnp.bfloat16).reshape(flat_shape)
+    key = projection[:, channels : 2 * channels].astype(jnp.bfloat16).reshape(flat_shape)
+    value = projection[:, 2 * channels :].astype(jnp.bfloat16).reshape(flat_shape)
+    grad = window_g.astype(jnp.bfloat16)
+    head_mask = (
+        lax.broadcasted_iota(jnp.int32, (HEADS, channels), 1) // HEAD_DIM
+        == lax.broadcasted_iota(jnp.int32, (HEADS, channels), 0)
+    ).astype(jnp.bfloat16)
+
+    def spread(values):
+        return values[:, None, :, :] * head_mask[None, :, None, :]
+
+    query_spread = spread(query)
+    grad_spread = spread(grad)
+    scores = jnp.einsum("wnqc,wkc->wnqk", query_spread, key, preferred_element_type=jnp.float32)
     peak_score = jnp.max(scores, axis=-1, keepdims=True)
     exponent = jnp.exp(scores - peak_score)
     attn_probs = exponent / jnp.sum(exponent, axis=-1, keepdims=True)
     probs_low = attn_probs.astype(jnp.bfloat16)
-    grad_heads = window_g.reshape(head_shape)
-    attn_grad = jnp.einsum(
-        "wqne,wkne->wnqk", grad_heads, value_heads, preferred_element_type=jnp.float32
-    )
+    attn_grad = jnp.einsum("wnqc,wkc->wnqk", grad_spread, value, preferred_element_type=jnp.float32)
     value_grad = jnp.einsum(
-        "wnqk,wqne->wkne", probs_low, grad_heads, preferred_element_type=jnp.float32
+        "wnqk,wnqc->wkc", probs_low, grad_spread, preferred_element_type=jnp.float32
     ).astype(jnp.bfloat16)
     score_grad = (
         attn_probs * (attn_grad - jnp.sum(attn_probs * attn_grad, axis=-1, keepdims=True))
     ).astype(jnp.bfloat16)
+    key_grad = jnp.einsum(
+        "wnqk,wnqc->wkc", score_grad, query_spread, preferred_element_type=jnp.float32
+    ).astype(jnp.bfloat16)
+    query_full = jnp.einsum("wnqk,wkc->wnqc", score_grad, key, preferred_element_type=jnp.float32)
     query_grad = (
-        jnp.einsum("wnqk,wkne->wqne", score_grad, key_heads, preferred_element_type=jnp.float32)
+        jnp.sum(query_full * head_mask[None, :, None, :].astype(jnp.float32), axis=1)
         * HEAD_DIM ** (-0.5)
-    ).astype(jnp.bfloat16)
-    key_grad = jnp.einsum(
-        "wnqk,wqne->wkne", score_grad, query_heads, preferred_element_type=jnp.float32
     ).astype(jnp.bfloat16)
     flat_shape = (win_count * win_tokens, channels)
     proj_grad = jnp.concatenate(

time: 167 us -> 142 us (0.85)
  blocking collectives: 23.9 us -> 0 us
  local copies, waits for them, and re-layouts: 31.3 us -> 8.16 us
  starting transfers between devices: 12.8 us -> 25.9 us
  waiting for transfers between devices: 8.89 us -> 17.9 us
    all_to_all x1 -> x0, blocking collectives: 23.9 us -> none  [shards(): lax.all_to_all(tokens.reshape(split_shape), ('ty', 'tx'), split_axis=1, c...]
    all_to_all x0 -> x1, starting transfers between devices: none -> 13.1 us  [shards(): lax.all_to_all(tokens.reshape(split_shape), ('ty', 'tx'), split_axis=1, c...]
    reshape x9 -> x0, local copies, waits for them, and re-layouts: 12.9 us -> none  [the longest x2 2.86 us: window_grads(): value_grad.reshape(flat_shape)]
    all_to_all x0 -> x1, waiting for transfers between devices: none -> 10.1 us  [shards(): lax.all_to_all(tokens.reshape(split_shape), ('ty', 'tx'), split_axis=1, c...]
    another operation x2 -> x0, local copies, waits for them, and re-layouts: 5.44 us -> none  [window_grads(): grad_heads = window_g.reshape(head_shape)]
    convert_element_type x4 -> x0, local copies, waits for them, and re-layouts: 5.08 us -> none  [the longest x1 1.78 us: window_grads(): (projection[:, :channels] * HEAD_DIM ** (-0.5)).astype(jnp.bfloat16)]
    slice x3 -> x1, local copies, waits for them, and re-layouts: 2.66 us -> 0.82 us  [window_grads(): projection[:, 2 * channels:].astype(jnp.bfloat16).reshape(flat_shape)]
    convert_element_type x1, other arithmetic: 1.79 us -> 0.04 us  [window_grads(): (projection[:, :channels] * HEAD_DIM ** (-0.5)).astype(jnp.bfloat16)]
  transfers between devices with their start and end apart: 2 -> 3, of which waited for: 1 -> 2; matrix products, arithmetic and copies ran while one was open for 3% -> 5% of each run, Pallas kernels for 40% -> 47%
where the time goes in v4:
time: 142 us
  Pallas kernels  67 us (47%)
  starting transfers between devices  25.9 us (18%)
  waiting for transfers between devices  17.9 us (13%)
  matrix products  15.7 us (11%)
  local copies, waits for them, and re-layouts  8.16 us (6%)
  other arithmetic  6.16 us (4%)
    pallas_call x1, Pallas kernels, weight_sum(): pl.pallas_call(functools.partial(weight_sum_kernel, rep_count, tile_count...  67 us
    all_to_all x1, starting transfers between devices, shards(): lax.all_to_all(tokens.reshape(split_shape), ('ty', 'tx'), split_axis=1, c...  13.1 us
    all_to_all x1, waiting for transfers between devices, shards(): lax.all_to_all(tokens.reshape(split_shape), ('ty', 'tx'), split_axis=1, c...  10.1 us
    all_to_all x1, waiting for transfers between devices, shards(): lax.all_to_all(cotangent.reshape(split_shape), ('ty', 'tx'), split_axis=1...  7.78 us
    all_to_all x1, starting transfers between devices, shards(): lax.all_to_all(cotangent.reshape(split_shape), ('ty', 'tx'), split_axis=1...  6.53 us
    all_to_all x1, starting transfers between devices, shards(): lax.all_to_all(spread, ('ty', 'tx'), split_axis=1, concat_axis=1, tiled=T...  6.31 us
    sub x1, matrix products, window_grads(): exponent = jnp.exp(scores - peak_score)  5.12 us
  transfers between devices with their start and end apart: 3, of which 2 were waited for; matrix products, arithmetic and copies ran while one was open for 5% of the time, Pallas kernels for 47%

profile of v4, /device:TPU:1, one launch (start us, length us, event | category | flops | bytes accessed | tf_op | source)
XLA Modules:
  0.0 141.9 jit_solution(15426320505629857310)
XLA Ops:
  0.6 0.0 copy-start
  0.6 13.1 %all-to-all-start.1 = ((bf16[1,64,1,4,512]{4,3,2,0,1:T(4,128)(2,1)}), bf16[1,64,1,4,512]{4,3,2,0,1:T(4,128)(2,1)S(1)}, u32[]{:S(2)}, u32[]{:S(2)}) async-start(bf16[1,64,1,4,512]{4,3,2,0,1:T(4,128)(2,1)} %bitcast.75), calls=%async_computation.1 | async-start | bytes 524288 | tf_op jit(solution)/shard_map/all_to_all | solution.py:212
  13.7 0.6 fusion.44
  14.4 10.1 %all-to-all-done.1 = bf16[1,64,1,4,512]{4,3,2,0,1:T(4,128)(2,1)S(1)} async-done(((bf16[1,64,1,4,512]{4,3,2,0,1:T(4,128)(2,1)}), bf16[1,64,1,4,512]{4,3,2,0,1:T(4,128)(2,1)S(1)}, u32[]{:S(2)}, u32[]{:S(2)}) %all-to-all-start.1) | async-done | bytes 262176 | tf_op jit(solution)/shard_map/all_to_all | solution.py:212
  24.5 6.5 %all-to-all-start = ((bf16[1,64,1,4,512]{4,3,2,0,1:T(4,128)(2,1)}), bf16[1,64,1,4,512]{4,3,2,0,1:T(4,128)(2,1)S(1)}, u32[]{:S(2)}, u32[]{:S(2)}) async-start(bf16[1,64,1,4,512]{4,3,2,0,1:T(4,128)(2,1)} %bitcast.76), calls=%async_computation | async-start | bytes 524288 | tf_op jit(solution)/shard_map/all_to_all | solution.py:215
  31.1 0.3 reshape.255
  31.3 0.4 fusion.48
  31.7 0.3 copy.35
  32.0 0.7 div.47
  32.7 0.5 multiply_reduce_fusion.3
  33.3 0.7 rsqrt.13
  34.0 7.8 %all-to-all-done = bf16[1,64,1,4,512]{4,3,2,0,1:T(4,128)(2,1)S(1)} async-done(((bf16[1,64,1,4,512]{4,3,2,0,1:T(4,128)(2,1)}), bf16[1,64,1,4,512]{4,3,2,0,1:T(4,128)(2,1)S(1)}, u32[]{:S(2)}, u32[]{:S(2)}) %all-to-all-start) | async-done | bytes 262176 | tf_op jit(solution)/shard_map/all_to_all | solution.py:215
  41.8 0.1 reshape.245
  41.9 0.2 copy.36
  42.1 0.8 mul.107
  42.9 0.4 reshape.254
  43.3 1.3 fusion.51
  44.5 0.8 fusion.50
  45.4 0.0 copy-start.5
  45.4 5.1 %fusion.52 = (f32[4,16,64]{2,1,0:T(8,128)}, f32[4,16,64,64]{2,3,1,0:T(8,128)}) fusion(bf16[4,64,512,1]{2,1,3,0:T(8,128)(2,1)} %bitcast.77, bf16[16,512]{1,0:T(8,128)(2,1)S(1)} %get-tuple-element.8, bf16[4,64,512]{2,1,0:T(8,128)(2,1)S(1)} %bitcast.73), kind=kOutput, calls=%fused_computation.66 | convolution fusion | flops 271056960 | bytes 1605632 | tf_op jit(solution)/shard_map/sub | solution.py:46
  50.5 0.0 copy-done.5
  50.6 2.6 %fusion.23 = bf16[4,64,512]{2,1,0:T(8,128)(2,1)S(1)} fusion(bf16[4,64,512]{2,1,0:T(8,128)(2,1)S(1)} %copy-done.5, bf16[16,512]{1,0:T(8,128)(2,1)S(1)} %get-tuple-element.8, f32[4,16,64,64]{2,3,1,0:T(8,128)} %get-tuple-element.12, f32[4,16,64]{2,1,0:T(8,128)} %get-tuple-element.11), kind=kOutput, calls=%fused_computation.24 | convolution fusion | flops 271187968 | bytes 1605632 | tf_op jit(solution)/shard_map/wnqk,wnqc->wkc/dot_general | solution.py:50
  53.2 0.0 copy-start.12
  53.2 0.0 copy-done.1
  53.2 2.1 %multiply_reduce_fusion.1 = (f32[4,16,64]{2,1,0:T(8,128)S(1)}, f32[4,16,64,64]{2,3,1,0:T(8,128)S(1)}) fusion(f32[4,16,64,64]{2,3,1,0:T(8,128)S(1)} %copy-done.1, f32[4,16,64]{2,1,0:T(8,128)S(1)} %copy-done.9, bf16[4,64,512,1]{2,1,3,0:T(8,128)(2,1)S(1)} %bitcast.79, bf16[4,64,512]{2,1,0:T(8,128)(2,1)S(1)} %copy-done.5, bf16[16,512]{1,0:T(8,128)(2,1)S(1)} %get-tuple-element.8), kind=kOutput, calls=%fused_computation.12 | convolution fusion | flops 271314944 | bytes 2670592 | tf_op jit(solution)/shard_map/wnqc,wkc->wnqk/dot_general | solution.py:49
  55.4 0.7 multiply_convert_fusion
  56.1 0.0 copy-start.8
  56.1 0.9 fusion.26
  57.0 0.0 copy-done.6
  57.0 1.3 multiply_reduce_fusion
  58.4 0.6 fusion.33
  59.0 0.0 copy-done.3
  59.0 0.0 copy-done.11
  59.1 0.8 fusion.49
  59.9 0.3 reshape.251
  60.2 0.0 copy-start.2
  60.3 0.8 div.55
  61.1 0.8 div.53
  61.8 1.5 %fusion.35 = bf16[1,8,2,4,1,2,2,512]{7,5,3,1,6,2,0,4:T(2,128)(2,1)S(1)} fusion(f32[2,2,8,4,2]{4,3,2,1,0:T(4,128)} %div.55, f32[2,2,8,4,2]{4,3,2,1,0:T(4,128)S(1)} %broadcast_multiply_fusion, f32[2,1,2,8,1,4,2,512]{7,6,5,3,2,0,4,1:T(2,128)S(1)} %reshape.251, f32[2,2,8,4,2]{4,3,2,1,0:T(4,128)} %div.53, f32[2,2,8,4,2]{4,3,2,1,0:T(4,128)S(1)} %add_rsqrt_fusion, ...), kind=kLoop, calls=%fused_computation.42 | loop fusion | flops 1179648 | bytes 1576960 | tf_op jit(solution)/shard_map/transpose | solution.py:249
  63.4 0.3 copy.18
  63.7 0.8 reshape.252
  64.5 6.3 %all-to-all-start.2 = ((bf16[1,64,1,4,512]{4,3,2,0,1:T(4,128)(2,1)}), bf16[1,64,1,4,512]{4,3,2,0,1:T(4,128)(2,1)S(1)}, u32[]{:S(2)}, u32[]{:S(2)}) async-start(bf16[1,64,1,4,512]{4,3,2,0,1:T(4,128)(2,1)} %reshape.252), calls=%async_computation.2 | async-start | bytes 524288 | tf_op jit(solution)/shard_map/all_to_all | solution.py:250
  70.8 0.1 copy.19
  71.0 1.7 %convolution_convert_fusion.blocks_ref = bf16[64,8,1536]{2,1,0:T(8,128)(2,1)} fusion(bf16[256,512]{1,0:T(8,128)(2,1)S(1)} %bitcast.81, bf16[256,512]{1,0:T(8,128)(2,1)S(1)} %bitcast.83, bf16[256,512]{1,0:T(8,128)(2,1)S(1)} %bitcast.72, bf16[512,256]{1,0:T(8,128)(2,1)S(1)} %copy.19), kind=kOutput, calls=%fused_computation.10 | convolution fusion | flops 405798912 | bytes 2621440 | tf_op jit(solution)/shard_map/dot_general | solution.py:77
  72.7 67.0 %shard_map.50 = f32[8,1536]{1,0:T(8,128)} custom-call(bf16[64,8,1536]{2,1,0:T(8,128)(2,1)} %convolution_convert_fusion.blocks_ref), custom_call_target="tpu_custom_call" | custom-call | tf_op jit(solution)/shard_map/pallas_call | solution.py:177
  139.8 1.4 %broadcast_multiply_fusion.1 = f32[8,1536]{1,0:T(8,128)} fusion(f32[8,1536]{1,0:T(8,128)} %shard_map.50), kind=kLoop, calls=%fused_computation.47 | loop fusion | flops 12288 | bytes 98304 | tf_op jit(solution)/shard_map/div | solution.py:254
  141.2 0.0 all-to-all-done.2
  141.2 0.7 copy.38
  (30 shorter events, 0.2 us)
Async XLA Ops:
  0.6 42.6 %copy-start = (bf16[512,1536]{1,0:T(8,128)(2,1)S(1)}, bf16[512,1536]{1,0:T(8,128)(2,1)}, u32[]{:S(2)}) copy-start(bf16[512,1536]{1,0:T(8,128)(2,1)} %param.4) | copy-start | bytes 4718596
  0.6 23.9 %all-to-all-start.1 = ((bf16[1,64,1,4,512]{4,3,2,0,1:T(4,128)(2,1)}), bf16[1,64,1,4,512]{4,3,2,0,1:T(4,128)(2,1)S(1)}, u32[]{:S(2)}, u32[]{:S(2)}) async-start(bf16[1,64,1,4,512]{4,3,2,0,1:T(4,128)(2,1)} %bitcast.75), calls=%async_computation.1 | async-start | bytes 524288 | tf_op jit(solution)/shard_map/all_to_all | solution.py:212
  24.5 17.3 %all-to-all-start = ((bf16[1,64,1,4,512]{4,3,2,0,1:T(4,128)(2,1)}), bf16[1,64,1,4,512]{4,3,2,0,1:T(4,128)(2,1)S(1)}, u32[]{:S(2)}, u32[]{:S(2)}) async-start(bf16[1,64,1,4,512]{4,3,2,0,1:T(4,128)(2,1)} %bitcast.76), calls=%async_computation | async-start | bytes 524288 | tf_op jit(solution)/shard_map/all_to_all | solution.py:215
  45.4 5.1 %copy-start.5 = (bf16[4,64,512]{2,1,0:T(8,128)(2,1)S(1)}, bf16[4,64,512]{2,1,0:T(8,128)(2,1)}, u32[]{:S(2)}) copy-start(bf16[4,64,512]{2,1,0:T(8,128)(2,1)} %mul.107) | copy-start | bytes 786436
  50.5 2.7 %copy-start.1 = (f32[4,16,64,64]{2,3,1,0:T(8,128)S(1)}, f32[4,16,64,64]{2,3,1,0:T(8,128)}, u32[]{:S(2)}) copy-start(f32[4,16,64,64]{2,3,1,0:T(8,128)} %get-tuple-element.12) | copy-start | bytes 3145732
  50.5 2.7 %copy-start.7 = (bf16[256,512]{1,0:T(8,128)(2,1)S(1)}, bf16[256,512]{1,0:T(8,128)(2,1)}, u32[]{:S(2)}) copy-start(bf16[256,512]{1,0:T(8,128)(2,1)} %get-tuple-element.4) | copy-start | bytes 786436
  50.6 2.7 %copy-start.9 = (f32[4,16,64]{2,1,0:T(8,128)S(1)}, f32[4,16,64]{2,1,0:T(8,128)}, u32[]{:S(2)}) copy-start(f32[4,16,64]{2,1,0:T(8,128)} %get-tuple-element.11) | copy-start | bytes 49156
  53.2 5.2 %copy-start.12 = (bf16[4,64,512]{2,1,0:T(8,128)(2,1)}, bf16[4,64,512]{2,1,0:T(8,128)(2,1)S(1)}, u32[]{:S(2)}) copy-start(bf16[4,64,512]{2,1,0:T(8,128)(2,1)S(1)} %fusion.23) | copy-start | bytes 786436
  56.0 1.0 copy-start.6
  56.1 0.9 copy-start.8
  57.0 1.4 %copy-start.14 = (bf16[4,64,512]{2,1,0:T(8,128)(2,1)}, bf16[4,64,512]{2,1,0:T(8,128)(2,1)S(1)}, u32[]{:S(2)}) copy-start(bf16[4,64,512]{2,1,0:T(8,128)(2,1)S(1)} %fusion.26) | copy-start | bytes 786436
  58.4 0.7 copy-start.3
  58.4 0.7 copy-start.10
  58.4 0.7 copy-start.11
  60.2 10.6 %copy-start.2 = (bf16[512,256]{0,1:T(8,128)(2,1)S(1)}, bf16[512,256]{0,1:T(8,128)(2,1)}, u32[]{:S(2)}) copy-start(bf16[512,256]{0,1:T(8,128)(2,1)} %get-tuple-element.6) | copy-start | bytes 786436
  60.2 10.7 %copy-start.4 = (bf16[4,64,512]{2,1,0:T(8,128)(2,1)S(1)}, bf16[4,64,512]{2,1,0:T(8,128)(2,1)}, u32[]{:S(2)}) copy-start(bf16[4,64,512]{2,1,0:T(8,128)(2,1)} %copy-done.3) | copy-start | bytes 786436
  63.4 7.6 %copy-start.13 = (bf16[4,64,512]{2,1,0:T(8,128)(2,1)S(1)}, bf16[4,64,512]{2,1,0:T(8,128)(2,1)}, u32[]{:S(2)}) copy-start(bf16[4,64,512]{2,1,0:T(8,128)(2,1)} %copy-done.12) | copy-start | bytes 786436
  63.4 7.6 %copy-start.15 = (bf16[4,64,512]{2,1,0:T(8,128)(2,1)S(1)}, bf16[4,64,512]{2,1,0:T(8,128)(2,1)}, u32[]{:S(2)}) copy-start(bf16[4,64,512]{2,1,0:T(8,128)(2,1)} %copy-done.14) | copy-start | bytes 786436
  64.5 76.7 %all-to-all-start.2 = ((bf16[1,64,1,4,512]{4,3,2,0,1:T(4,128)(2,1)}), bf16[1,64,1,4,512]{4,3,2,0,1:T(4,128)(2,1)S(1)}, u32[]{:S(2)}, u32[]{:S(2)}) async-start(bf16[1,64,1,4,512]{4,3,2,0,1:T(4,128)(2,1)} %reshape.252), calls=%async_computation.2 | async-start | bytes 524288 | tf_op jit(solution)/shard_map/all_to_all | solution.py:250

commit v5 on v4

--- a/solution.py
+++ b/solution.py
@@ -192,6 +192,83 @@
     )(row_blocks)
 
 
+def exchange_kernel(tile_count, col_tiles, tokens_ref, cot_ref, tokens_out, cot_out,
+                    tokens_held, cot_held, send_sems, recv_sems, own_sems):
+    me = lax.axis_index("rep")
+    row = lax.axis_index("ty")
+    col = lax.axis_index("tx")
+    tile = row * col_tiles + col
+    barrier = pltpu.get_barrier_semaphore()
+
+    def tile_peer(step):
+        peer = lax.rem(tile + step, tile_count)
+        return (me, peer // col_tiles, lax.rem(peer, col_tiles))
+
+    @pl.loop(1, tile_count)
+    def _(step):
+        pl.semaphore_signal(barrier, inc=1, device_id=tile_peer(step),
+                            device_id_type=pl.DeviceIdType.MESH)
+
+    pl.semaphore_wait(barrier, tile_count - 1)
+
+    def tile_copies(step):
+        peer = lax.rem(tile + step, tile_count)
+        return [
+            pltpu.make_async_remote_copy(
+                src_ref=source.at[0, peer],
+                dst_ref=held.at[tile],
+                send_sem=send_sems.at[step, index],
+                recv_sem=recv_sems.at[step, index],
+                device_id=tile_peer(step),
+                device_id_type=pl.DeviceIdType.MESH,
+            )
+            for index, (source, held) in enumerate(((tokens_ref, tokens_held), (cot_ref, cot_held)))
+        ]
+
+    own = [
+        pltpu.make_async_copy(tokens_ref.at[0, tile], tokens_held.at[tile], own_sems.at[0]),
+        pltpu.make_async_copy(cot_ref.at[0, tile], cot_held.at[tile], own_sems.at[1]),
+    ]
+    for copy in own:
+        copy.start()
+
+    @pl.loop(1, tile_count)
+    def _(step):
+        for copy in tile_copies(step):
+            copy.start()
+
+    for copy in own:
+        copy.wait()
+
+    @pl.loop(1, tile_count)
+    def _(step):
+        for copy in tile_copies(step):
+            copy.wait()
+
+    tokens_out[...] = tokens_held[...]
+    cot_out[...] = cot_held[...]
+
+
+def exchange(tokens, cotangent):
+    col_tiles = lax.axis_size("tx")
+    tile_count = lax.axis_size("ty") * col_tiles
+    held_shape = (tile_count,) + tokens.shape[2:]
+    return pl.pallas_call(
+        functools.partial(exchange_kernel, tile_count, col_tiles),
+        out_shape=[jax.ShapeDtypeStruct(held_shape, tokens.dtype)] * 2,
+        in_specs=[pl.BlockSpec(memory_space=pltpu.VMEM)] * 2,
+        out_specs=[pl.BlockSpec(memory_space=pltpu.VMEM)] * 2,
+        scratch_shapes=[
+            pltpu.VMEM(held_shape, tokens.dtype),
+            pltpu.VMEM(held_shape, tokens.dtype),
+            pltpu.SemaphoreType.DMA((tile_count, 2)),
+            pltpu.SemaphoreType.DMA((tile_count, 2)),
+            pltpu.SemaphoreType.DMA((2,)),
+        ],
+        compiler_params=pltpu.CompilerParams(collective_id=1, has_side_effects=True),
+    )(tokens, cotangent)
+
+
 def shards(tokens, qkv_weight, cotangent):
     rep_count = lax.axis_size("rep")
     row_tiles = lax.axis_size("ty")
@@ -208,14 +285,17 @@
     outer_rows = tile_height // block_rows
     inner_rows = block_rows // tile_count
     split_shape = (outer_rows, tile_count, inner_rows, tile_width, channels)
-    grid_x, grid_g = (
-        lax.all_to_all(
-            tokens.reshape(split_shape), ("ty", "tx"), split_axis=1, concat_axis=1, tiled=True
-        ),
-        lax.all_to_all(
-            cotangent.reshape(split_shape), ("ty", "tx"), split_axis=1, concat_axis=1, tiled=True
-        ),
-    )
+    if tile_height == tile_count and outer_rows == 1 and inner_rows == 1:
+        grid_x, grid_g = (
+            values.reshape(split_shape) for values in exchange(tokens, cotangent)
+        )
+    else:
+        grid_x, grid_g = (
+            lax.all_to_all(
+                values.reshape(split_shape), ("ty", "tx"), split_axis=1, concat_axis=1, tiled=True
+            )
+            for values in (tokens, cotangent)
+        )
     token_shape = (
         outer_rows,
         row_tiles // fold_rows,

time: 142 us -> 135 us (0.951)
  the two profiles are of different devices: /device:TPU:1 before, /device:TPU:3 now
where the time goes in v5:
time: 135 us
  Pallas kernels  94.1 us (70%)
  matrix products  15 us (11%)
  starting transfers between devices  9.47 us (7%)
  local copies, waits for them, and re-layouts  8.09 us (6%)
  other arithmetic  7.26 us (5%)
    pallas_call x1, Pallas kernels, weight_sum(): pl.pallas_call(functools.partial(weight_sum_kernel, rep_count, tile_count...  67.6 us
    pallas_call x1, Pallas kernels, exchange(): pl.pallas_call(functools.partial(exchange_kernel, tile_count, col_tiles),...  26.5 us
    all_to_all x1, starting transfers between devices, shards(): lax.all_to_all(spread, ('ty', 'tx'), split_axis=1, concat_axis=1, tiled=T...  9.47 us
    sub x1, matrix products, window_grads(): exponent = jnp.exp(scores - peak_score)  5.13 us
  transfers between devices with their start and end apart: 1, of which 0 were waited for; matrix products, arithmetic and copies ran while one was open for 2% of the time, Pallas kernels for 50%

profile of v5, /device:TPU:3, one launch (start us, length us, event | category | flops | bytes accessed | tf_op | source)
XLA Modules:
  0.0 135.0 jit_solution(3637181575507774678)
XLA Ops:
  0.6 0.0 copy-start
  0.6 0.5 fusion.41
  1.2 0.6 iota_shift-right-logical_fusion
  1.8 26.5 %shard_map.50 = (bf16[64,4,512]{2,1,0:T(4,128)(2,1)}, bf16[64,4,512]{2,1,0:T(4,128)(2,1)}) custom-call(bf16[1,64,4,512]{3,2,1,0:T(4,128)(2,1)} %tokens_ref.1, bf16[1,64,4,512]{3,2,1,0:T(4,128)(2,1)} %cot_ref.1), custom_call_target="tpu_custom_call" | custom-call | tf_op jit(solution)/shard_map/pallas_call | solution.py:256
  28.2 1.2 reshape.242
  29.5 0.4 fusion.48
  29.9 0.1 div.47
  30.1 0.5 multiply_reduce_fusion.3
  30.6 0.3 copy.34
  30.9 0.1 reshape_reshape.4
  31.0 0.2 copy.35
  31.2 0.8 mul.107
  32.1 0.1 rsqrt.13
  32.2 0.0 copy-start.13
  32.2 0.4 reshape.241
  32.6 0.0 copy-start.15
  32.6 0.6 fusion.51
  33.3 0.8 fusion.50
  34.2 0.6 fusion.44
  34.8 5.1 %fusion.52 = (f32[4,16,64]{2,1,0:T(8,128)}, f32[4,16,64,64]{2,3,1,0:T(8,128)}) fusion(bf16[4,64,512,1]{2,1,3,0:T(8,128)(2,1)} %bitcast.69, bf16[16,512]{1,0:T(8,128)(2,1)S(1)} %get-tuple-element.12, bf16[4,64,512]{2,1,0:T(8,128)(2,1)S(1)} %bitcast.67), kind=kOutput, calls=%fused_computation.66 | convolution fusion | flops 271056960 | bytes 1605632 | tf_op jit(solution)/shard_map/sub | solution.py:46
  39.9 0.0 copy-done.5
  39.9 2.6 %fusion.23 = bf16[4,64,512]{2,1,0:T(8,128)(2,1)S(1)} fusion(bf16[4,64,512]{2,1,0:T(8,128)(2,1)S(1)} %copy-done.5, bf16[16,512]{1,0:T(8,128)(2,1)S(1)} %get-tuple-element.12, f32[4,16,64,64]{2,3,1,0:T(8,128)} %get-tuple-element.16, f32[4,16,64]{2,1,0:T(8,128)} %get-tuple-element.15), kind=kOutput, calls=%fused_computation.24 | convolution fusion | flops 271187968 | bytes 1605632 | tf_op jit(solution)/shard_map/wnqk,wnqc->wkc/dot_general | solution.py:50
  42.6 2.1 %multiply_reduce_fusion.1 = (f32[4,16,64]{2,1,0:T(8,128)S(1)}, f32[4,16,64,64]{2,3,1,0:T(8,128)S(1)}) fusion(f32[4,16,64,64]{2,3,1,0:T(8,128)S(1)} %copy-done.1, f32[4,16,64]{2,1,0:T(8,128)S(1)} %copy-done.10, bf16[4,64,512,1]{2,1,3,0:T(8,128)(2,1)S(1)} %bitcast.71, bf16[4,64,512]{2,1,0:T(8,128)(2,1)S(1)} %copy-done.5, ...), kind=kOutput, calls=%fused_computation.12 | convolution fusion | flops 271314944 | bytes 2670592 | tf_op jit(solution)/shard_map/wnqc,wkc->wnqk/dot_general | solution.py:49
  44.8 0.7 multiply_convert_fusion
  45.4 0.0 copy-start.9
  45.5 0.9 fusion.26
  46.4 0.0 copy-done.7
  46.4 1.3 multiply_reduce_fusion
  47.7 0.0 copy-start.3
  47.7 0.0 copy-start.12
  47.8 0.0 copy-start.14
  47.8 0.6 fusion.33
  48.4 0.1 copy-done.3
  48.5 0.8 fusion.49
  49.3 0.3 reshape.238
  49.6 0.0 copy-start.2
  49.7 0.8 div.55
  50.5 0.8 div.53
  51.2 1.5 %fusion.35 = bf16[1,8,2,4,1,2,2,512]{7,5,3,1,6,2,0,4:T(2,128)(2,1)S(1)} fusion(f32[2,2,8,4,2]{4,3,2,1,0:T(4,128)} %div.55, f32[2,2,8,4,2]{4,3,2,1,0:T(4,128)S(1)} %broadcast_multiply_fusion, f32[2,1,2,8,1,4,2,512]{7,6,5,3,2,0,4,1:T(2,128)S(1)} %reshape.238, f32[2,2,8,4,2]{4,3,2,1,0:T(4,128)} %div.53, f32[2,2,8,4,2]{4,3,2,1,0:T(4,128)S(1)} %add_rsqrt_fusion, ...), kind=kLoop, calls=%fused_computation.42 | loop fusion | flops 1179648 | bytes 1576960 | tf_op jit(solution)/shard_map/transpose | solution.py:329
  52.8 0.3 copy.17
  53.1 0.8 reshape.239
  53.9 9.5 %all-to-all-start = ((bf16[1,64,1,4,512]{4,3,2,0,1:T(4,128)(2,1)}), bf16[1,64,1,4,512]{4,3,2,0,1:T(4,128)(2,1)S(1)}, u32[]{:S(2)}, u32[]{:S(2)}) async-start(bf16[1,64,1,4,512]{4,3,2,0,1:T(4,128)(2,1)} %reshape.239), calls=%async_computation | async-start | bytes 524288 | tf_op jit(solution)/shard_map/all_to_all | solution.py:330
  63.4 0.1 copy.18
  63.5 1.7 %convolution_convert_fusion.blocks_ref = bf16[64,8,1536]{2,1,0:T(8,128)(2,1)} fusion(bf16[256,512]{1,0:T(8,128)(2,1)S(1)} %bitcast.73, bf16[256,512]{1,0:T(8,128)(2,1)S(1)} %bitcast.75, bf16[256,512]{1,0:T(8,128)(2,1)S(1)} %bitcast.66, bf16[512,256]{1,0:T(8,128)(2,1)S(1)} %copy.18), kind=kOutput, calls=%fused_computation.10 | convolution fusion | flops 405798912 | bytes 2621440 | tf_op jit(solution)/shard_map/dot_general | solution.py:77
  65.3 67.6 %shard_map.51 = f32[8,1536]{1,0:T(8,128)} custom-call(bf16[64,8,1536]{2,1,0:T(8,128)(2,1)} %convolution_convert_fusion.blocks_ref), custom_call_target="tpu_custom_call" | custom-call | tf_op jit(solution)/shard_map/pallas_call | solution.py:177
  132.9 1.4 %broadcast_multiply_fusion.1 = f32[8,1536]{1,0:T(8,128)} fusion(f32[8,1536]{1,0:T(8,128)} %shard_map.51), kind=kLoop, calls=%fused_computation.47 | loop fusion | flops 12288 | bytes 98304 | tf_op jit(solution)/shard_map/div | solution.py:334
  134.3 0.0 all-to-all-done
  134.3 0.7 copy.37
  (39 shorter events, 0.2 us)
Async XLA Ops:
  0.6 32.0 %copy-start = (bf16[512,1536]{1,0:T(8,128)(2,1)S(1)}, bf16[512,1536]{1,0:T(8,128)(2,1)}, u32[]{:S(2)}) copy-start(bf16[512,1536]{1,0:T(8,128)(2,1)} %param.4) | copy-start | bytes 4718596
  28.2 2.7 %copy-start.6 = (bf16[64,4,512]{2,1,0:T(4,128)(2,1)S(1)}, bf16[64,4,512]{2,1,0:T(4,128)(2,1)}, u32[]{:S(2)}) copy-start(bf16[64,4,512]{2,1,0:T(4,128)(2,1)} %get-tuple-element.4) | copy-start | bytes 786436
  30.1 2.5 %copy-start.11 = (f32[256]{0:T(256)}, f32[256]{0:T(256)S(1)}, u32[]{:S(2)}) copy-start(f32[256]{0:T(256)S(1)} %div.47) | copy-start | bytes 3076
  32.2 1.1 copy-start.13
  32.6 1.5 %copy-start.15 = (s32[512]{0:T(512)S(1)}, s32[512]{0:T(512)}, u32[]{:S(2)}) copy-start(s32[512]{0:T(512)} %get-tuple-element.19) | copy-start | bytes 6148
  32.6 1.5 %copy-start.16 = (s32[512]{0:T(512)S(1)}, s32[512]{0:T(512)}, u32[]{:S(2)}) copy-start(s32[512]{0:T(512)} %get-tuple-element.20) | copy-start | bytes 6148
  32.6 1.5 %copy-start.17 = (pred[512]{0:T(512)(128)(4,1)S(1)}, pred[512]{0:T(512)(128)(4,1)}, u32[]{:S(2)}) copy-start(pred[512]{0:T(512)(128)(4,1)} %fusion.41) | copy-start | bytes 1540
  34.8 5.1 %copy-start.5 = (bf16[4,64,512]{2,1,0:T(8,128)(2,1)S(1)}, bf16[4,64,512]{2,1,0:T(8,128)(2,1)}, u32[]{:S(2)}) copy-start(bf16[4,64,512]{2,1,0:T(8,128)(2,1)} %mul.107) | copy-start | bytes 786436
  39.9 2.7 %copy-start.1 = (f32[4,16,64,64]{2,3,1,0:T(8,128)S(1)}, f32[4,16,64,64]{2,3,1,0:T(8,128)}, u32[]{:S(2)}) copy-start(f32[4,16,64,64]{2,3,1,0:T(8,128)} %get-tuple-element.16) | copy-start | bytes 3145732
  39.9 2.7 %copy-start.8 = (bf16[256,512]{1,0:T(8,128)(2,1)S(1)}, bf16[256,512]{1,0:T(8,128)(2,1)}, u32[]{:S(2)}) copy-start(bf16[256,512]{1,0:T(8,128)(2,1)} %get-tuple-element.8) | copy-start | bytes 786436
  39.9 2.7 %copy-start.10 = (f32[4,16,64]{2,1,0:T(8,128)S(1)}, f32[4,16,64]{2,1,0:T(8,128)}, u32[]{:S(2)}) copy-start(f32[4,16,64]{2,1,0:T(8,128)} %get-tuple-element.15) | copy-start | bytes 49156
  42.6 5.2 %copy-start.18 = (bf16[4,64,512]{2,1,0:T(8,128)(2,1)}, bf16[4,64,512]{2,1,0:T(8,128)(2,1)S(1)}, u32[]{:S(2)}) copy-start(bf16[4,64,512]{2,1,0:T(8,128)(2,1)S(1)} %fusion.23) | copy-start | bytes 786436
  45.4 1.0 copy-start.7
  45.4 0.9 copy-start.9
  46.3 1.4 %copy-start.20 = (bf16[4,64,512]{2,1,0:T(8,128)(2,1)}, bf16[4,64,512]{2,1,0:T(8,128)(2,1)S(1)}, u32[]{:S(2)}) copy-start(bf16[4,64,512]{2,1,0:T(8,128)(2,1)S(1)} %fusion.26) | copy-start | bytes 786436
  47.7 0.7 copy-start.3
  47.7 0.7 copy-start.12
  47.8 0.7 copy-start.14
  49.6 13.8 %copy-start.2 = (bf16[512,256]{0,1:T(8,128)(2,1)S(1)}, bf16[512,256]{0,1:T(8,128)(2,1)}, u32[]{:S(2)}) copy-start(bf16[512,256]{0,1:T(8,128)(2,1)} %get-tuple-element.10) | copy-start | bytes 786436
  49.6 13.9 %copy-start.4 = (bf16[4,64,512]{2,1,0:T(8,128)(2,1)S(1)}, bf16[4,64,512]{2,1,0:T(8,128)(2,1)}, u32[]{:S(2)}) copy-start(bf16[4,64,512]{2,1,0:T(8,128)(2,1)} %copy-done.3) | copy-start | bytes 786436
  52.8 10.7 %copy-start.19 = (bf16[4,64,512]{2,1,0:T(8,128)(2,1)S(1)}, bf16[4,64,512]{2,1,0:T(8,128)(2,1)}, u32[]{:S(2)}) copy-start(bf16[4,64,512]{2,1,0:T(8,128)(2,1)} %copy-done.18) | copy-start | bytes 786436
  52.8 10.7 %copy-start.21 = (bf16[4,64,512]{2,1,0:T(8,128)(2,1)S(1)}, bf16[4,64,512]{2,1,0:T(8,128)(2,1)}, u32[]{:S(2)}) copy-start(bf16[4,64,512]{2,1,0:T(8,128)(2,1)} %copy-done.20) | copy-start | bytes 786436
  53.9 80.4 %all-to-all-start = ((bf16[1,64,1,4,512]{4,3,2,0,1:T(4,128)(2,1)}), bf16[1,64,1,4,512]{4,3,2,0,1:T(4,128)(2,1)S(1)}, u32[]{:S(2)}, u32[]{:S(2)}) async-start(bf16[1,64,1,4,512]{4,3,2,0,1:T(4,128)(2,1)} %reshape.239), calls=%async_computation | async-start | bytes 524288 | tf_op jit(solution)/shard_map/all_to_all | solution.py:330

commit v6 on v5

--- a/solution.py
+++ b/solution.py
@@ -86,8 +86,9 @@
     return (token_grad, weight_term)
 
 
-def weight_sum_kernel(rep_count, tile_count, col_tiles, blocks_ref, out_ref, arrived,
-                      partial, held, send_sems, recv_sems, rep_send_sems, rep_recv_sems):
+def weight_sum_kernel(rep_count, tile_count, col_tiles, blocks_ref, spread_ref, out_ref,
+                      returned_ref, arrived, partial, held, returned_held, send_sems, recv_sems,
+                      rep_send_sems, rep_recv_sems, back_send_sems, back_recv_sems, back_own_sem):
     me = lax.axis_index("rep")
     row = lax.axis_index("ty")
     col = lax.axis_index("tx")
@@ -112,6 +113,24 @@
                             device_id_type=pl.DeviceIdType.MESH)
 
     pl.semaphore_wait(barrier, tile_count + rep_count - 2)
+
+    def back_copy(step):
+        peer = lax.rem(tile + step, tile_count)
+        return pltpu.make_async_remote_copy(
+            src_ref=spread_ref.at[peer],
+            dst_ref=returned_held.at[tile],
+            send_sem=back_send_sems.at[step],
+            recv_sem=back_recv_sems.at[step],
+            device_id=tile_peer(step),
+            device_id_type=pl.DeviceIdType.MESH,
+        )
+
+    back_own = pltpu.make_async_copy(spread_ref.at[tile], returned_held.at[tile], back_own_sem.at[0])
+    back_own.start()
+
+    @pl.loop(1, tile_count)
+    def _(step):
+        back_copy(step).start()
 
     def tile_copy(step):
         peer = lax.rem(tile + step, tile_count)
@@ -163,33 +182,47 @@
     def _(step):
         rep_copy(step).wait()
 
+    back_own.wait()
+
+    @pl.loop(1, tile_count)
+    def _(step):
+        back_copy(step).wait()
+
+    returned_ref[...] = returned_held[...]
     total = held[0]
     for source in range(1, rep_count):
         total = total + held[source]
     out_ref[...] = total
 
 
-def weight_sum(row_blocks):
+def weight_sum(row_blocks, spread):
     rep_count = lax.axis_size("rep")
     col_tiles = lax.axis_size("tx")
     tile_count = row_blocks.shape[0]
     block_shape = row_blocks.shape[1:]
     return pl.pallas_call(
         functools.partial(weight_sum_kernel, rep_count, tile_count, col_tiles),
-        out_shape=jax.ShapeDtypeStruct(block_shape, jnp.float32),
-        in_specs=[pl.BlockSpec(memory_space=pltpu.VMEM)],
-        out_specs=pl.BlockSpec(memory_space=pltpu.VMEM),
+        out_shape=[
+            jax.ShapeDtypeStruct(block_shape, jnp.float32),
+            jax.ShapeDtypeStruct(spread.shape, spread.dtype),
+        ],
+        in_specs=[pl.BlockSpec(memory_space=pltpu.VMEM)] * 2,
+        out_specs=[pl.BlockSpec(memory_space=pltpu.VMEM)] * 2,
         scratch_shapes=[
             pltpu.VMEM(row_blocks.shape, row_blocks.dtype),
             pltpu.VMEM(block_shape, jnp.float32),
             pltpu.VMEM((rep_count,) + block_shape, jnp.float32),
+            pltpu.VMEM(spread.shape, spread.dtype),
             pltpu.SemaphoreType.DMA((tile_count,)),
             pltpu.SemaphoreType.DMA((tile_count,)),
             pltpu.SemaphoreType.DMA((rep_count,)),
             pltpu.SemaphoreType.DMA((rep_count,)),
+            pltpu.SemaphoreType.DMA((tile_count,)),
+            pltpu.SemaphoreType.DMA((tile_count,)),
+            pltpu.SemaphoreType.DMA((1,)),
         ],
         compiler_params=pltpu.CompilerParams(collective_id=0, has_side_effects=True),
-    )(row_blocks)
+    )(row_blocks, spread)
 
 
 def exchange_kernel(tile_count, col_tiles, tokens_ref, cot_ref, tokens_out, cot_out,
@@ -327,10 +360,16 @@
         channels,
     )
     spread = grad_windows.reshape(back_shape).transpose(4, 3, 0, 5, 1, 6, 2, 7).reshape(split_shape)
-    returned = lax.all_to_all(spread, ("ty", "tx"), split_axis=1, concat_axis=1, tiled=True)
+    row_blocks = weight_term.reshape(tile_count, channels // tile_count, weight_term.shape[1])
+    if tile_height == tile_count and outer_rows == 1 and inner_rows == 1:
+        weight_grad, returned = weight_sum(
+            row_blocks.astype(jnp.bfloat16), spread.reshape((tile_count,) + tokens.shape[2:])
+        )
+    else:
+        returned = lax.all_to_all(spread, ("ty", "tx"), split_axis=1, concat_axis=1, tiled=True)
+        gathered = lax.all_to_all(row_blocks.astype(jnp.bfloat16), ("ty", "tx"), 0, 0, tiled=True)
+        weight_grad = lax.psum(jnp.sum(gathered.astype(jnp.float32), axis=0), "rep")
     token_grad = returned.reshape(1, tile_height, tile_width, channels)
-    row_blocks = weight_term.reshape(tile_count, channels // tile_count, weight_term.shape[1])
-    weight_grad = weight_sum(row_blocks.astype(jnp.bfloat16))
     weight_grad = weight_grad / (rep_count * tile_count)
     return (token_grad, weight_grad)
 

time: 135 us -> 135 us (level)
  the two profiles are of different devices: /device:TPU:3 before, /device:TPU:7 now
where the time goes in v6:
time: 135 us; the launch traced here: 134 us
  Pallas kernels  100 us (74%)
  matrix products  16.7 us (12%)
  local copies, waits for them, and re-layouts  10.3 us (8%)
  other arithmetic  6.15 us (5%)
    pallas_call x1, Pallas kernels, weight_sum(): pl.pallas_call(functools.partial(weight_sum_kernel, rep_count, tile_count...  73 us
    pallas_call x1, Pallas kernels, exchange(): pl.pallas_call(functools.partial(exchange_kernel, tile_count, col_tiles),...  27 us
    sub x1, matrix products, window_grads(): exponent = jnp.exp(scores - peak_score)  5.13 us
    dot_general x1, matrix products, window_grads(): lax.dot_general(normed, proj_grad, (((0,), (0,)), ((), ())), preferred_el...  2.76 us

profile of v6, /device:TPU:7, one launch (start us, length us, event | category | flops | bytes accessed | tf_op | source)
XLA Modules:
  0.0 134.1 jit_solution(4539403863079311098)
XLA Ops:
  0.6 0.0 copy-start
  0.7 0.6 fusion.44
  1.3 27.0 %shard_map.50 = (bf16[64,4,512]{2,1,0:T(4,128)(2,1)}, bf16[64,4,512]{2,1,0:T(4,128)(2,1)}) custom-call(bf16[1,64,4,512]{3,2,1,0:T(4,128)(2,1)} %tokens_ref.1, bf16[1,64,4,512]{3,2,1,0:T(4,128)(2,1)} %cot_ref.1), custom_call_target="tpu_custom_call" | custom-call | tf_op jit(solution)/shard_map/pallas_call | solution.py:289
  28.3 0.0 copy-start.6
  28.3 1.2 reshape.239
  29.5 0.4 fusion.48
  30.0 0.7 div.46
  30.7 0.5 multiply_reduce_fusion.3
  31.2 0.7 rsqrt.13
  32.0 0.0 copy-done.6
  32.0 0.1 reshape_reshape.7
  32.1 0.2 copy.30
  32.3 0.8 mul.106
  33.1 0.3 copy.29
  33.4 0.4 reshape.237
  33.7 0.0 copy-done
  33.8 1.3 fusion.51
  35.1 0.9 fusion.50
  36.0 0.0 copy-start.5
  36.0 5.1 %fusion.52 = (f32[4,16,64]{2,1,0:T(8,128)}, f32[4,16,64,64]{2,3,1,0:T(8,128)}) fusion(bf16[4,64,512,1]{2,1,3,0:T(8,128)(2,1)} %bitcast.69, bf16[16,512]{1,0:T(8,128)(2,1)S(1)} %get-tuple-element.16, bf16[4,64,512]{2,1,0:T(8,128)(2,1)S(1)} %bitcast.66), kind=kOutput, calls=%fused_computation.66 | convolution fusion | flops 271056960 | bytes 1605632 | tf_op jit(solution)/shard_map/sub | solution.py:46
  41.1 0.0 copy-done.5
  41.1 2.6 %fusion.23 = bf16[4,64,512]{2,1,0:T(8,128)(2,1)S(1)} fusion(bf16[4,64,512]{2,1,0:T(8,128)(2,1)S(1)} %copy-done.5, bf16[16,512]{1,0:T(8,128)(2,1)S(1)} %get-tuple-element.16, f32[4,16,64,64]{2,3,1,0:T(8,128)} %get-tuple-element.20, f32[4,16,64]{2,1,0:T(8,128)} %get-tuple-element.19), kind=kOutput, calls=%fused_computation.24 | convolution fusion | flops 271187968 | bytes 1605632 | tf_op jit(solution)/shard_map/wnqk,wnqc->wkc/dot_general | solution.py:50
  43.8 0.0 copy-start.13
  43.8 0.0 copy-done.1
  43.8 0.0 copy-done.8
  43.8 2.1 %multiply_reduce_fusion.1 = (f32[4,16,64]{2,1,0:T(8,128)S(1)}, f32[4,16,64,64]{2,3,1,0:T(8,128)S(1)}) fusion(f32[4,16,64,64]{2,3,1,0:T(8,128)S(1)} %copy-done.1, f32[4,16,64]{2,1,0:T(8,128)S(1)} %copy-done.10, bf16[4,64,512,1]{2,1,3,0:T(8,128)(2,1)S(1)} %bitcast.71, bf16[4,64,512]{2,1,0:T(8,128)(2,1)S(1)} %copy-done.5, ...), kind=kOutput, calls=%fused_computation.12 | convolution fusion | flops 271314944 | bytes 2670592 | tf_op jit(solution)/shard_map/wnqc,wkc->wnqk/dot_general | solution.py:49
  46.0 0.7 multiply_convert_fusion
  46.6 0.0 copy-start.7
  46.6 0.0 copy-start.9
  46.6 0.9 fusion.26
  47.5 0.0 copy-done.7
  47.6 0.0 copy-done.9
  47.6 1.3 multiply_reduce_fusion
  49.0 0.6 fusion.33
  49.6 0.0 copy-done.3
  49.6 0.0 copy-done.12
  49.6 0.8 fusion.49
  50.5 0.3 reshape.235
  50.8 0.8 div.55
  51.6 0.8 div.53
  52.4 1.5 %fusion.35 = bf16[1,8,2,4,1,2,2,512]{7,5,3,1,6,2,0,4:T(2,128)(2,1)S(1)} fusion(f32[2,2,8,4,2]{4,3,2,1,0:T(4,128)} %div.55, f32[2,2,8,4,2]{4,3,2,1,0:T(4,128)S(1)} %broadcast_multiply_fusion, f32[2,1,2,8,1,4,2,512]{7,6,5,3,2,0,4,1:T(2,128)S(1)} %reshape.235, f32[2,2,8,4,2]{4,3,2,1,0:T(4,128)} %div.53, f32[2,2,8,4,2]{4,3,2,1,0:T(4,128)S(1)} %add_rsqrt_fusion, ...), kind=kLoop, calls=%fused_computation.42 | loop fusion | flops 1179648 | bytes 1576960 | tf_op jit(solution)/shard_map/transpose | solution.py:362
  54.0 0.3 copy.13
  54.3 0.8 reshape_reshape.8.spread_ref
  55.1 0.1 copy.10
  55.2 2.8 %convolution_convert_fusion.blocks_ref = bf16[64,8,1536]{2,1,0:T(8,128)(2,1)} fusion(bf16[256,512]{1,0:T(8,128)(2,1)} %bitcast.73, bf16[256,512]{1,0:T(8,128)(2,1)} %bitcast.75, bf16[256,512]{1,0:T(8,128)(2,1)S(1)} %bitcast.65, bf16[512,256]{1,0:T(8,128)(2,1)S(1)} %copy.10), kind=kOutput, calls=%fused_computation.10 | convolution fusion | flops 405798912 | bytes 2621440 | tf_op jit(solution)/shard_map/dot_general | solution.py:77
  58.0 73.0 %shard_map.51 = (f32[8,1536]{1,0:T(8,128)}, bf16[64,4,512]{2,1,0:T(4,128)(2,1)}) custom-call(bf16[64,8,1536]{2,1,0:T(8,128)(2,1)} %convolution_convert_fusion.blocks_ref, bf16[64,4,512]{2,1,0:T(4,128)(2,1)} %reshape_reshape.8.spread_ref), custom_call_target="tpu_custom_call" | custom-call | tf_op jit(solution)/shard_map/pallas_call | solution.py:203
  131.0 1.4 %broadcast_multiply_fusion.1 = f32[8,1536]{1,0:T(8,128)} fusion(f32[8,1536]{1,0:T(8,128)} %get-tuple-element.9), kind=kLoop, calls=%fused_computation.47 | loop fusion | flops 12288 | bytes 98304 | tf_op jit(solution)/shard_map/div | solution.py:373
  132.4 1.7 %copy.32 = bf16[1,64,4,512]{3,2,1,0:T(4,128)(2,1)} copy(bf16[1,64,4,512]{3,2,1,0:T(4,128)(2,1)} %bitcast.68) | data formatting | bytes 524288
  (23 shorter events, 0.2 us)
Async XLA Ops:
  0.6 33.1 %copy-start = (bf16[512,1536]{1,0:T(8,128)(2,1)S(1)}, bf16[512,1536]{1,0:T(8,128)(2,1)}, u32[]{:S(2)}) copy-start(bf16[512,1536]{1,0:T(8,128)(2,1)} %param.4) | copy-start | bytes 4718596
  28.3 3.7 %copy-start.6 = (bf16[64,4,512]{2,1,0:T(4,128)(2,1)S(1)}, bf16[64,4,512]{2,1,0:T(4,128)(2,1)}, u32[]{:S(2)}) copy-start(bf16[64,4,512]{2,1,0:T(4,128)(2,1)} %get-tuple-element.7) | copy-start | bytes 786436
  36.0 5.1 %copy-start.5 = (bf16[4,64,512]{2,1,0:T(8,128)(2,1)S(1)}, bf16[4,64,512]{2,1,0:T(8,128)(2,1)}, u32[]{:S(2)}) copy-start(bf16[4,64,512]{2,1,0:T(8,128)(2,1)} %mul.106) | copy-start | bytes 786436
  41.1 2.7 %copy-start.1 = (f32[4,16,64,64]{2,3,1,0:T(8,128)S(1)}, f32[4,16,64,64]{2,3,1,0:T(8,128)}, u32[]{:S(2)}) copy-start(f32[4,16,64,64]{2,3,1,0:T(8,128)} %get-tuple-element.20) | copy-start | bytes 3145732
  41.1 2.7 %copy-start.8 = (bf16[256,512]{1,0:T(8,128)(2,1)S(1)}, bf16[256,512]{1,0:T(8,128)(2,1)}, u32[]{:S(2)}) copy-start(bf16[256,512]{1,0:T(8,128)(2,1)} %get-tuple-element.12) | copy-start | bytes 786436
  41.1 2.7 %copy-start.10 = (f32[4,16,64]{2,1,0:T(8,128)S(1)}, f32[4,16,64]{2,1,0:T(8,128)}, u32[]{:S(2)}) copy-start(f32[4,16,64]{2,1,0:T(8,128)} %get-tuple-element.19) | copy-start | bytes 49156
  43.8 5.2 %copy-start.13 = (bf16[4,64,512]{2,1,0:T(8,128)(2,1)}, bf16[4,64,512]{2,1,0:T(8,128)(2,1)S(1)}, u32[]{:S(2)}) copy-start(bf16[4,64,512]{2,1,0:T(8,128)(2,1)S(1)} %fusion.23) | copy-start | bytes 786436
  46.6 1.0 copy-start.7
  46.6 0.9 copy-start.9
  47.6 1.4 %copy-start.14 = (bf16[4,64,512]{2,1,0:T(8,128)(2,1)}, bf16[4,64,512]{2,1,0:T(8,128)(2,1)S(1)}, u32[]{:S(2)}) copy-start(bf16[4,64,512]{2,1,0:T(8,128)(2,1)S(1)} %fusion.26) | copy-start | bytes 786436
  48.9 0.7 copy-start.3
  48.9 0.7 copy-start.11
  48.9 0.7 copy-start.12
  50.8 4.3 %copy-start.2 = (bf16[512,256]{0,1:T(8,128)(2,1)S(1)}, bf16[512,256]{0,1:T(8,128)(2,1)}, u32[]{:S(2)}) copy-start(bf16[512,256]{0,1:T(8,128)(2,1)} %get-tuple-element.14) | copy-start | bytes 786436
  50.8 4.4 %copy-start.4 = (bf16[4,64,512]{2,1,0:T(8,128)(2,1)S(1)}, bf16[4,64,512]{2,1,0:T(8,128)(2,1)}, u32[]{:S(2)}) copy-start(bf16[4,64,512]{2,1,0:T(8,128)(2,1)} %copy-done.3) | copy-start | bytes 786436

commit v7 on v6

--- a/solution.py
+++ b/solution.py
@@ -225,6 +225,221 @@
     )(row_blocks, spread)
 
 
+def paired_sum_kernel(rep_count, tile_count, col_tiles, blocks_ref, spread_ref, out_ref,
+                      returned_ref, pair_held, pair_sum, arrived, partial, held, final,
+                      returned_held, pair_sems, tile_send_sems, tile_recv_sems, zh_send_sems,
+                      zh_recv_sems, final_sems, back_send_sems, back_recv_sems, own_sems):
+    me = lax.axis_index("rep")
+    row = lax.axis_index("ty")
+    col = lax.axis_index("tx")
+    tile = row * col_tiles + col
+    core = lax.rem(me, 2)
+    plane = me // 2
+    planes = rep_count // 2
+    partner = me + 1 - 2 * core
+    half = tile_count // 2
+    mine_start = core * half
+    receiver = tile // half == core
+    barrier = pltpu.get_barrier_semaphore()
+
+    def tile_device(peer):
+        return (me, peer // col_tiles, lax.rem(peer, col_tiles))
+
+    def tile_peer(step):
+        return tile_device(lax.rem(tile + step, tile_count))
+
+    def plane_peer(step):
+        return (2 * lax.rem(plane + step, planes) + core, row, col)
+
+    mesh_id = pl.DeviceIdType.MESH
+    pl.semaphore_signal(barrier, inc=1, device_id=(partner, row, col), device_id_type=mesh_id)
+
+    @pl.loop(1, tile_count)
+    def _(step):
+        pl.semaphore_signal(barrier, inc=1, device_id=tile_peer(step), device_id_type=mesh_id)
+
+    @pl.when(receiver)
+    def _():
+        @pl.loop(1, planes)
+        def _(step):
+            pl.semaphore_signal(barrier, inc=1, device_id=plane_peer(step), device_id_type=mesh_id)
+
+    pl.semaphore_wait(barrier, tile_count + (planes - 1) * receiver.astype(jnp.int32))
+
+    pair_copy = pltpu.make_async_remote_copy(
+        src_ref=blocks_ref.at[pl.ds((1 - core) * half, half)],
+        dst_ref=pair_held,
+        send_sem=pair_sems.at[0],
+        recv_sem=pair_sems.at[1],
+        device_id=(partner, row, col),
+        device_id_type=mesh_id,
+    )
+    pair_copy.start()
+
+    def back_copy(step):
+        peer = lax.rem(tile + step, tile_count)
+        return pltpu.make_async_remote_copy(
+            src_ref=spread_ref.at[peer],
+            dst_ref=returned_held.at[tile],
+            send_sem=back_send_sems.at[step],
+            recv_sem=back_recv_sems.at[step],
+            device_id=tile_peer(step),
+            device_id_type=mesh_id,
+        )
+
+    back_own = pltpu.make_async_copy(spread_ref.at[tile], returned_held.at[tile], own_sems.at[0])
+    back_own.start()
+
+    @pl.loop(1, tile_count)
+    def _(step):
+        back_copy(step).start()
+
+    pair_copy.wait()
+
+    @pl.loop(0, half)
+    def _(index):
+        pair_sum[index] = (
+            blocks_ref[mine_start + index].astype(jnp.float32)
+            + pair_held[index].astype(jnp.float32)
+        ).astype(pair_sum.dtype)
+
+    def sum_copy(index):
+        target = mine_start + index
+        step = lax.rem(target - tile + tile_count, tile_count)
+        return pltpu.make_async_remote_copy(
+            src_ref=pair_sum.at[index],
+            dst_ref=arrived.at[tile],
+            send_sem=tile_send_sems.at[step],
+            recv_sem=tile_recv_sems.at[step],
+            device_id=tile_device(target),
+            device_id_type=mesh_id,
+        )
+
+    @pl.loop(0, half)
+    def _(index):
+        @pl.when(mine_start + index != tile)
+        def _():
+            sum_copy(index).start()
+
+    def final_copy():
+        return pltpu.make_async_remote_copy(
+            src_ref=final,
+            dst_ref=final,
+            send_sem=final_sems.at[0],
+            recv_sem=final_sems.at[1],
+            device_id=(partner, row, col),
+            device_id_type=mesh_id,
+        )
+
+    @pl.when(receiver)
+    def _():
+        own = pltpu.make_async_copy(
+            pair_sum.at[tile - mine_start], arrived.at[tile], own_sems.at[1]
+        )
+        own.start()
+        own.wait()
+
+        @pl.loop(1, tile_count)
+        def _(step):
+            pltpu.make_async_remote_copy(
+                src_ref=pair_sum.at[0],
+                dst_ref=arrived.at[tile],
+                send_sem=tile_send_sems.at[step],
+                recv_sem=tile_recv_sems.at[step],
+                device_id=tile_peer(step),
+                device_id_type=mesh_id,
+            ).wait_recv()
+
+        def add_source(source, total):
+            return total + arrived[source].astype(jnp.float32)
+
+        partial[...] = lax.fori_loop(
+            0, tile_count, add_source, jnp.zeros(partial.shape, jnp.float32)
+        )
+        held[plane] = partial[...]
+
+        def plane_copy(step):
+            return pltpu.make_async_remote_copy(
+                src_ref=partial,
+                dst_ref=held.at[plane],
+                send_sem=zh_send_sems.at[step],
+                recv_sem=zh_recv_sems.at[step],
+                device_id=plane_peer(step),
+                device_id_type=mesh_id,
+            )
+
+        @pl.loop(1, planes)
+        def _(step):
+            plane_copy(step).start()
+
+        @pl.loop(1, planes)
+        def _(step):
+            plane_copy(step).wait()
+
+        total = held[0]
+        for source in range(1, planes):
+            total = total + held[source]
+        final[...] = total
+        copy = final_copy()
+        copy.start()
+        copy.wait_send()
+
+    @pl.when(jnp.logical_not(receiver))
+    def _():
+        final_copy().wait_recv()
+
+    @pl.loop(0, half)
+    def _(index):
+        @pl.when(mine_start + index != tile)
+        def _():
+            sum_copy(index).wait_send()
+
+    back_own.wait()
+
+    @pl.loop(1, tile_count)
+    def _(step):
+        back_copy(step).wait()
+
+    returned_ref[...] = returned_held[...]
+    out_ref[...] = final[...]
+
+
+def paired_sum(row_blocks, spread):
+    rep_count = lax.axis_size("rep")
+    col_tiles = lax.axis_size("tx")
+    tile_count = row_blocks.shape[0]
+    block_shape = row_blocks.shape[1:]
+    half_shape = (tile_count // 2,) + block_shape
+    return pl.pallas_call(
+        functools.partial(paired_sum_kernel, rep_count, tile_count, col_tiles),
+        out_shape=[
+            jax.ShapeDtypeStruct(block_shape, jnp.float32),
+            jax.ShapeDtypeStruct(spread.shape, spread.dtype),
+        ],
+        in_specs=[pl.BlockSpec(memory_space=pltpu.VMEM)] * 2,
+        out_specs=[pl.BlockSpec(memory_space=pltpu.VMEM)] * 2,
+        scratch_shapes=[
+            pltpu.VMEM(half_shape, row_blocks.dtype),
+            pltpu.VMEM(half_shape, row_blocks.dtype),
+            pltpu.VMEM(row_blocks.shape, row_blocks.dtype),
+            pltpu.VMEM(block_shape, jnp.float32),
+            pltpu.VMEM((rep_count // 2,) + block_shape, jnp.float32),
+            pltpu.VMEM(block_shape, jnp.float32),
+            pltpu.VMEM(spread.shape, spread.dtype),
+            pltpu.SemaphoreType.DMA((2,)),
+            pltpu.SemaphoreType.DMA((tile_count,)),
+            pltpu.SemaphoreType.DMA((tile_count,)),
+            pltpu.SemaphoreType.DMA((rep_count // 2,)),
+            pltpu.SemaphoreType.DMA((rep_count // 2,)),
+            pltpu.SemaphoreType.DMA((2,)),
+            pltpu.SemaphoreType.DMA((tile_count,)),
+            pltpu.SemaphoreType.DMA((tile_count,)),
+            pltpu.SemaphoreType.DMA((2,)),
+        ],
+        compiler_params=pltpu.CompilerParams(collective_id=2, has_side_effects=True),
+    )(row_blocks, spread)
+
+
 def exchange_kernel(tile_count, col_tiles, tokens_ref, cot_ref, tokens_out, cot_out,
                     tokens_held, cot_held, send_sems, recv_sems, own_sems):
     me = lax.axis_index("rep")
@@ -362,7 +577,7 @@
     spread = grad_windows.reshape(back_shape).transpose(4, 3, 0, 5, 1, 6, 2, 7).reshape(split_shape)
     row_blocks = weight_term.reshape(tile_count, channels // tile_count, weight_term.shape[1])
     if tile_height == tile_count and outer_rows == 1 and inner_rows == 1:
-        weight_grad, returned = weight_sum(
+        weight_grad, returned = paired_sum(
             row_blocks.astype(jnp.bfloat16), spread.reshape((tile_count,) + tokens.shape[2:])
         )
     else:

time: 135 us -> 114 us (0.84)
  the two profiles are of different devices: /device:TPU:7 before, /device:TPU:63 now
where the time goes in v7:
time: 114 us; the launch traced here: 113 us
  Pallas kernels  79.2 us (69%)
  matrix products  16.8 us (15%)
  local copies, waits for them, and re-layouts  10.3 us (9%)
  other arithmetic  6.15 us (5%)
    pallas_call x1, Pallas kernels, paired_sum(): pl.pallas_call(functools.partial(paired_sum_kernel, rep_count, tile_count...  51.8 us
    pallas_call x1, Pallas kernels, exchange(): pl.pallas_call(functools.partial(exchange_kernel, tile_count, col_tiles),...  27.5 us
    sub x1, matrix products, window_grads(): exponent = jnp.exp(scores - peak_score)  5.13 us
    dot_general x1, matrix products, window_grads(): lax.dot_general(normed, proj_grad, (((0,), (0,)), ((), ())), preferred_el...  2.76 us
    dot_general x1, matrix products, window_grads(): jnp.einsum('wnqk,wnqc->wkc', probs_low, grad_spread, preferred_element_ty...  2.63 us

profile of v7, /device:TPU:63, one launch (start us, length us, event | category | flops | bytes accessed | tf_op | source)
XLA Modules:
  0.0 113.4 jit_solution(2906048961330224678)
XLA Ops:
  0.6 0.0 copy-start
  0.7 0.6 fusion.44
  1.3 27.5 %shard_map.50 = (bf16[64,4,512]{2,1,0:T(4,128)(2,1)}, bf16[64,4,512]{2,1,0:T(4,128)(2,1)}) custom-call(bf16[1,64,4,512]{3,2,1,0:T(4,128)(2,1)} %tokens_ref.1, bf16[1,64,4,512]{3,2,1,0:T(4,128)(2,1)} %cot_ref.1), custom_call_target="tpu_custom_call" | custom-call | tf_op jit(solution)/shard_map/pallas_call | solution.py:504
  28.8 1.2 %reshape.239 = f32[1,8,2,4,1,2,2,512]{7,6,5,3,2,1,4,0:T(2,128)S(1)} reshape(bf16[64,4,512]{2,1,0:T(4,128)(2,1)} %get-tuple-element.6) | data formatting | bytes 786432 | tf_op jit(solution)/shard_map/convert_element_type | solution.py:26
  30.0 0.4 fusion.48
  30.4 0.7 div.46
  31.2 0.5 multiply_reduce_fusion.3
  31.7 0.7 rsqrt.13
  32.4 0.0 copy-done.6
  32.4 0.1 reshape_reshape.7
  32.6 0.2 copy.30
  32.8 0.8 mul.106
  33.6 0.3 copy.29
  33.9 0.4 reshape.237
  34.2 0.0 copy-done
  34.2 1.3 %fusion.51 = (bf16[256,1536]{1,0:T(8,128)(2,1)S(1)}, f32[256,1536]{1,0:T(8,128)S(1)}) fusion(bf16[512,1536]{1,0:T(8,128)(2,1)S(1)} %copy-done, f32[256,512]{1,0:T(8,128)S(1)} %reshape.237, f32[256]{0:T(256)} %rsqrt.13, f32[256]{0:T(256)} %div.46), kind=kOutput, calls=%fused_computation.65 | convolution fusion | flops 403439616 | bytes 4458496 | tf_op jit(solution)/shard_map/dot_general | solution.py:28
  35.6 0.9 fusion.50
  36.5 0.0 copy-start.5
  36.5 5.1 %fusion.52 = (f32[4,16,64]{2,1,0:T(8,128)}, f32[4,16,64,64]{2,3,1,0:T(8,128)}) fusion(bf16[4,64,512,1]{2,1,3,0:T(8,128)(2,1)} %bitcast.69, bf16[16,512]{1,0:T(8,128)(2,1)S(1)} %get-tuple-element.16, bf16[4,64,512]{2,1,0:T(8,128)(2,1)S(1)} %bitcast.66), kind=kOutput, calls=%fused_computation.66 | convolution fusion | flops 271056960 | bytes 1605632 | tf_op jit(solution)/shard_map/sub | solution.py:46
  41.6 0.0 copy-done.5
  41.6 2.6 %fusion.23 = bf16[4,64,512]{2,1,0:T(8,128)(2,1)S(1)} fusion(bf16[4,64,512]{2,1,0:T(8,128)(2,1)S(1)} %copy-done.5, bf16[16,512]{1,0:T(8,128)(2,1)S(1)} %get-tuple-element.16, f32[4,16,64,64]{2,3,1,0:T(8,128)} %get-tuple-element.20, f32[4,16,64]{2,1,0:T(8,128)} %get-tuple-element.19), kind=kOutput, calls=%fused_computation.24 | convolution fusion | flops 271187968 | bytes 1605632 | tf_op jit(solution)/shard_map/wnqk,wnqc->wkc/dot_general | solution.py:50
  44.3 0.0 copy-start.13
  44.3 2.1 %multiply_reduce_fusion.1 = (f32[4,16,64]{2,1,0:T(8,128)S(1)}, f32[4,16,64,64]{2,3,1,0:T(8,128)S(1)}) fusion(f32[4,16,64,64]{2,3,1,0:T(8,128)S(1)} %copy-done.1, f32[4,16,64]{2,1,0:T(8,128)S(1)} %copy-done.10, bf16[4,64,512,1]{2,1,3,0:T(8,128)(2,1)S(1)} %bitcast.71, bf16[4,64,512]{2,1,0:T(8,128)(2,1)S(1)} %copy-done.5, ...), kind=kOutput, calls=%fused_computation.12 | convolution fusion | flops 271314944 | bytes 2670592 | tf_op jit(solution)/shard_map/wnqc,wkc->wnqk/dot_general | solution.py:49
  46.4 0.7 multiply_convert_fusion
  47.1 0.0 copy-start.9
  47.1 0.9 fusion.26
  48.0 0.0 copy-done.7
  48.1 1.3 %multiply_reduce_fusion = f32[4,64,512]{2,1,0:T(8,128)S(1)} fusion(f32[16,512]{1,0:T(8,128)S(1)} %copy-done.9, bf16[4,16,64,64]{2,3,1,0:T(8,128)(2,1)S(1)} %multiply_convert_fusion, bf16[4,64,512,1]{2,1,3,0:T(8,128)(2,1)S(1)} %bitcast.70), kind=kOutput, calls=%fused_computation.1 | convolution fusion | flops 272498688 | bytes 1343488 | tf_op jit(solution)/shard_map/wnqk,wkc->wnqc/dot_general | solution.py:59
  49.4 0.0 copy-start.3
  49.4 0.0 copy-start.11
  49.4 0.0 copy-start.12
  49.4 0.0 copy-done.13
  49.4 0.0 copy-done.14
  49.5 0.6 fusion.33
  50.1 0.0 copy-done.3
  50.1 0.0 copy-done.12
  50.1 0.8 fusion.49
  51.0 0.3 reshape.235
  51.3 0.8 div.55
  52.1 0.8 div.53
  52.9 1.5 %fusion.35 = bf16[1,8,2,4,1,2,2,512]{7,5,3,1,6,2,0,4:T(2,128)(2,1)S(1)} fusion(f32[2,2,8,4,2]{4,3,2,1,0:T(4,128)} %div.55, f32[2,2,8,4,2]{4,3,2,1,0:T(4,128)S(1)} %broadcast_multiply_fusion, f32[2,1,2,8,1,4,2,512]{7,6,5,3,2,0,4,1:T(2,128)S(1)} %reshape.235, f32[2,2,8,4,2]{4,3,2,1,0:T(4,128)} %div.53, f32[2,2,8,4,2]{4,3,2,1,0:T(4,128)S(1)} %add_rsqrt_fusion, ...), kind=kLoop, calls=%fused_computation.42 | loop fusion | flops 1179648 | bytes 1576960 | tf_op jit(solution)/shard_map/transpose | solution.py:577
  54.5 0.3 copy.13
  54.7 0.8 reshape_reshape.8.spread_ref
  55.6 0.1 copy.10
  55.7 2.8 %convolution_convert_fusion.blocks_ref = bf16[64,8,1536]{2,1,0:T(8,128)(2,1)} fusion(bf16[256,512]{1,0:T(8,128)(2,1)} %bitcast.73, bf16[256,512]{1,0:T(8,128)(2,1)} %bitcast.75, bf16[256,512]{1,0:T(8,128)(2,1)S(1)} %bitcast.65, bf16[512,256]{1,0:T(8,128)(2,1)S(1)} %copy.10), kind=kOutput, calls=%fused_computation.10 | convolution fusion | flops 405798912 | bytes 2621440 | tf_op jit(solution)/shard_map/dot_general | solution.py:77
  58.5 51.8 %shard_map.51 = (f32[8,1536]{1,0:T(8,128)}, bf16[64,4,512]{2,1,0:T(4,128)(2,1)}) custom-call(bf16[64,8,1536]{2,1,0:T(8,128)(2,1)} %convolution_convert_fusion.blocks_ref, bf16[64,4,512]{2,1,0:T(4,128)(2,1)} %reshape_reshape.8.spread_ref), custom_call_target="tpu_custom_call" | custom-call | tf_op jit(solution)/shard_map/pallas_call | solution.py:413
  110.2 1.4 %broadcast_multiply_fusion.1 = f32[8,1536]{1,0:T(8,128)} fusion(f32[8,1536]{1,0:T(8,128)} %get-tuple-element.9), kind=kLoop, calls=%fused_computation.47 | loop fusion | flops 12288 | bytes 98304 | tf_op jit(solution)/shard_map/div | solution.py:588
  111.7 1.7 %copy.32 = bf16[1,64,4,512]{3,2,1,0:T(4,128)(2,1)} copy(bf16[1,64,4,512]{3,2,1,0:T(4,128)(2,1)} %bitcast.68) | data formatting | bytes 524288
  (23 shorter events, 0.2 us)
Async XLA Ops:
  0.6 33.6 %copy-start = (bf16[512,1536]{1,0:T(8,128)(2,1)S(1)}, bf16[512,1536]{1,0:T(8,128)(2,1)}, u32[]{:S(2)}) copy-start(bf16[512,1536]{1,0:T(8,128)(2,1)} %param.4) | copy-start | bytes 4718596
  28.8 3.7 %copy-start.6 = (bf16[64,4,512]{2,1,0:T(4,128)(2,1)S(1)}, bf16[64,4,512]{2,1,0:T(4,128)(2,1)}, u32[]{:S(2)}) copy-start(bf16[64,4,512]{2,1,0:T(4,128)(2,1)} %get-tuple-element.7) | copy-start | bytes 786436
  36.5 5.1 %copy-start.5 = (bf16[4,64,512]{2,1,0:T(8,128)(2,1)S(1)}, bf16[4,64,512]{2,1,0:T(8,128)(2,1)}, u32[]{:S(2)}) copy-start(bf16[4,64,512]{2,1,0:T(8,128)(2,1)} %mul.106) | copy-start | bytes 786436
  41.6 2.7 %copy-start.1 = (f32[4,16,64,64]{2,3,1,0:T(8,128)S(1)}, f32[4,16,64,64]{2,3,1,0:T(8,128)}, u32[]{:S(2)}) copy-start(f32[4,16,64,64]{2,3,1,0:T(8,128)} %get-tuple-element.20) | copy-start | bytes 3145732
  41.6 2.7 %copy-start.8 = (bf16[256,512]{1,0:T(8,128)(2,1)S(1)}, bf16[256,512]{1,0:T(8,128)(2,1)}, u32[]{:S(2)}) copy-start(bf16[256,512]{1,0:T(8,128)(2,1)} %get-tuple-element.12) | copy-start | bytes 786436
  41.6 2.7 %copy-start.10 = (f32[4,16,64]{2,1,0:T(8,128)S(1)}, f32[4,16,64]{2,1,0:T(8,128)}, u32[]{:S(2)}) copy-start(f32[4,16,64]{2,1,0:T(8,128)} %get-tuple-element.19) | copy-start | bytes 49156
  44.3 5.2 %copy-start.13 = (bf16[4,64,512]{2,1,0:T(8,128)(2,1)}, bf16[4,64,512]{2,1,0:T(8,128)(2,1)S(1)}, u32[]{:S(2)}) copy-start(bf16[4,64,512]{2,1,0:T(8,128)(2,1)S(1)} %fusion.23) | copy-start | bytes 786436
  47.1 1.0 copy-start.7
  47.1 0.9 copy-start.9
  48.1 1.4 %copy-start.14 = (bf16[4,64,512]{2,1,0:T(8,128)(2,1)}, bf16[4,64,512]{2,1,0:T(8,128)(2,1)S(1)}, u32[]{:S(2)}) copy-start(bf16[4,64,512]{2,1,0:T(8,128)(2,1)S(1)} %fusion.26) | copy-start | bytes 786436
  49.4 0.7 copy-start.3
  49.4 0.7 copy-start.11
  49.4 0.7 copy-start.12
  51.3 4.3 %copy-start.2 = (bf16[512,256]{0,1:T(8,128)(2,1)S(1)}, bf16[512,256]{0,1:T(8,128)(2,1)}, u32[]{:S(2)}) copy-start(bf16[512,256]{0,1:T(8,128)(2,1)} %get-tuple-element.14) | copy-start | bytes 786436
  51.3 4.4 %copy-start.4 = (bf16[4,64,512]{2,1,0:T(8,128)(2,1)S(1)}, bf16[4,64,512]{2,1,0:T(8,128)(2,1)}, u32[]{:S(2)}) copy-start(bf16[4,64,512]{2,1,0:T(8,128)(2,1)} %copy-done.3) | copy-start | bytes 786436

commit v8 on v7

--- a/solution.py
+++ b/solution.py
@@ -440,6 +440,207 @@
     )(row_blocks, spread)
 
 
+def balanced_sum_kernel(rep_count, tile_count, col_tiles, blocks_ref, spread_ref, out_ref,
+                        returned_ref, pair_held, pair_sum, arrived, partial, held,
+                        returned_held, pair_sems, sum_send_sems, sum_recv_sems, rep_send_sems,
+                        rep_recv_sems, back_send_sems, back_recv_sems, own_sems):
+    me = lax.axis_index("rep")
+    row = lax.axis_index("ty")
+    col = lax.axis_index("tx")
+    tile = row * col_tiles + col
+    core = lax.rem(me, 2)
+    partner = me + 1 - 2 * core
+    target_rep = me - core + lax.rem(tile, 2)
+    half = tile_count // 2
+    mine_start = core * half
+    barrier = pltpu.get_barrier_semaphore()
+    mesh_id = pl.DeviceIdType.MESH
+
+    def tile_device(rep, peer):
+        return (rep, peer // col_tiles, lax.rem(peer, col_tiles))
+
+    def tile_peer(step):
+        return tile_device(me, lax.rem(tile + step, tile_count))
+
+    def rep_peer(step):
+        return (lax.rem(me + step, rep_count), row, col)
+
+    @pl.loop(1, tile_count)
+    def _(step):
+        pl.semaphore_signal(barrier, inc=1, device_id=tile_peer(step), device_id_type=mesh_id)
+
+    @pl.loop(0, tile_count)
+    def _(peer):
+        pl.semaphore_signal(
+            barrier, inc=1, device_id=tile_device(partner, peer), device_id_type=mesh_id
+        )
+
+    @pl.loop(1, rep_count)
+    def _(step):
+        @pl.when(lax.rem(me + step, rep_count) != partner)
+        def _():
+            pl.semaphore_signal(barrier, inc=1, device_id=rep_peer(step), device_id_type=mesh_id)
+
+    pl.semaphore_wait(barrier, 2 * tile_count + rep_count - 3)
+
+    pair_copy = pltpu.make_async_remote_copy(
+        src_ref=blocks_ref.at[pl.ds((1 - core) * half, half)],
+        dst_ref=pair_held,
+        send_sem=pair_sems.at[0],
+        recv_sem=pair_sems.at[1],
+        device_id=(partner, row, col),
+        device_id_type=mesh_id,
+    )
+    pair_copy.start()
+
+    def back_copy(step):
+        peer = lax.rem(tile + step, tile_count)
+        return pltpu.make_async_remote_copy(
+            src_ref=spread_ref.at[peer],
+            dst_ref=returned_held.at[tile],
+            send_sem=back_send_sems.at[step],
+            recv_sem=back_recv_sems.at[step],
+            device_id=tile_peer(step),
+            device_id_type=mesh_id,
+        )
+
+    back_own = pltpu.make_async_copy(spread_ref.at[tile], returned_held.at[tile], own_sems.at[0])
+    back_own.start()
+
+    @pl.loop(1, tile_count)
+    def _(step):
+        back_copy(step).start()
+
+    pair_copy.wait()
+
+    @pl.loop(0, half)
+    def _(index):
+        pair_sum[index] = (
+            blocks_ref[mine_start + index].astype(jnp.float32)
+            + pair_held[index].astype(jnp.float32)
+        ).astype(pair_sum.dtype)
+
+    def is_self(target):
+        return jnp.logical_and(target_rep == me, target == tile)
+
+    def sum_copy(index):
+        target = mine_start + index
+        return pltpu.make_async_remote_copy(
+            src_ref=pair_sum.at[index],
+            dst_ref=arrived.at[tile],
+            send_sem=sum_send_sems.at[index],
+            recv_sem=sum_recv_sems.at[tile],
+            device_id=tile_device(target_rep, target),
+            device_id_type=mesh_id,
+        )
+
+    @pl.loop(0, half)
+    def _(index):
+        target = mine_start + index
+
+        @pl.when(is_self(target))
+        def _():
+            own = pltpu.make_async_copy(pair_sum.at[index], arrived.at[tile], own_sems.at[1])
+            own.start()
+            own.wait()
+
+        @pl.when(jnp.logical_not(is_self(target)))
+        def _():
+            sum_copy(index).start()
+
+    @pl.loop(0, half)
+    def _(index):
+        source = core + 2 * index
+        from_self = jnp.logical_and(source == tile, tile // half == core)
+
+        @pl.when(jnp.logical_not(from_self))
+        def _():
+            pltpu.make_async_remote_copy(
+                src_ref=pair_sum.at[0],
+                dst_ref=arrived.at[source],
+                send_sem=sum_send_sems.at[0],
+                recv_sem=sum_recv_sems.at[source],
+                device_id=tile_peer(1),
+                device_id_type=mesh_id,
+            ).wait_recv()
+
+    def add_source(index, total):
+        return total + arrived[core + 2 * index].astype(jnp.float32)
+
+    partial[...] = lax.fori_loop(0, half, add_source, jnp.zeros(partial.shape, jnp.float32))
+    held[me] = partial[...]
+
+    def rep_copy(step):
+        return pltpu.make_async_remote_copy(
+            src_ref=partial,
+            dst_ref=held.at[me],
+            send_sem=rep_send_sems.at[step],
+            recv_sem=rep_recv_sems.at[step],
+            device_id=rep_peer(step),
+            device_id_type=mesh_id,
+        )
+
+    @pl.loop(1, rep_count)
+    def _(step):
+        rep_copy(step).start()
+
+    @pl.loop(1, rep_count)
+    def _(step):
+        rep_copy(step).wait()
+
+    @pl.loop(0, half)
+    def _(index):
+        @pl.when(jnp.logical_not(is_self(mine_start + index)))
+        def _():
+            sum_copy(index).wait_send()
+
+    back_own.wait()
+
+    @pl.loop(1, tile_count)
+    def _(step):
+        back_copy(step).wait()
+
+    returned_ref[...] = returned_held[...]
+    total = held[0]
+    for source in range(1, rep_count):
+        total = total + held[source]
+    out_ref[...] = total
+
+
+def balanced_sum(row_blocks, spread):
+    rep_count = lax.axis_size("rep")
+    col_tiles = lax.axis_size("tx")
+    tile_count = row_blocks.shape[0]
+    block_shape = row_blocks.shape[1:]
+    half_shape = (tile_count // 2,) + block_shape
+    return pl.pallas_call(
+        functools.partial(balanced_sum_kernel, rep_count, tile_count, col_tiles),
+        out_shape=[
+            jax.ShapeDtypeStruct(block_shape, jnp.float32),
+            jax.ShapeDtypeStruct(spread.shape, spread.dtype),
+        ],
+        in_specs=[pl.BlockSpec(memory_space=pltpu.VMEM)] * 2,
+        out_specs=[pl.BlockSpec(memory_space=pltpu.VMEM)] * 2,
+        scratch_shapes=[
+            pltpu.VMEM(half_shape, row_blocks.dtype),
+            pltpu.VMEM(half_shape, row_blocks.dtype),
+            pltpu.VMEM(row_blocks.shape, row_blocks.dtype),
+            pltpu.VMEM(block_shape, jnp.float32),
+            pltpu.VMEM((rep_count,) + block_shape, jnp.float32),
+            pltpu.VMEM(spread.shape, spread.dtype),
+            pltpu.SemaphoreType.DMA((2,)),
+            pltpu.SemaphoreType.DMA((tile_count // 2,)),
+            pltpu.SemaphoreType.DMA((tile_count,)),
+            pltpu.SemaphoreType.DMA((rep_count,)),
+            pltpu.SemaphoreType.DMA((rep_count,)),
+            pltpu.SemaphoreType.DMA((tile_count,)),
+            pltpu.SemaphoreType.DMA((tile_count,)),
+            pltpu.SemaphoreType.DMA((2,)),
+        ],
+        compiler_params=pltpu.CompilerParams(collective_id=3, has_side_effects=True),
+    )(row_blocks, spread)
+
+
 def exchange_kernel(tile_count, col_tiles, tokens_ref, cot_ref, tokens_out, cot_out,
                     tokens_held, cot_held, send_sems, recv_sems, own_sems):
     me = lax.axis_index("rep")
@@ -577,7 +778,7 @@
     spread = grad_windows.reshape(back_shape).transpose(4, 3, 0, 5, 1, 6, 2, 7).reshape(split_shape)
     row_blocks = weight_term.reshape(tile_count, channels // tile_count, weight_term.shape[1])
     if tile_height == tile_count and outer_rows == 1 and inner_rows == 1:
-        weight_grad, returned = paired_sum(
+        weight_grad, returned = balanced_sum(
             row_blocks.astype(jnp.bfloat16), spread.reshape((tile_count,) + tokens.shape[2:])
         )
     else:

time: 114 us -> 119 us (1.044)
  Pallas kernels: 79.2 us -> 83.9 us
    pallas_call x1, Pallas kernels: 51.8 us -> 56.5 us  [balanced_sum(): pl.pallas_call(functools.partial(balanced_sum_kernel, rep_count, tile_cou...]
where the time goes in v8:
time: 119 us; the launch traced here: 118 us
  Pallas kernels  83.9 us (71%)
  matrix products  16.8 us (14%)
  local copies, waits for them, and re-layouts  10.3 us (9%)
  other arithmetic  6.15 us (5%)
    pallas_call x1, Pallas kernels, balanced_sum(): pl.pallas_call(functools.partial(balanced_sum_kernel, rep_count, tile_cou...  56.5 us
    pallas_call x1, Pallas kernels, exchange(): pl.pallas_call(functools.partial(exchange_kernel, tile_count, col_tiles),...  27.5 us
    sub x1, matrix products, window_grads(): exponent = jnp.exp(scores - peak_score)  5.13 us
    dot_general x1, matrix products, window_grads(): lax.dot_general(normed, proj_grad, (((0,), (0,)), ((), ())), preferred_el...  2.76 us
    dot_general x1, matrix products, window_grads(): jnp.einsum('wnqk,wnqc->wkc', probs_low, grad_spread, preferred_element_ty...  2.63 us

profile of v8, /device:TPU:63, one launch (start us, length us, event | category | flops | bytes accessed | tf_op | source)
XLA Modules:
  0.0 118.1 jit_solution(6861682647434661242)
XLA Ops:
  0.6 0.0 copy-start
  0.7 0.6 fusion.44
  1.3 27.5 %shard_map.50 = (bf16[64,4,512]{2,1,0:T(4,128)(2,1)}, bf16[64,4,512]{2,1,0:T(4,128)(2,1)}) custom-call(bf16[1,64,4,512]{3,2,1,0:T(4,128)(2,1)} %tokens_ref.1, bf16[1,64,4,512]{3,2,1,0:T(4,128)(2,1)} %cot_ref.1), custom_call_target="tpu_custom_call" | custom-call | tf_op jit(solution)/shard_map/pallas_call | solution.py:705
  28.8 1.2 %reshape.239 = f32[1,8,2,4,1,2,2,512]{7,6,5,3,2,1,4,0:T(2,128)S(1)} reshape(bf16[64,4,512]{2,1,0:T(4,128)(2,1)} %get-tuple-element.6) | data formatting | bytes 786432 | tf_op jit(solution)/shard_map/convert_element_type | solution.py:26
  30.0 0.4 fusion.48
  30.4 0.7 div.46
  31.2 0.5 multiply_reduce_fusion.3
  31.7 0.7 rsqrt.13
  32.4 0.0 copy-done.6
  32.4 0.1 reshape_reshape.7
  32.6 0.2 copy.30
  32.8 0.8 mul.106
  33.6 0.3 copy.29
  33.9 0.4 reshape.237
  34.2 0.0 copy-done
  34.2 1.3 %fusion.51 = (bf16[256,1536]{1,0:T(8,128)(2,1)S(1)}, f32[256,1536]{1,0:T(8,128)S(1)}) fusion(bf16[512,1536]{1,0:T(8,128)(2,1)S(1)} %copy-done, f32[256,512]{1,0:T(8,128)S(1)} %reshape.237, f32[256]{0:T(256)} %rsqrt.13, f32[256]{0:T(256)} %div.46), kind=kOutput, calls=%fused_computation.65 | convolution fusion | flops 403439616 | bytes 4458496 | tf_op jit(solution)/shard_map/dot_general | solution.py:28
  35.6 0.9 fusion.50
  36.5 0.0 copy-start.5
  36.5 5.1 %fusion.52 = (f32[4,16,64]{2,1,0:T(8,128)}, f32[4,16,64,64]{2,3,1,0:T(8,128)}) fusion(bf16[4,64,512,1]{2,1,3,0:T(8,128)(2,1)} %bitcast.69, bf16[16,512]{1,0:T(8,128)(2,1)S(1)} %get-tuple-element.16, bf16[4,64,512]{2,1,0:T(8,128)(2,1)S(1)} %bitcast.66), kind=kOutput, calls=%fused_computation.66 | convolution fusion | flops 271056960 | bytes 1605632 | tf_op jit(solution)/shard_map/sub | solution.py:46
  41.6 0.0 copy-done.5
  41.6 2.6 %fusion.23 = bf16[4,64,512]{2,1,0:T(8,128)(2,1)S(1)} fusion(bf16[4,64,512]{2,1,0:T(8,128)(2,1)S(1)} %copy-done.5, bf16[16,512]{1,0:T(8,128)(2,1)S(1)} %get-tuple-element.16, f32[4,16,64,64]{2,3,1,0:T(8,128)} %get-tuple-element.20, f32[4,16,64]{2,1,0:T(8,128)} %get-tuple-element.19), kind=kOutput, calls=%fused_computation.24 | convolution fusion | flops 271187968 | bytes 1605632 | tf_op jit(solution)/shard_map/wnqk,wnqc->wkc/dot_general | solution.py:50
  44.3 0.0 copy-start.13
  44.3 2.1 %multiply_reduce_fusion.1 = (f32[4,16,64]{2,1,0:T(8,128)S(1)}, f32[4,16,64,64]{2,3,1,0:T(8,128)S(1)}) fusion(f32[4,16,64,64]{2,3,1,0:T(8,128)S(1)} %copy-done.1, f32[4,16,64]{2,1,0:T(8,128)S(1)} %copy-done.10, bf16[4,64,512,1]{2,1,3,0:T(8,128)(2,1)S(1)} %bitcast.71, bf16[4,64,512]{2,1,0:T(8,128)(2,1)S(1)} %copy-done.5, ...), kind=kOutput, calls=%fused_computation.12 | convolution fusion | flops 271314944 | bytes 2670592 | tf_op jit(solution)/shard_map/wnqc,wkc->wnqk/dot_general | solution.py:49
  46.4 0.7 multiply_convert_fusion
  47.1 0.0 copy-start.9
  47.1 0.9 fusion.26
  48.0 0.0 copy-done.7
  48.1 1.3 %multiply_reduce_fusion = f32[4,64,512]{2,1,0:T(8,128)S(1)} fusion(f32[16,512]{1,0:T(8,128)S(1)} %copy-done.9, bf16[4,16,64,64]{2,3,1,0:T(8,128)(2,1)S(1)} %multiply_convert_fusion, bf16[4,64,512,1]{2,1,3,0:T(8,128)(2,1)S(1)} %bitcast.70), kind=kOutput, calls=%fused_computation.1 | convolution fusion | flops 272498688 | bytes 1343488 | tf_op jit(solution)/shard_map/wnqk,wkc->wnqc/dot_general | solution.py:59
  49.4 0.0 copy-start.3
  49.4 0.0 copy-start.11
  49.4 0.0 copy-start.12
  49.4 0.0 copy-done.13
  49.4 0.0 copy-done.14
  49.5 0.6 fusion.33
  50.1 0.0 copy-done.3
  50.1 0.0 copy-done.12
  50.1 0.8 fusion.49
  51.0 0.3 reshape.235
  51.3 0.8 div.55
  52.1 0.8 div.53
  52.9 1.5 %fusion.35 = bf16[1,8,2,4,1,2,2,512]{7,5,3,1,6,2,0,4:T(2,128)(2,1)S(1)} fusion(f32[2,2,8,4,2]{4,3,2,1,0:T(4,128)} %div.55, f32[2,2,8,4,2]{4,3,2,1,0:T(4,128)S(1)} %broadcast_multiply_fusion, f32[2,1,2,8,1,4,2,512]{7,6,5,3,2,0,4,1:T(2,128)S(1)} %reshape.235, f32[2,2,8,4,2]{4,3,2,1,0:T(4,128)} %div.53, f32[2,2,8,4,2]{4,3,2,1,0:T(4,128)S(1)} %add_rsqrt_fusion, ...), kind=kLoop, calls=%fused_computation.42 | loop fusion | flops 1179648 | bytes 1576960 | tf_op jit(solution)/shard_map/transpose | solution.py:778
  54.5 0.3 copy.13
  54.7 0.8 reshape_reshape.8.spread_ref
  55.6 0.1 copy.10
  55.7 2.8 %convolution_convert_fusion.blocks_ref = bf16[64,8,1536]{2,1,0:T(8,128)(2,1)} fusion(bf16[256,512]{1,0:T(8,128)(2,1)} %bitcast.73, bf16[256,512]{1,0:T(8,128)(2,1)} %bitcast.75, bf16[256,512]{1,0:T(8,128)(2,1)S(1)} %bitcast.65, bf16[512,256]{1,0:T(8,128)(2,1)S(1)} %copy.10), kind=kOutput, calls=%fused_computation.10 | convolution fusion | flops 405798912 | bytes 2621440 | tf_op jit(solution)/shard_map/dot_general | solution.py:77
  58.5 56.5 %shard_map.51 = (f32[8,1536]{1,0:T(8,128)}, bf16[64,4,512]{2,1,0:T(4,128)(2,1)}) custom-call(bf16[64,8,1536]{2,1,0:T(8,128)(2,1)} %convolution_convert_fusion.blocks_ref, bf16[64,4,512]{2,1,0:T(4,128)(2,1)} %reshape_reshape.8.spread_ref), custom_call_target="tpu_custom_call" | custom-call | tf_op jit(solution)/shard_map/pallas_call | solution.py:616
  115.0 1.4 %broadcast_multiply_fusion.1 = f32[8,1536]{1,0:T(8,128)} fusion(f32[8,1536]{1,0:T(8,128)} %get-tuple-element.9), kind=kLoop, calls=%fused_computation.47 | loop fusion | flops 12288 | bytes 98304 | tf_op jit(solution)/shard_map/div | solution.py:789
  116.4 1.7 %copy.32 = bf16[1,64,4,512]{3,2,1,0:T(4,128)(2,1)} copy(bf16[1,64,4,512]{3,2,1,0:T(4,128)(2,1)} %bitcast.68) | data formatting | bytes 524288
  (23 shorter events, 0.2 us)
Async XLA Ops:
  0.6 33.6 %copy-start = (bf16[512,1536]{1,0:T(8,128)(2,1)S(1)}, bf16[512,1536]{1,0:T(8,128)(2,1)}, u32[]{:S(2)}) copy-start(bf16[512,1536]{1,0:T(8,128)(2,1)} %param.4) | copy-start | bytes 4718596
  28.8 3.7 %copy-start.6 = (bf16[64,4,512]{2,1,0:T(4,128)(2,1)S(1)}, bf16[64,4,512]{2,1,0:T(4,128)(2,1)}, u32[]{:S(2)}) copy-start(bf16[64,4,512]{2,1,0:T(4,128)(2,1)} %get-tuple-element.7) | copy-start | bytes 786436
  36.5 5.1 %copy-start.5 = (bf16[4,64,512]{2,1,0:T(8,128)(2,1)S(1)}, bf16[4,64,512]{2,1,0:T(8,128)(2,1)}, u32[]{:S(2)}) copy-start(bf16[4,64,512]{2,1,0:T(8,128)(2,1)} %mul.106) | copy-start | bytes 786436
  41.6 2.7 %copy-start.1 = (f32[4,16,64,64]{2,3,1,0:T(8,128)S(1)}, f32[4,16,64,64]{2,3,1,0:T(8,128)}, u32[]{:S(2)}) copy-start(f32[4,16,64,64]{2,3,1,0:T(8,128)} %get-tuple-element.20) | copy-start | bytes 3145732
  41.6 2.7 %copy-start.8 = (bf16[256,512]{1,0:T(8,128)(2,1)S(1)}, bf16[256,512]{1,0:T(8,128)(2,1)}, u32[]{:S(2)}) copy-start(bf16[256,512]{1,0:T(8,128)(2,1)} %get-tuple-element.12) | copy-start | bytes 786436
  41.6 2.7 %copy-start.10 = (f32[4,16,64]{2,1,0:T(8,128)S(1)}, f32[4,16,64]{2,1,0:T(8,128)}, u32[]{:S(2)}) copy-start(f32[4,16,64]{2,1,0:T(8,128)} %get-tuple-element.19) | copy-start | bytes 49156
  44.3 5.2 %copy-start.13 = (bf16[4,64,512]{2,1,0:T(8,128)(2,1)}, bf16[4,64,512]{2,1,0:T(8,128)(2,1)S(1)}, u32[]{:S(2)}) copy-start(bf16[4,64,512]{2,1,0:T(8,128)(2,1)S(1)} %fusion.23) | copy-start | bytes 786436
  47.1 1.0 copy-start.7
  47.1 0.9 copy-start.9
  48.1 1.4 %copy-start.14 = (bf16[4,64,512]{2,1,0:T(8,128)(2,1)}, bf16[4,64,512]{2,1,0:T(8,128)(2,1)S(1)}, u32[]{:S(2)}) copy-start(bf16[4,64,512]{2,1,0:T(8,128)(2,1)S(1)} %fusion.26) | copy-start | bytes 786436
  49.4 0.7 copy-start.3
  49.4 0.7 copy-start.11
  49.4 0.7 copy-start.12
  51.3 4.3 %copy-start.2 = (bf16[512,256]{0,1:T(8,128)(2,1)S(1)}, bf16[512,256]{0,1:T(8,128)(2,1)}, u32[]{:S(2)}) copy-start(bf16[512,256]{0,1:T(8,128)(2,1)} %get-tuple-element.14) | copy-start | bytes 786436
  51.3 4.4 %copy-start.4 = (bf16[4,64,512]{2,1,0:T(8,128)(2,1)S(1)}, bf16[4,64,512]{2,1,0:T(8,128)(2,1)}, u32[]{:S(2)}) copy-start(bf16[4,64,512]{2,1,0:T(8,128)(2,1)} %copy-done.3) | copy-start | bytes 786436

commit v9 on v7

--- a/solution.py
+++ b/solution.py
@@ -440,8 +440,8 @@
     )(row_blocks, spread)
 
 
-def exchange_kernel(tile_count, col_tiles, tokens_ref, cot_ref, tokens_out, cot_out,
-                    tokens_held, cot_held, send_sems, recv_sems, own_sems):
+def exchange_kernel(tile_count, col_tiles, rows_ref, rows_out, held, send_sems, recv_sems,
+                    own_sems):
     me = lax.axis_index("rep")
     row = lax.axis_index("ty")
     col = lax.axis_index("tx")
@@ -459,62 +459,52 @@
 
     pl.semaphore_wait(barrier, tile_count - 1)
 
-    def tile_copies(step):
+    def tile_copy(step):
         peer = lax.rem(tile + step, tile_count)
-        return [
-            pltpu.make_async_remote_copy(
-                src_ref=source.at[0, peer],
-                dst_ref=held.at[tile],
-                send_sem=send_sems.at[step, index],
-                recv_sem=recv_sems.at[step, index],
-                device_id=tile_peer(step),
-                device_id_type=pl.DeviceIdType.MESH,
-            )
-            for index, (source, held) in enumerate(((tokens_ref, tokens_held), (cot_ref, cot_held)))
-        ]
-
-    own = [
-        pltpu.make_async_copy(tokens_ref.at[0, tile], tokens_held.at[tile], own_sems.at[0]),
-        pltpu.make_async_copy(cot_ref.at[0, tile], cot_held.at[tile], own_sems.at[1]),
-    ]
-    for copy in own:
-        copy.start()
-
-    @pl.loop(1, tile_count)
-    def _(step):
-        for copy in tile_copies(step):
-            copy.start()
-
-    for copy in own:
-        copy.wait()
-
-    @pl.loop(1, tile_count)
-    def _(step):
-        for copy in tile_copies(step):
-            copy.wait()
-
-    tokens_out[...] = tokens_held[...]
-    cot_out[...] = cot_held[...]
+        return pltpu.make_async_remote_copy(
+            src_ref=rows_ref.at[peer],
+            dst_ref=held.at[tile],
+            send_sem=send_sems.at[step],
+            recv_sem=recv_sems.at[step],
+            device_id=tile_peer(step),
+            device_id_type=pl.DeviceIdType.MESH,
+        )
+
+    own = pltpu.make_async_copy(rows_ref.at[tile], held.at[tile], own_sems.at[0])
+    own.start()
+
+    @pl.loop(1, tile_count)
+    def _(step):
+        tile_copy(step).start()
+
+    own.wait()
+
+    @pl.loop(1, tile_count)
+    def _(step):
+        tile_copy(step).wait()
+
+    rows_out[...] = held[...]
 
 
 def exchange(tokens, cotangent):
     col_tiles = lax.axis_size("tx")
     tile_count = lax.axis_size("ty") * col_tiles
-    held_shape = (tile_count,) + tokens.shape[2:]
-    return pl.pallas_call(
+    row_shape = (tile_count,) + tokens.shape[2:]
+    rows = jnp.stack([tokens.reshape(row_shape), cotangent.reshape(row_shape)], axis=1)
+    held = pl.pallas_call(
         functools.partial(exchange_kernel, tile_count, col_tiles),
-        out_shape=[jax.ShapeDtypeStruct(held_shape, tokens.dtype)] * 2,
-        in_specs=[pl.BlockSpec(memory_space=pltpu.VMEM)] * 2,
-        out_specs=[pl.BlockSpec(memory_space=pltpu.VMEM)] * 2,
+        out_shape=jax.ShapeDtypeStruct(rows.shape, rows.dtype),
+        in_specs=[pl.BlockSpec(memory_space=pltpu.VMEM)],
+        out_specs=pl.BlockSpec(memory_space=pltpu.VMEM),
         scratch_shapes=[
-            pltpu.VMEM(held_shape, tokens.dtype),
-            pltpu.VMEM(held_shape, tokens.dtype),
-            pltpu.SemaphoreType.DMA((tile_count, 2)),
-            pltpu.SemaphoreType.DMA((tile_count, 2)),
-            pltpu.SemaphoreType.DMA((2,)),
+            pltpu.VMEM(rows.shape, rows.dtype),
+            pltpu.SemaphoreType.DMA((tile_count,)),
+            pltpu.SemaphoreType.DMA((tile_count,)),
+            pltpu.SemaphoreType.DMA((1,)),
         ],
         compiler_params=pltpu.CompilerParams(collective_id=1, has_side_effects=True),
-    )(tokens, cotangent)
+    )(rows)
+    return held[:, 0], held[:, 1]
 
 
 def shards(tokens, qkv_weight, cotangent):

time: 114 us -> 115 us (level)
  other arithmetic: 6.15 us -> 9.5 us
  Pallas kernels: 79.2 us -> 77.7 us
    another operation x0 -> x1, other arithmetic: none -> 2.16 us  [exchange(): jnp.stack([tokens.reshape(row_shape), cotangent.reshape(row_shape)], axis=1)]
    pallas_call x1, Pallas kernels: 27.5 us -> 26 us  [exchange(): pl.pallas_call(functools.partial(exchange_kernel, tile_count, col_tiles),...]
    convert_element_type x0 -> x1, other arithmetic: none -> 1.19 us  [window_grads(): standard, inv_std = normalize(window_x.astype(jnp.float32))]
where the time goes in v9:
time: 115 us; the launch traced here: 114 us
  Pallas kernels  77.7 us (68%)
  matrix products  16.7 us (15%)
  other arithmetic  9.5 us (8%)
  local copies, waits for them, and re-layouts  9.45 us (8%)
    pallas_call x1, Pallas kernels, paired_sum(): pl.pallas_call(functools.partial(paired_sum_kernel, rep_count, tile_count...  51.7 us
    pallas_call x1, Pallas kernels, exchange(): pl.pallas_call(functools.partial(exchange_kernel, tile_count, col_tiles),...  26 us
    sub x1, matrix products, window_grads(): exponent = jnp.exp(scores - peak_score)  5.13 us
    dot_general x1, matrix products, window_grads(): lax.dot_general(normed, proj_grad, (((0,), (0,)), ((), ())), preferred_el...  2.76 us
    dot_general x1, matrix products, window_grads(): jnp.einsum('wnqk,wnqc->wkc', probs_low, grad_spread, preferred_element_ty...  2.63 us

profile of v9, /device:TPU:63, one launch (start us, length us, event | category | flops | bytes accessed | tf_op | source)
XLA Modules:
  0.0 114.4 jit_solution(6727482340749372271)
XLA Ops:
  0.6 0.0 copy-start
  0.7 0.6 fusion.44
  1.3 2.2 %pad_maximum_fusion.1.rows_ref = bf16[64,2,4,512]{3,2,1,0:T(4,128)(2,1)} fusion(bf16[64,1,4,512]{3,2,1,0:T(4,128)(2,1)} %bitcast.71, bf16[64,1,4,512]{3,2,1,0:T(4,128)(2,1)} %bitcast.72), kind=kLoop, calls=%fused_computation.32 | loop fusion | flops 262144 | bytes 1048576 | tf_op jit(solution)/shard_map/stack | solution.py:493
  3.5 26.0 %shard_map.50 = bf16[64,2,4,512]{3,2,1,0:T(4,128)(2,1)} custom-call(bf16[64,2,4,512]{3,2,1,0:T(4,128)(2,1)} %pad_maximum_fusion.1.rows_ref), custom_call_target="tpu_custom_call" | custom-call | tf_op jit(solution)/shard_map/pallas_call | solution.py:494
  29.5 1.2 %slice_convert_fusion = (f32[64,1,4,512]{3,2,1,0:T(4,128)S(1)}, bf16[64,1,4,512]{3,2,1,0:T(4,128)(2,1)S(1)}) fusion(bf16[64,2,4,512]{3,2,1,0:T(4,128)(2,1)} %shard_map.50), kind=kLoop, calls=%fused_computation.43 | loop fusion | flops 131072 | bytes 1310720 | tf_op jit(solution)/shard_map/convert_element_type | solution.py:26
  30.7 0.4 reshape.239
  31.1 0.4 fusion.48
  31.5 0.7 div.46
  32.2 0.5 multiply_reduce_fusion.3
  32.8 0.7 rsqrt.13
  33.5 0.1 reshape_reshape_squeeze.4
  33.6 0.2 copy.30
  33.9 0.8 mul.106
  34.7 0.3 copy.29
  34.9 0.4 reshape.237
  35.3 0.0 copy-done
  35.3 1.3 %fusion.51 = (bf16[256,1536]{1,0:T(8,128)(2,1)S(1)}, f32[256,1536]{1,0:T(8,128)S(1)}) fusion(bf16[512,1536]{1,0:T(8,128)(2,1)S(1)} %copy-done, f32[256,512]{1,0:T(8,128)S(1)} %reshape.237, f32[256]{0:T(256)} %rsqrt.13, f32[256]{0:T(256)} %div.46), kind=kOutput, calls=%fused_computation.67 | convolution fusion | flops 403439616 | bytes 4458496 | tf_op jit(solution)/shard_map/dot_general | solution.py:28
  36.6 0.8 fusion.50
  37.5 0.0 copy-start.5
  37.5 5.1 %fusion.52 = (f32[4,16,64]{2,1,0:T(8,128)}, f32[4,16,64,64]{2,3,1,0:T(8,128)}) fusion(bf16[4,64,512,1]{2,1,3,0:T(8,128)(2,1)} %bitcast.73, bf16[16,512]{1,0:T(8,128)(2,1)S(1)} %get-tuple-element.14, bf16[4,64,512]{2,1,0:T(8,128)(2,1)S(1)} %bitcast.68), kind=kOutput, calls=%fused_computation.68 | convolution fusion | flops 271056960 | bytes 1605632 | tf_op jit(solution)/shard_map/sub | solution.py:46
  42.7 2.6 %fusion.23 = bf16[4,64,512]{2,1,0:T(8,128)(2,1)S(1)} fusion(bf16[4,64,512]{2,1,0:T(8,128)(2,1)S(1)} %copy-done.5, bf16[16,512]{1,0:T(8,128)(2,1)S(1)} %get-tuple-element.14, f32[4,16,64,64]{2,3,1,0:T(8,128)} %get-tuple-element.18, f32[4,16,64]{2,1,0:T(8,128)} %get-tuple-element.17), kind=kOutput, calls=%fused_computation.24 | convolution fusion | flops 271187968 | bytes 1605632 | tf_op jit(solution)/shard_map/wnqk,wnqc->wkc/dot_general | solution.py:50
  45.3 0.0 copy-start.12
  45.3 0.0 copy-done.1
  45.3 0.0 copy-done.7
  45.3 0.0 copy-done.9
  45.3 2.1 %multiply_reduce_fusion.1 = (f32[4,16,64]{2,1,0:T(8,128)S(1)}, f32[4,16,64,64]{2,3,1,0:T(8,128)S(1)}) fusion(f32[4,16,64,64]{2,3,1,0:T(8,128)S(1)} %copy-done.1, f32[4,16,64]{2,1,0:T(8,128)S(1)} %copy-done.9, bf16[4,64,512,1]{2,1,3,0:T(8,128)(2,1)S(1)} %bitcast.75, bf16[4,64,512]{2,1,0:T(8,128)(2,1)S(1)} %copy-done.5, bf16[16,512]{1,0:T(8,128)(2,1)S(1)} %get-tuple-element.14), kind=kOutput, calls=%fused_computation.12 | convolution fusion | flops 271314944 | bytes 2670592 | tf_op jit(solution)/shard_map/wnqc,wkc->wnqk/dot_general | solution.py:49
  47.5 0.7 multiply_convert_fusion
  48.2 0.0 copy-start.6
  48.2 0.0 copy-start.8
  48.2 0.9 fusion.26
  49.1 0.0 copy-done.6
  49.1 0.0 copy-done.8
  49.1 1.3 %multiply_reduce_fusion = f32[4,64,512]{2,1,0:T(8,128)S(1)} fusion(f32[16,512]{1,0:T(8,128)S(1)} %copy-done.8, bf16[4,16,64,64]{2,3,1,0:T(8,128)(2,1)S(1)} %multiply_convert_fusion, bf16[4,64,512,1]{2,1,3,0:T(8,128)(2,1)S(1)} %bitcast.74), kind=kOutput, calls=%fused_computation.1 | convolution fusion | flops 272498688 | bytes 1343488 | tf_op jit(solution)/shard_map/wnqk,wkc->wnqc/dot_general | solution.py:59
  50.5 0.6 fusion.33
  51.1 0.0 copy-done.3
  51.1 0.0 copy-done.11
  51.2 0.8 fusion.49
  52.0 0.3 reshape.235
  52.4 0.8 div.55
  53.2 0.8 div.53
  54.0 1.5 %fusion.35 = bf16[1,8,2,4,1,2,2,512]{7,5,3,1,6,2,0,4:T(2,128)(2,1)S(1)} fusion(f32[2,2,8,4,2]{4,3,2,1,0:T(4,128)} %div.55, f32[2,2,8,4,2]{4,3,2,1,0:T(4,128)S(1)} %broadcast_multiply_fusion, f32[2,1,2,8,1,4,2,512]{7,6,5,3,2,0,4,1:T(2,128)S(1)} %reshape.235, f32[2,2,8,4,2]{4,3,2,1,0:T(4,128)} %div.53, f32[2,2,8,4,2]{4,3,2,1,0:T(4,128)S(1)} %add_rsqrt_fusion, ...), kind=kLoop, calls=%fused_computation.44 | loop fusion | flops 1179648 | bytes 1576960 | tf_op jit(solution)/shard_map/transpose | solution.py:567
  55.5 0.3 copy.13
  55.8 0.8 reshape_reshape.3.spread_ref
  56.6 0.1 copy.10
  56.7 2.8 %convolution_convert_fusion.blocks_ref = bf16[64,8,1536]{2,1,0:T(8,128)(2,1)} fusion(bf16[256,512]{1,0:T(8,128)(2,1)} %bitcast.77, bf16[256,512]{1,0:T(8,128)(2,1)} %bitcast.79, bf16[256,512]{1,0:T(8,128)(2,1)S(1)} %bitcast.67, bf16[512,256]{1,0:T(8,128)(2,1)S(1)} %copy.10), kind=kOutput, calls=%fused_computation.10 | convolution fusion | flops 405798912 | bytes 2621440 | tf_op jit(solution)/shard_map/dot_general | solution.py:77
  59.5 51.7 %shard_map.51 = (f32[8,1536]{1,0:T(8,128)}, bf16[64,4,512]{2,1,0:T(4,128)(2,1)}) custom-call(bf16[64,8,1536]{2,1,0:T(8,128)(2,1)} %convolution_convert_fusion.blocks_ref, bf16[64,4,512]{2,1,0:T(4,128)(2,1)} %reshape_reshape.3.spread_ref), custom_call_target="tpu_custom_call" | custom-call | tf_op jit(solution)/shard_map/pallas_call | solution.py:413
  111.2 1.4 %broadcast_multiply_fusion.1 = f32[8,1536]{1,0:T(8,128)} fusion(f32[8,1536]{1,0:T(8,128)} %get-tuple-element.5), kind=kLoop, calls=%fused_computation.49 | loop fusion | flops 12288 | bytes 98304 | tf_op jit(solution)/shard_map/div | solution.py:578
  112.6 1.7 %copy.32 = bf16[1,64,4,512]{3,2,1,0:T(4,128)(2,1)} copy(bf16[1,64,4,512]{3,2,1,0:T(4,128)(2,1)} %bitcast.70) | data formatting | bytes 524288
  (23 shorter events, 0.2 us)
Async XLA Ops:
  0.6 34.7 %copy-start = (bf16[512,1536]{1,0:T(8,128)(2,1)S(1)}, bf16[512,1536]{1,0:T(8,128)(2,1)}, u32[]{:S(2)}) copy-start(bf16[512,1536]{1,0:T(8,128)(2,1)} %param.4) | copy-start | bytes 4718596
  37.5 5.1 %copy-start.5 = (bf16[4,64,512]{2,1,0:T(8,128)(2,1)S(1)}, bf16[4,64,512]{2,1,0:T(8,128)(2,1)}, u32[]{:S(2)}) copy-start(bf16[4,64,512]{2,1,0:T(8,128)(2,1)} %mul.106) | copy-start | bytes 786436
  42.7 2.7 %copy-start.1 = (f32[4,16,64,64]{2,3,1,0:T(8,128)S(1)}, f32[4,16,64,64]{2,3,1,0:T(8,128)}, u32[]{:S(2)}) copy-start(f32[4,16,64,64]{2,3,1,0:T(8,128)} %get-tuple-element.18) | copy-start | bytes 3145732
  42.7 2.7 %copy-start.7 = (bf16[256,512]{1,0:T(8,128)(2,1)S(1)}, bf16[256,512]{1,0:T(8,128)(2,1)}, u32[]{:S(2)}) copy-start(bf16[256,512]{1,0:T(8,128)(2,1)} %get-tuple-element.8) | copy-start | bytes 786436
  42.7 2.7 %copy-start.9 = (f32[4,16,64]{2,1,0:T(8,128)S(1)}, f32[4,16,64]{2,1,0:T(8,128)}, u32[]{:S(2)}) copy-start(f32[4,16,64]{2,1,0:T(8,128)} %get-tuple-element.17) | copy-start | bytes 49156
  45.3 5.2 %copy-start.12 = (bf16[4,64,512]{2,1,0:T(8,128)(2,1)}, bf16[4,64,512]{2,1,0:T(8,128)(2,1)S(1)}, u32[]{:S(2)}) copy-start(bf16[4,64,512]{2,1,0:T(8,128)(2,1)S(1)} %fusion.23) | copy-start | bytes 786436
  48.2 1.0 copy-start.6
  48.2 0.9 copy-start.8
  49.1 1.4 %copy-start.13 = (bf16[4,64,512]{2,1,0:T(8,128)(2,1)}, bf16[4,64,512]{2,1,0:T(8,128)(2,1)S(1)}, u32[]{:S(2)}) copy-start(bf16[4,64,512]{2,1,0:T(8,128)(2,1)S(1)} %fusion.26) | copy-start | bytes 786436
  50.5 0.7 copy-start.3
  50.5 0.7 copy-start.10
  50.5 0.7 copy-start.11
  52.3 4.3 %copy-start.2 = (bf16[512,256]{0,1:T(8,128)(2,1)S(1)}, bf16[512,256]{0,1:T(8,128)(2,1)}, u32[]{:S(2)}) copy-start(bf16[512,256]{0,1:T(8,128)(2,1)} %get-tuple-element.10) | copy-start | bytes 786436
  52.3 4.4 %copy-start.4 = (bf16[4,64,512]{2,1,0:T(8,128)(2,1)S(1)}, bf16[4,64,512]{2,1,0:T(8,128)(2,1)}, u32[]{:S(2)}) copy-start(bf16[4,64,512]{2,1,0:T(8,128)(2,1)} %copy-done.3) | copy-start | bytes 786436

commit v10 on v7

--- a/solution.py
+++ b/solution.py
@@ -288,11 +288,6 @@
         )
 
     back_own = pltpu.make_async_copy(spread_ref.at[tile], returned_held.at[tile], own_sems.at[0])
-    back_own.start()
-
-    @pl.loop(1, tile_count)
-    def _(step):
-        back_copy(step).start()
 
     pair_copy.wait()
 
@@ -320,6 +315,12 @@
         @pl.when(mine_start + index != tile)
         def _():
             sum_copy(index).start()
+
+    back_own.start()
+
+    @pl.loop(1, tile_count)
+    def _(step):
+        back_copy(step).start()
 
     def final_copy():
         return pltpu.make_async_remote_copy(

time: 114 us -> 114 us (level)
  no operation moved by 1% of the time
where the time goes in v10:
time: 114 us
  Pallas kernels  79.5 us (70%)
  matrix products  16.8 us (15%)
  local copies, waits for them, and re-layouts  10.3 us (9%)
  other arithmetic  6.15 us (5%)
    pallas_call x1, Pallas kernels, paired_sum(): pl.pallas_call(functools.partial(paired_sum_kernel, rep_count, tile_count...  52.1 us
    pallas_call x1, Pallas kernels, exchange(): pl.pallas_call(functools.partial(exchange_kernel, tile_count, col_tiles),...  27.5 us
    sub x1, matrix products, window_grads(): exponent = jnp.exp(scores - peak_score)  5.13 us
    dot_general x1, matrix products, window_grads(): lax.dot_general(normed, proj_grad, (((0,), (0,)), ((), ())), preferred_el...  2.76 us
    dot_general x1, matrix products, window_grads(): jnp.einsum('wnqk,wnqc->wkc', probs_low, grad_spread, preferred_element_ty...  2.63 us

profile of v10, /device:TPU:63, one launch (start us, length us, event | category | flops | bytes accessed | tf_op | source)
XLA Modules:
  0.0 113.7 jit_solution(17250314470301177164)
XLA Ops:
  0.6 0.0 copy-start
  0.7 0.6 fusion.44
  1.3 27.5 %shard_map.50 = (bf16[64,4,512]{2,1,0:T(4,128)(2,1)}, bf16[64,4,512]{2,1,0:T(4,128)(2,1)}) custom-call(bf16[1,64,4,512]{3,2,1,0:T(4,128)(2,1)} %tokens_ref.1, bf16[1,64,4,512]{3,2,1,0:T(4,128)(2,1)} %cot_ref.1), custom_call_target="tpu_custom_call" | custom-call | tf_op jit(solution)/shard_map/pallas_call | solution.py:505
  28.8 1.2 %reshape.239 = f32[1,8,2,4,1,2,2,512]{7,6,5,3,2,1,4,0:T(2,128)S(1)} reshape(bf16[64,4,512]{2,1,0:T(4,128)(2,1)} %get-tuple-element.6) | data formatting | bytes 786432 | tf_op jit(solution)/shard_map/convert_element_type | solution.py:26
  30.0 0.4 fusion.48
  30.4 0.7 div.46
  31.2 0.5 multiply_reduce_fusion.3
  31.7 0.7 rsqrt.13
  32.4 0.0 copy-done.6
  32.4 0.1 reshape_reshape.7
  32.6 0.2 copy.30
  32.8 0.8 mul.106
  33.6 0.3 copy.29
  33.9 0.4 reshape.237
  34.2 0.0 copy-done
  34.2 1.3 %fusion.51 = (bf16[256,1536]{1,0:T(8,128)(2,1)S(1)}, f32[256,1536]{1,0:T(8,128)S(1)}) fusion(bf16[512,1536]{1,0:T(8,128)(2,1)S(1)} %copy-done, f32[256,512]{1,0:T(8,128)S(1)} %reshape.237, f32[256]{0:T(256)} %rsqrt.13, f32[256]{0:T(256)} %div.46), kind=kOutput, calls=%fused_computation.65 | convolution fusion | flops 403439616 | bytes 4458496 | tf_op jit(solution)/shard_map/dot_general | solution.py:28
  35.6 0.9 fusion.50
  36.5 0.0 copy-start.5
  36.5 5.1 %fusion.52 = (f32[4,16,64]{2,1,0:T(8,128)}, f32[4,16,64,64]{2,3,1,0:T(8,128)}) fusion(bf16[4,64,512,1]{2,1,3,0:T(8,128)(2,1)} %bitcast.69, bf16[16,512]{1,0:T(8,128)(2,1)S(1)} %get-tuple-element.16, bf16[4,64,512]{2,1,0:T(8,128)(2,1)S(1)} %bitcast.66), kind=kOutput, calls=%fused_computation.66 | convolution fusion | flops 271056960 | bytes 1605632 | tf_op jit(solution)/shard_map/sub | solution.py:46
  41.6 0.0 copy-done.5
  41.6 2.6 %fusion.23 = bf16[4,64,512]{2,1,0:T(8,128)(2,1)S(1)} fusion(bf16[4,64,512]{2,1,0:T(8,128)(2,1)S(1)} %copy-done.5, bf16[16,512]{1,0:T(8,128)(2,1)S(1)} %get-tuple-element.16, f32[4,16,64,64]{2,3,1,0:T(8,128)} %get-tuple-element.20, f32[4,16,64]{2,1,0:T(8,128)} %get-tuple-element.19), kind=kOutput, calls=%fused_computation.24 | convolution fusion | flops 271187968 | bytes 1605632 | tf_op jit(solution)/shard_map/wnqk,wnqc->wkc/dot_general | solution.py:50
  44.3 0.0 copy-start.13
  44.3 2.1 %multiply_reduce_fusion.1 = (f32[4,16,64]{2,1,0:T(8,128)S(1)}, f32[4,16,64,64]{2,3,1,0:T(8,128)S(1)}) fusion(f32[4,16,64,64]{2,3,1,0:T(8,128)S(1)} %copy-done.1, f32[4,16,64]{2,1,0:T(8,128)S(1)} %copy-done.10, bf16[4,64,512,1]{2,1,3,0:T(8,128)(2,1)S(1)} %bitcast.71, bf16[4,64,512]{2,1,0:T(8,128)(2,1)S(1)} %copy-done.5, ...), kind=kOutput, calls=%fused_computation.12 | convolution fusion | flops 271314944 | bytes 2670592 | tf_op jit(solution)/shard_map/wnqc,wkc->wnqk/dot_general | solution.py:49
  46.4 0.7 multiply_convert_fusion
  47.1 0.0 copy-start.9
  47.1 0.9 fusion.26
  48.0 0.0 copy-done.7
  48.1 1.3 %multiply_reduce_fusion = f32[4,64,512]{2,1,0:T(8,128)S(1)} fusion(f32[16,512]{1,0:T(8,128)S(1)} %copy-done.9, bf16[4,16,64,64]{2,3,1,0:T(8,128)(2,1)S(1)} %multiply_convert_fusion, bf16[4,64,512,1]{2,1,3,0:T(8,128)(2,1)S(1)} %bitcast.70), kind=kOutput, calls=%fused_computation.1 | convolution fusion | flops 272498688 | bytes 1343488 | tf_op jit(solution)/shard_map/wnqk,wkc->wnqc/dot_general | solution.py:59
  49.4 0.0 copy-start.3
  49.4 0.0 copy-start.11
  49.4 0.0 copy-start.12
  49.4 0.0 copy-done.13
  49.4 0.0 copy-done.14
  49.5 0.6 fusion.33
  50.1 0.0 copy-done.3
  50.1 0.0 copy-done.12
  50.1 0.8 fusion.49
  51.0 0.3 reshape.235
  51.3 0.8 div.55
  52.1 0.8 div.53
  52.9 1.5 %fusion.35 = bf16[1,8,2,4,1,2,2,512]{7,5,3,1,6,2,0,4:T(2,128)(2,1)S(1)} fusion(f32[2,2,8,4,2]{4,3,2,1,0:T(4,128)} %div.55, f32[2,2,8,4,2]{4,3,2,1,0:T(4,128)S(1)} %broadcast_multiply_fusion, f32[2,1,2,8,1,4,2,512]{7,6,5,3,2,0,4,1:T(2,128)S(1)} %reshape.235, f32[2,2,8,4,2]{4,3,2,1,0:T(4,128)} %div.53, f32[2,2,8,4,2]{4,3,2,1,0:T(4,128)S(1)} %add_rsqrt_fusion, ...), kind=kLoop, calls=%fused_computation.42 | loop fusion | flops 1179648 | bytes 1576960 | tf_op jit(solution)/shard_map/transpose | solution.py:578
  54.5 0.3 copy.13
  54.7 0.8 reshape_reshape.8.spread_ref
  55.6 0.1 copy.10
  55.7 2.8 %convolution_convert_fusion.blocks_ref = bf16[64,8,1536]{2,1,0:T(8,128)(2,1)} fusion(bf16[256,512]{1,0:T(8,128)(2,1)} %bitcast.73, bf16[256,512]{1,0:T(8,128)(2,1)} %bitcast.75, bf16[256,512]{1,0:T(8,128)(2,1)S(1)} %bitcast.65, bf16[512,256]{1,0:T(8,128)(2,1)S(1)} %copy.10), kind=kOutput, calls=%fused_computation.10 | convolution fusion | flops 405798912 | bytes 2621440 | tf_op jit(solution)/shard_map/dot_general | solution.py:77
  58.5 52.1 %shard_map.51 = (f32[8,1536]{1,0:T(8,128)}, bf16[64,4,512]{2,1,0:T(4,128)(2,1)}) custom-call(bf16[64,8,1536]{2,1,0:T(8,128)(2,1)} %convolution_convert_fusion.blocks_ref, bf16[64,4,512]{2,1,0:T(4,128)(2,1)} %reshape_reshape.8.spread_ref), custom_call_target="tpu_custom_call" | custom-call | tf_op jit(solution)/shard_map/pallas_call | solution.py:414
  110.6 1.4 %broadcast_multiply_fusion.1 = f32[8,1536]{1,0:T(8,128)} fusion(f32[8,1536]{1,0:T(8,128)} %get-tuple-element.9), kind=kLoop, calls=%fused_computation.47 | loop fusion | flops 12288 | bytes 98304 | tf_op jit(solution)/shard_map/div | solution.py:589
  112.0 1.7 %copy.32 = bf16[1,64,4,512]{3,2,1,0:T(4,128)(2,1)} copy(bf16[1,64,4,512]{3,2,1,0:T(4,128)(2,1)} %bitcast.68) | data formatting | bytes 524288
  (23 shorter events, 0.2 us)
Async XLA Ops:
  0.6 33.6 %copy-start = (bf16[512,1536]{1,0:T(8,128)(2,1)S(1)}, bf16[512,1536]{1,0:T(8,128)(2,1)}, u32[]{:S(2)}) copy-start(bf16[512,1536]{1,0:T(8,128)(2,1)} %param.4) | copy-start | bytes 4718596
  28.8 3.7 %copy-start.6 = (bf16[64,4,512]{2,1,0:T(4,128)(2,1)S(1)}, bf16[64,4,512]{2,1,0:T(4,128)(2,1)}, u32[]{:S(2)}) copy-start(bf16[64,4,512]{2,1,0:T(4,128)(2,1)} %get-tuple-element.7) | copy-start | bytes 786436
  36.5 5.1 %copy-start.5 = (bf16[4,64,512]{2,1,0:T(8,128)(2,1)S(1)}, bf16[4,64,512]{2,1,0:T(8,128)(2,1)}, u32[]{:S(2)}) copy-start(bf16[4,64,512]{2,1,0:T(8,128)(2,1)} %mul.106) | copy-start | bytes 786436
  41.6 2.7 %copy-start.1 = (f32[4,16,64,64]{2,3,1,0:T(8,128)S(1)}, f32[4,16,64,64]{2,3,1,0:T(8,128)}, u32[]{:S(2)}) copy-start(f32[4,16,64,64]{2,3,1,0:T(8,128)} %get-tuple-element.20) | copy-start | bytes 3145732
  41.6 2.7 %copy-start.8 = (bf16[256,512]{1,0:T(8,128)(2,1)S(1)}, bf16[256,512]{1,0:T(8,128)(2,1)}, u32[]{:S(2)}) copy-start(bf16[256,512]{1,0:T(8,128)(2,1)} %get-tuple-element.12) | copy-start | bytes 786436
  41.6 2.7 %copy-start.10 = (f32[4,16,64]{2,1,0:T(8,128)S(1)}, f32[4,16,64]{2,1,0:T(8,128)}, u32[]{:S(2)}) copy-start(f32[4,16,64]{2,1,0:T(8,128)} %get-tuple-element.19) | copy-start | bytes 49156
  44.3 5.2 %copy-start.13 = (bf16[4,64,512]{2,1,0:T(8,128)(2,1)}, bf16[4,64,512]{2,1,0:T(8,128)(2,1)S(1)}, u32[]{:S(2)}) copy-start(bf16[4,64,512]{2,1,0:T(8,128)(2,1)S(1)} %fusion.23) | copy-start | bytes 786436
  47.1 1.0 copy-start.7
  47.1 0.9 copy-start.9
  48.1 1.4 %copy-start.14 = (bf16[4,64,512]{2,1,0:T(8,128)(2,1)}, bf16[4,64,512]{2,1,0:T(8,128)(2,1)S(1)}, u32[]{:S(2)}) copy-start(bf16[4,64,512]{2,1,0:T(8,128)(2,1)S(1)} %fusion.26) | copy-start | bytes 786436
  49.4 0.7 copy-start.3
  49.4 0.7 copy-start.11
  49.4 0.7 copy-start.12
  51.3 4.3 %copy-start.2 = (bf16[512,256]{0,1:T(8,128)(2,1)S(1)}, bf16[512,256]{0,1:T(8,128)(2,1)}, u32[]{:S(2)}) copy-start(bf16[512,256]{0,1:T(8,128)(2,1)} %get-tuple-element.14) | copy-start | bytes 786436
  51.3 4.4 %copy-start.4 = (bf16[4,64,512]{2,1,0:T(8,128)(2,1)S(1)}, bf16[4,64,512]{2,1,0:T(8,128)(2,1)}, u32[]{:S(2)}) copy-start(bf16[4,64,512]{2,1,0:T(8,128)(2,1)} %copy-done.3) | copy-start | bytes 786436

commit v11 on v8

--- a/solution.py
+++ b/solution.py
@@ -441,14 +441,17 @@
 
 
 def balanced_sum_kernel(rep_count, tile_count, col_tiles, blocks_ref, spread_ref, out_ref,
-                        returned_ref, pair_held, pair_sum, arrived, partial, held,
-                        returned_held, pair_sems, sum_send_sems, sum_recv_sems, rep_send_sems,
-                        rep_recv_sems, back_send_sems, back_recv_sems, own_sems):
+                        returned_ref, pair_held, pair_sum, arrived, partial, pair_part,
+                        pair_total, held, returned_held, pair_sems, sum_send_sems, sum_recv_sems,
+                        part_sems, rep_send_sems, rep_recv_sems, back_send_sems, back_recv_sems,
+                        own_sems):
     me = lax.axis_index("rep")
     row = lax.axis_index("ty")
     col = lax.axis_index("tx")
     tile = row * col_tiles + col
     core = lax.rem(me, 2)
+    plane = me // 2
+    planes = rep_count // 2
     partner = me + 1 - 2 * core
     target_rep = me - core + lax.rem(tile, 2)
     half = tile_count // 2
@@ -462,8 +465,8 @@
     def tile_peer(step):
         return tile_device(me, lax.rem(tile + step, tile_count))
 
-    def rep_peer(step):
-        return (lax.rem(me + step, rep_count), row, col)
+    def plane_peer(step):
+        return (2 * lax.rem(plane + step, planes) + core, row, col)
 
     @pl.loop(1, tile_count)
     def _(step):
@@ -475,13 +478,11 @@
             barrier, inc=1, device_id=tile_device(partner, peer), device_id_type=mesh_id
         )
 
-    @pl.loop(1, rep_count)
-    def _(step):
-        @pl.when(lax.rem(me + step, rep_count) != partner)
-        def _():
-            pl.semaphore_signal(barrier, inc=1, device_id=rep_peer(step), device_id_type=mesh_id)
-
-    pl.semaphore_wait(barrier, 2 * tile_count + rep_count - 3)
+    @pl.loop(1, planes)
+    def _(step):
+        pl.semaphore_signal(barrier, inc=1, device_id=plane_peer(step), device_id_type=mesh_id)
+
+    pl.semaphore_wait(barrier, 2 * tile_count + planes - 2)
 
     pair_copy = pltpu.make_async_remote_copy(
         src_ref=blocks_ref.at[pl.ds((1 - core) * half, half)],
@@ -568,25 +569,37 @@
         return total + arrived[core + 2 * index].astype(jnp.float32)
 
     partial[...] = lax.fori_loop(0, half, add_source, jnp.zeros(partial.shape, jnp.float32))
-    held[me] = partial[...]
-
-    def rep_copy(step):
+    pair_part[core] = partial[...]
+    part_copy = pltpu.make_async_remote_copy(
+        src_ref=partial,
+        dst_ref=pair_part.at[core],
+        send_sem=part_sems.at[0],
+        recv_sem=part_sems.at[1],
+        device_id=(partner, row, col),
+        device_id_type=mesh_id,
+    )
+    part_copy.start()
+    part_copy.wait()
+    pair_total[...] = pair_part[0] + pair_part[1]
+    held[plane] = pair_total[...]
+
+    def plane_copy(step):
         return pltpu.make_async_remote_copy(
-            src_ref=partial,
-            dst_ref=held.at[me],
+            src_ref=pair_total,
+            dst_ref=held.at[plane],
             send_sem=rep_send_sems.at[step],
             recv_sem=rep_recv_sems.at[step],
-            device_id=rep_peer(step),
+            device_id=plane_peer(step),
             device_id_type=mesh_id,
         )
 
-    @pl.loop(1, rep_count)
-    def _(step):
-        rep_copy(step).start()
-
-    @pl.loop(1, rep_count)
-    def _(step):
-        rep_copy(step).wait()
+    @pl.loop(1, planes)
+    def _(step):
+        plane_copy(step).start()
+
+    @pl.loop(1, planes)
+    def _(step):
+        plane_copy(step).wait()
 
     @pl.loop(0, half)
     def _(index):
@@ -602,7 +615,7 @@
 
     returned_ref[...] = returned_held[...]
     total = held[0]
-    for source in range(1, rep_count):
+    for source in range(1, planes):
         total = total + held[source]
     out_ref[...] = total
 
@@ -626,13 +639,16 @@
             pltpu.VMEM(half_shape, row_blocks.dtype),
             pltpu.VMEM(row_blocks.shape, row_blocks.dtype),
             pltpu.VMEM(block_shape, jnp.float32),
-            pltpu.VMEM((rep_count,) + block_shape, jnp.float32),
+            pltpu.VMEM((2,) + block_shape, jnp.float32),
+            pltpu.VMEM(block_shape, jnp.float32),
+            pltpu.VMEM((rep_count // 2,) + block_shape, jnp.float32),
             pltpu.VMEM(spread.shape, spread.dtype),
             pltpu.SemaphoreType.DMA((2,)),
             pltpu.SemaphoreType.DMA((tile_count // 2,)),
             pltpu.SemaphoreType.DMA((tile_count,)),
-            pltpu.SemaphoreType.DMA((rep_count,)),
-            pltpu.SemaphoreType.DMA((rep_count,)),
+            pltpu.SemaphoreType.DMA((2,)),
+            pltpu.SemaphoreType.DMA((rep_count // 2,)),
+            pltpu.SemaphoreType.DMA((rep_count // 2,)),
             pltpu.SemaphoreType.DMA((tile_count,)),
             pltpu.SemaphoreType.DMA((tile_count,)),
             pltpu.SemaphoreType.DMA((2,)),

time: 119 us -> 116 us (0.975)
  Pallas kernels: 83.9 us -> 81.2 us
    pallas_call x1, Pallas kernels: 56.5 us -> 53.7 us  [balanced_sum(): pl.pallas_call(functools.partial(balanced_sum_kernel, rep_count, tile_cou...]
where the time goes in v11:
time: 116 us; the launch traced here: 115 us
  Pallas kernels  81.2 us (70%)
  matrix products  16.8 us (14%)
  local copies, waits for them, and re-layouts  10.3 us (9%)
  other arithmetic  6.15 us (5%)
    pallas_call x1, Pallas kernels, balanced_sum(): pl.pallas_call(functools.partial(balanced_sum_kernel, rep_count, tile_cou...  53.7 us
    pallas_call x1, Pallas kernels, exchange(): pl.pallas_call(functools.partial(exchange_kernel, tile_count, col_tiles),...  27.5 us
    sub x1, matrix products, window_grads(): exponent = jnp.exp(scores - peak_score)  5.13 us
    dot_general x1, matrix products, window_grads(): lax.dot_general(normed, proj_grad, (((0,), (0,)), ((), ())), preferred_el...  2.76 us
    dot_general x1, matrix products, window_grads(): jnp.einsum('wnqk,wnqc->wkc', probs_low, grad_spread, preferred_element_ty...  2.63 us

profile of v11, /device:TPU:63, one launch (start us, length us, event | category | flops | bytes accessed | tf_op | source)
XLA Modules:
  0.0 115.4 jit_solution(14828002977582358482)
XLA Ops:
  0.6 0.0 copy-start
  0.7 0.6 fusion.44
  1.3 27.5 %shard_map.50 = (bf16[64,4,512]{2,1,0:T(4,128)(2,1)}, bf16[64,4,512]{2,1,0:T(4,128)(2,1)}) custom-call(bf16[1,64,4,512]{3,2,1,0:T(4,128)(2,1)} %tokens_ref.1, bf16[1,64,4,512]{3,2,1,0:T(4,128)(2,1)} %cot_ref.1), custom_call_target="tpu_custom_call" | custom-call | tf_op jit(solution)/shard_map/pallas_call | solution.py:721
  28.8 1.2 %reshape.239 = f32[1,8,2,4,1,2,2,512]{7,6,5,3,2,1,4,0:T(2,128)S(1)} reshape(bf16[64,4,512]{2,1,0:T(4,128)(2,1)} %get-tuple-element.6) | data formatting | bytes 786432 | tf_op jit(solution)/shard_map/convert_element_type | solution.py:26
  30.0 0.4 fusion.48
  30.4 0.7 div.46
  31.2 0.5 multiply_reduce_fusion.3
  31.7 0.7 rsqrt.13
  32.4 0.0 copy-done.6
  32.4 0.1 reshape_reshape.7
  32.6 0.2 copy.30
  32.8 0.8 mul.106
  33.6 0.3 copy.29
  33.9 0.4 reshape.237
  34.2 0.0 copy-done
  34.2 1.3 %fusion.51 = (bf16[256,1536]{1,0:T(8,128)(2,1)S(1)}, f32[256,1536]{1,0:T(8,128)S(1)}) fusion(bf16[512,1536]{1,0:T(8,128)(2,1)S(1)} %copy-done, f32[256,512]{1,0:T(8,128)S(1)} %reshape.237, f32[256]{0:T(256)} %rsqrt.13, f32[256]{0:T(256)} %div.46), kind=kOutput, calls=%fused_computation.65 | convolution fusion | flops 403439616 | bytes 4458496 | tf_op jit(solution)/shard_map/dot_general | solution.py:28
  35.6 0.9 fusion.50
  36.5 0.0 copy-start.5
  36.5 5.1 %fusion.52 = (f32[4,16,64]{2,1,0:T(8,128)}, f32[4,16,64,64]{2,3,1,0:T(8,128)}) fusion(bf16[4,64,512,1]{2,1,3,0:T(8,128)(2,1)} %bitcast.69, bf16[16,512]{1,0:T(8,128)(2,1)S(1)} %get-tuple-element.16, bf16[4,64,512]{2,1,0:T(8,128)(2,1)S(1)} %bitcast.66), kind=kOutput, calls=%fused_computation.66 | convolution fusion | flops 271056960 | bytes 1605632 | tf_op jit(solution)/shard_map/sub | solution.py:46
  41.6 0.0 copy-done.5
  41.6 2.6 %fusion.23 = bf16[4,64,512]{2,1,0:T(8,128)(2,1)S(1)} fusion(bf16[4,64,512]{2,1,0:T(8,128)(2,1)S(1)} %copy-done.5, bf16[16,512]{1,0:T(8,128)(2,1)S(1)} %get-tuple-element.16, f32[4,16,64,64]{2,3,1,0:T(8,128)} %get-tuple-element.20, f32[4,16,64]{2,1,0:T(8,128)} %get-tuple-element.19), kind=kOutput, calls=%fused_computation.24 | convolution fusion | flops 271187968 | bytes 1605632 | tf_op jit(solution)/shard_map/wnqk,wnqc->wkc/dot_general | solution.py:50
  44.3 0.0 copy-start.13
  44.3 2.1 %multiply_reduce_fusion.1 = (f32[4,16,64]{2,1,0:T(8,128)S(1)}, f32[4,16,64,64]{2,3,1,0:T(8,128)S(1)}) fusion(f32[4,16,64,64]{2,3,1,0:T(8,128)S(1)} %copy-done.1, f32[4,16,64]{2,1,0:T(8,128)S(1)} %copy-done.10, bf16[4,64,512,1]{2,1,3,0:T(8,128)(2,1)S(1)} %bitcast.71, bf16[4,64,512]{2,1,0:T(8,128)(2,1)S(1)} %copy-done.5, ...), kind=kOutput, calls=%fused_computation.12 | convolution fusion | flops 271314944 | bytes 2670592 | tf_op jit(solution)/shard_map/wnqc,wkc->wnqk/dot_general | solution.py:49
  46.4 0.7 multiply_convert_fusion
  47.1 0.0 copy-start.9
  47.1 0.9 fusion.26
  48.0 0.0 copy-done.7
  48.1 1.3 %multiply_reduce_fusion = f32[4,64,512]{2,1,0:T(8,128)S(1)} fusion(f32[16,512]{1,0:T(8,128)S(1)} %copy-done.9, bf16[4,16,64,64]{2,3,1,0:T(8,128)(2,1)S(1)} %multiply_convert_fusion, bf16[4,64,512,1]{2,1,3,0:T(8,128)(2,1)S(1)} %bitcast.70), kind=kOutput, calls=%fused_computation.1 | convolution fusion | flops 272498688 | bytes 1343488 | tf_op jit(solution)/shard_map/wnqk,wkc->wnqc/dot_general | solution.py:59
  49.4 0.0 copy-start.3
  49.4 0.0 copy-start.11
  49.4 0.0 copy-start.12
  49.4 0.0 copy-done.13
  49.4 0.0 copy-done.14
  49.5 0.6 fusion.33
  50.1 0.0 copy-done.3
  50.1 0.0 copy-done.12
  50.1 0.8 fusion.49
  51.0 0.3 reshape.235
  51.3 0.8 div.55
  52.1 0.8 div.53
  52.9 1.5 %fusion.35 = bf16[1,8,2,4,1,2,2,512]{7,5,3,1,6,2,0,4:T(2,128)(2,1)S(1)} fusion(f32[2,2,8,4,2]{4,3,2,1,0:T(4,128)} %div.55, f32[2,2,8,4,2]{4,3,2,1,0:T(4,128)S(1)} %broadcast_multiply_fusion, f32[2,1,2,8,1,4,2,512]{7,6,5,3,2,0,4,1:T(2,128)S(1)} %reshape.235, f32[2,2,8,4,2]{4,3,2,1,0:T(4,128)} %div.53, f32[2,2,8,4,2]{4,3,2,1,0:T(4,128)S(1)} %add_rsqrt_fusion, ...), kind=kLoop, calls=%fused_computation.42 | loop fusion | flops 1179648 | bytes 1576960 | tf_op jit(solution)/shard_map/transpose | solution.py:794
  54.5 0.3 copy.13
  54.7 0.8 reshape_reshape.8.spread_ref
  55.6 0.1 copy.10
  55.7 2.8 %convolution_convert_fusion.blocks_ref = bf16[64,8,1536]{2,1,0:T(8,128)(2,1)} fusion(bf16[256,512]{1,0:T(8,128)(2,1)} %bitcast.73, bf16[256,512]{1,0:T(8,128)(2,1)} %bitcast.75, bf16[256,512]{1,0:T(8,128)(2,1)S(1)} %bitcast.65, bf16[512,256]{1,0:T(8,128)(2,1)S(1)} %copy.10), kind=kOutput, calls=%fused_computation.10 | convolution fusion | flops 405798912 | bytes 2621440 | tf_op jit(solution)/shard_map/dot_general | solution.py:77
  58.5 53.7 %shard_map.51 = (f32[8,1536]{1,0:T(8,128)}, bf16[64,4,512]{2,1,0:T(4,128)(2,1)}) custom-call(bf16[64,8,1536]{2,1,0:T(8,128)(2,1)} %convolution_convert_fusion.blocks_ref, bf16[64,4,512]{2,1,0:T(4,128)(2,1)} %reshape_reshape.8.spread_ref), custom_call_target="tpu_custom_call" | custom-call | tf_op jit(solution)/shard_map/pallas_call | solution.py:629
  112.2 1.4 %broadcast_multiply_fusion.1 = f32[8,1536]{1,0:T(8,128)} fusion(f32[8,1536]{1,0:T(8,128)} %get-tuple-element.9), kind=kLoop, calls=%fused_computation.47 | loop fusion | flops 12288 | bytes 98304 | tf_op jit(solution)/shard_map/div | solution.py:805
  113.6 1.7 %copy.32 = bf16[1,64,4,512]{3,2,1,0:T(4,128)(2,1)} copy(bf16[1,64,4,512]{3,2,1,0:T(4,128)(2,1)} %bitcast.68) | data formatting | bytes 524288
  (23 shorter events, 0.2 us)
Async XLA Ops:
  0.6 33.6 %copy-start = (bf16[512,1536]{1,0:T(8,128)(2,1)S(1)}, bf16[512,1536]{1,0:T(8,128)(2,1)}, u32[]{:S(2)}) copy-start(bf16[512,1536]{1,0:T(8,128)(2,1)} %param.4) | copy-start | bytes 4718596
  28.8 3.7 %copy-start.6 = (bf16[64,4,512]{2,1,0:T(4,128)(2,1)S(1)}, bf16[64,4,512]{2,1,0:T(4,128)(2,1)}, u32[]{:S(2)}) copy-start(bf16[64,4,512]{2,1,0:T(4,128)(2,1)} %get-tuple-element.7) | copy-start | bytes 786436
  36.5 5.1 %copy-start.5 = (bf16[4,64,512]{2,1,0:T(8,128)(2,1)S(1)}, bf16[4,64,512]{2,1,0:T(8,128)(2,1)}, u32[]{:S(2)}) copy-start(bf16[4,64,512]{2,1,0:T(8,128)(2,1)} %mul.106) | copy-start | bytes 786436
  41.6 2.7 %copy-start.1 = (f32[4,16,64,64]{2,3,1,0:T(8,128)S(1)}, f32[4,16,64,64]{2,3,1,0:T(8,128)}, u32[]{:S(2)}) copy-start(f32[4,16,64,64]{2,3,1,0:T(8,128)} %get-tuple-element.20) | copy-start | bytes 3145732
  41.6 2.7 %copy-start.8 = (bf16[256,512]{1,0:T(8,128)(2,1)S(1)}, bf16[256,512]{1,0:T(8,128)(2,1)}, u32[]{:S(2)}) copy-start(bf16[256,512]{1,0:T(8,128)(2,1)} %get-tuple-element.12) | copy-start | bytes 786436
  41.6 2.7 %copy-start.10 = (f32[4,16,64]{2,1,0:T(8,128)S(1)}, f32[4,16,64]{2,1,0:T(8,128)}, u32[]{:S(2)}) copy-start(f32[4,16,64]{2,1,0:T(8,128)} %get-tuple-element.19) | copy-start | bytes 49156
  44.3 5.2 %copy-start.13 = (bf16[4,64,512]{2,1,0:T(8,128)(2,1)}, bf16[4,64,512]{2,1,0:T(8,128)(2,1)S(1)}, u32[]{:S(2)}) copy-start(bf16[4,64,512]{2,1,0:T(8,128)(2,1)S(1)} %fusion.23) | copy-start | bytes 786436
  47.1 1.0 copy-start.7
  47.1 0.9 copy-start.9
  48.1 1.4 %copy-start.14 = (bf16[4,64,512]{2,1,0:T(8,128)(2,1)}, bf16[4,64,512]{2,1,0:T(8,128)(2,1)S(1)}, u32[]{:S(2)}) copy-start(bf16[4,64,512]{2,1,0:T(8,128)(2,1)S(1)} %fusion.26) | copy-start | bytes 786436
  49.4 0.7 copy-start.3
  49.4 0.7 copy-start.11
  49.4 0.7 copy-start.12
  51.3 4.3 %copy-start.2 = (bf16[512,256]{0,1:T(8,128)(2,1)S(1)}, bf16[512,256]{0,1:T(8,128)(2,1)}, u32[]{:S(2)}) copy-start(bf16[512,256]{0,1:T(8,128)(2,1)} %get-tuple-element.14) | copy-start | bytes 786436
  51.3 4.4 %copy-start.4 = (bf16[4,64,512]{2,1,0:T(8,128)(2,1)S(1)}, bf16[4,64,512]{2,1,0:T(8,128)(2,1)}, u32[]{:S(2)}) copy-start(bf16[4,64,512]{2,1,0:T(8,128)(2,1)} %copy-done.3) | copy-start | bytes 786436

commit v12 on v7

--- a/solution.py
+++ b/solution.py
@@ -296,13 +296,6 @@
 
     pair_copy.wait()
 
-    @pl.loop(0, half)
-    def _(index):
-        pair_sum[index] = (
-            blocks_ref[mine_start + index].astype(jnp.float32)
-            + pair_held[index].astype(jnp.float32)
-        ).astype(pair_sum.dtype)
-
     def sum_copy(index):
         target = mine_start + index
         step = lax.rem(target - tile + tile_count, tile_count)
@@ -317,6 +310,11 @@
 
     @pl.loop(0, half)
     def _(index):
+        pair_sum[index] = (
+            blocks_ref[mine_start + index].astype(jnp.float32)
+            + pair_held[index].astype(jnp.float32)
+        ).astype(pair_sum.dtype)
+
         @pl.when(mine_start + index != tile)
         def _():
             sum_copy(index).start()
@@ -339,8 +337,7 @@
         own.start()
         own.wait()
 
-        @pl.loop(1, tile_count)
-        def _(step):
+        def add_arrival(step, total):
             pltpu.make_async_remote_copy(
                 src_ref=pair_sum.at[0],
                 dst_ref=arrived.at[tile],
@@ -349,12 +346,11 @@
                 device_id=tile_peer(step),
                 device_id_type=mesh_id,
             ).wait_recv()
-
-        def add_source(source, total):
+            source = lax.rem(tile - step + tile_count, tile_count)
             return total + arrived[source].astype(jnp.float32)
 
         partial[...] = lax.fori_loop(
-            0, tile_count, add_source, jnp.zeros(partial.shape, jnp.float32)
+            1, tile_count, add_arrival, arrived[tile].astype(jnp.float32)
         )
         held[plane] = partial[...]
 
@@ -401,7 +397,7 @@
         back_copy(step).wait()
 
     returned_ref[...] = returned_held[...]
-    out_ref[...] = final[...]
+    out_ref[...] = final[...] * (1.0 / (rep_count * tile_count))
 
 
 def paired_sum(row_blocks, spread):
@@ -584,8 +580,8 @@
         returned = lax.all_to_all(spread, ("ty", "tx"), split_axis=1, concat_axis=1, tiled=True)
         gathered = lax.all_to_all(row_blocks.astype(jnp.bfloat16), ("ty", "tx"), 0, 0, tiled=True)
         weight_grad = lax.psum(jnp.sum(gathered.astype(jnp.float32), axis=0), "rep")
+        weight_grad = weight_grad / (rep_count * tile_count)
     token_grad = returned.reshape(1, tile_height, tile_width, channels)
-    weight_grad = weight_grad / (rep_count * tile_count)
     return (token_grad, weight_grad)
 
 

time: 114 us -> 113 us (level)
  other arithmetic: 6.15 us -> 4.73 us
  local copies, waits for them, and re-layouts: 10.3 us -> 11.7 us
    div x1 -> x0, other arithmetic: 1.42 us -> none  [shards(): weight_grad = weight_grad / (rep_count * tile_count)]
    unnamed x31 -> x32, local copies, waits for them, and re-layouts: 1.89 us -> 3.31 us
where the time goes in v12:
time: 113 us
  Pallas kernels  78.9 us (70%)
  matrix products  16.8 us (15%)
  local copies, waits for them, and re-layouts  11.7 us (10%)
  other arithmetic  4.73 us (4%)
    pallas_call x1, Pallas kernels, paired_sum(): pl.pallas_call(functools.partial(paired_sum_kernel, rep_count, tile_count...  51.4 us
    pallas_call x1, Pallas kernels, exchange(): pl.pallas_call(functools.partial(exchange_kernel, tile_count, col_tiles),...  27.5 us
    sub x1, matrix products, window_grads(): exponent = jnp.exp(scores - peak_score)  5.13 us
    unnamed x32, local copies, waits for them, and re-layouts  3.31 us
    dot_general x1, matrix products, window_grads(): lax.dot_general(normed, proj_grad, (((0,), (0,)), ((), ())), preferred_el...  2.76 us
    dot_general x1, matrix products, window_grads(): jnp.einsum('wnqk,wnqc->wkc', probs_low, grad_spread, preferred_element_ty...  2.63 us

profile of v12, /device:TPU:63, one launch (start us, length us, event | category | flops | bytes accessed | tf_op | source)
XLA Modules:
  0.0 113.0 jit_solution(7073276864551983096)
XLA Ops:
  0.6 0.0 copy-start
  0.7 0.6 fusion.44
  1.3 27.5 %shard_map.50 = (bf16[64,4,512]{2,1,0:T(4,128)(2,1)}, bf16[64,4,512]{2,1,0:T(4,128)(2,1)}) custom-call(bf16[1,64,4,512]{3,2,1,0:T(4,128)(2,1)} %tokens_ref.1, bf16[1,64,4,512]{3,2,1,0:T(4,128)(2,1)} %cot_ref.1), custom_call_target="tpu_custom_call" | custom-call | tf_op jit(solution)/shard_map/pallas_call | solution.py:500
  28.8 1.2 %reshape.239 = f32[1,8,2,4,1,2,2,512]{7,6,5,3,2,1,4,0:T(2,128)S(1)} reshape(bf16[64,4,512]{2,1,0:T(4,128)(2,1)} %get-tuple-element.6) | data formatting | bytes 786432 | tf_op jit(solution)/shard_map/convert_element_type | solution.py:26
  30.0 0.4 fusion.48
  30.4 0.7 div.40
  31.2 0.5 multiply_reduce_fusion.3
  31.7 0.7 rsqrt.13
  32.4 0.0 copy-done.6
  32.4 0.1 reshape_reshape.7
  32.6 0.2 copy.30
  32.8 0.8 mul.106
  33.6 0.3 copy.29
  33.9 0.4 reshape.237
  34.2 0.0 copy-done
  34.2 1.3 %fusion.51 = (bf16[256,1536]{1,0:T(8,128)(2,1)S(1)}, f32[256,1536]{1,0:T(8,128)S(1)}) fusion(bf16[512,1536]{1,0:T(8,128)(2,1)S(1)} %copy-done, f32[256,512]{1,0:T(8,128)S(1)} %reshape.237, f32[256]{0:T(256)} %rsqrt.13, f32[256]{0:T(256)} %div.40), kind=kOutput, calls=%fused_computation.64 | convolution fusion | flops 403439616 | bytes 4458496 | tf_op jit(solution)/shard_map/dot_general | solution.py:28
  35.6 0.9 fusion.50
  36.5 0.0 copy-start.5
  36.5 5.1 %fusion.52 = (f32[4,16,64]{2,1,0:T(8,128)}, f32[4,16,64,64]{2,3,1,0:T(8,128)}) fusion(bf16[4,64,512,1]{2,1,3,0:T(8,128)(2,1)} %bitcast.69, bf16[16,512]{1,0:T(8,128)(2,1)S(1)} %get-tuple-element.16, bf16[4,64,512]{2,1,0:T(8,128)(2,1)S(1)} %bitcast.66), kind=kOutput, calls=%fused_computation.65 | convolution fusion | flops 271056960 | bytes 1605632 | tf_op jit(solution)/shard_map/sub | solution.py:46
  41.6 0.0 copy-done.5
  41.6 2.6 %fusion.23 = bf16[4,64,512]{2,1,0:T(8,128)(2,1)S(1)} fusion(bf16[4,64,512]{2,1,0:T(8,128)(2,1)S(1)} %copy-done.5, bf16[16,512]{1,0:T(8,128)(2,1)S(1)} %get-tuple-element.16, f32[4,16,64,64]{2,3,1,0:T(8,128)} %get-tuple-element.20, f32[4,16,64]{2,1,0:T(8,128)} %get-tuple-element.19), kind=kOutput, calls=%fused_computation.24 | convolution fusion | flops 271187968 | bytes 1605632 | tf_op jit(solution)/shard_map/wnqk,wnqc->wkc/dot_general | solution.py:50
  44.3 0.0 copy-start.13
  44.3 2.1 %multiply_reduce_fusion.1 = (f32[4,16,64]{2,1,0:T(8,128)S(1)}, f32[4,16,64,64]{2,3,1,0:T(8,128)S(1)}) fusion(f32[4,16,64,64]{2,3,1,0:T(8,128)S(1)} %copy-done.1, f32[4,16,64]{2,1,0:T(8,128)S(1)} %copy-done.10, bf16[4,64,512,1]{2,1,3,0:T(8,128)(2,1)S(1)} %bitcast.71, bf16[4,64,512]{2,1,0:T(8,128)(2,1)S(1)} %copy-done.5, ...), kind=kOutput, calls=%fused_computation.12 | convolution fusion | flops 271314944 | bytes 2670592 | tf_op jit(solution)/shard_map/wnqc,wkc->wnqk/dot_general | solution.py:49
  46.4 0.7 multiply_convert_fusion
  47.1 0.0 copy-start.9
  47.1 0.9 fusion.26
  48.0 0.0 copy-done.7
  48.1 1.3 %multiply_reduce_fusion = f32[4,64,512]{2,1,0:T(8,128)S(1)} fusion(f32[16,512]{1,0:T(8,128)S(1)} %copy-done.9, bf16[4,16,64,64]{2,3,1,0:T(8,128)(2,1)S(1)} %multiply_convert_fusion, bf16[4,64,512,1]{2,1,3,0:T(8,128)(2,1)S(1)} %bitcast.70), kind=kOutput, calls=%fused_computation.1 | convolution fusion | flops 272498688 | bytes 1343488 | tf_op jit(solution)/shard_map/wnqk,wkc->wnqc/dot_general | solution.py:59
  49.4 0.0 copy-start.3
  49.4 0.0 copy-start.11
  49.4 0.0 copy-start.12
  49.4 0.0 copy-done.13
  49.4 0.0 copy-done.14
  49.5 0.6 fusion.33
  50.1 0.0 copy-done.3
  50.1 0.0 copy-done.12
  50.1 0.8 fusion.49
  51.0 0.3 reshape.235
  51.3 0.8 div.49
  52.1 0.8 div.47
  52.9 1.5 %fusion.35 = bf16[1,8,2,4,1,2,2,512]{7,5,3,1,6,2,0,4:T(2,128)(2,1)S(1)} fusion(f32[2,2,8,4,2]{4,3,2,1,0:T(4,128)} %div.49, f32[2,2,8,4,2]{4,3,2,1,0:T(4,128)S(1)} %broadcast_multiply_fusion, f32[2,1,2,8,1,4,2,512]{7,6,5,3,2,0,4,1:T(2,128)S(1)} %reshape.235, f32[2,2,8,4,2]{4,3,2,1,0:T(4,128)} %div.47, f32[2,2,8,4,2]{4,3,2,1,0:T(4,128)S(1)} %add_rsqrt_fusion, ...), kind=kLoop, calls=%fused_computation.42 | loop fusion | flops 1179648 | bytes 1576960 | tf_op jit(solution)/shard_map/transpose | solution.py:573
  54.5 0.3 copy.13
  54.7 0.8 reshape_reshape.8.spread_ref
  55.6 0.1 copy.10
  55.7 2.8 %convolution_convert_fusion.blocks_ref = bf16[64,8,1536]{2,1,0:T(8,128)(2,1)} fusion(bf16[256,512]{1,0:T(8,128)(2,1)} %bitcast.73, bf16[256,512]{1,0:T(8,128)(2,1)} %bitcast.75, bf16[256,512]{1,0:T(8,128)(2,1)S(1)} %bitcast.65, bf16[512,256]{1,0:T(8,128)(2,1)S(1)} %copy.10), kind=kOutput, calls=%fused_computation.10 | convolution fusion | flops 405798912 | bytes 2621440 | tf_op jit(solution)/shard_map/dot_general | solution.py:77
  58.5 51.4 %shard_map.51 = (f32[8,1536]{1,0:T(8,128)}, bf16[64,4,512]{2,1,0:T(4,128)(2,1)}) custom-call(bf16[64,8,1536]{2,1,0:T(8,128)(2,1)} %convolution_convert_fusion.blocks_ref, bf16[64,4,512]{2,1,0:T(4,128)(2,1)} %reshape_reshape.8.spread_ref), custom_call_target="tpu_custom_call" | custom-call | tf_op jit(solution)/shard_map/pallas_call | solution.py:409
  109.9 1.7 %copy.33 = bf16[1,64,4,512]{3,2,1,0:T(4,128)(2,1)} copy(bf16[1,64,4,512]{3,2,1,0:T(4,128)(2,1)} %bitcast.68) | data formatting | bytes 524288
  111.6 1.4 %copy.34 = f32[8,1536]{1,0:T(8,128)} copy(f32[8,1536]{1,0:T(8,128)} %get-tuple-element.28) | data formatting | bytes 98304
  (23 shorter events, 0.2 us)
Async XLA Ops:
  0.6 33.6 %copy-start = (bf16[512,1536]{1,0:T(8,128)(2,1)S(1)}, bf16[512,1536]{1,0:T(8,128)(2,1)}, u32[]{:S(2)}) copy-start(bf16[512,1536]{1,0:T(8,128)(2,1)} %param.4) | copy-start | bytes 4718596
  28.8 3.7 %copy-start.6 = (bf16[64,4,512]{2,1,0:T(4,128)(2,1)S(1)}, bf16[64,4,512]{2,1,0:T(4,128)(2,1)}, u32[]{:S(2)}) copy-start(bf16[64,4,512]{2,1,0:T(4,128)(2,1)} %get-tuple-element.7) | copy-start | bytes 786436
  36.5 5.1 %copy-start.5 = (bf16[4,64,512]{2,1,0:T(8,128)(2,1)S(1)}, bf16[4,64,512]{2,1,0:T(8,128)(2,1)}, u32[]{:S(2)}) copy-start(bf16[4,64,512]{2,1,0:T(8,128)(2,1)} %mul.106) | copy-start | bytes 786436
  41.6 2.7 %copy-start.1 = (f32[4,16,64,64]{2,3,1,0:T(8,128)S(1)}, f32[4,16,64,64]{2,3,1,0:T(8,128)}, u32[]{:S(2)}) copy-start(f32[4,16,64,64]{2,3,1,0:T(8,128)} %get-tuple-element.20) | copy-start | bytes 3145732
  41.6 2.7 %copy-start.8 = (bf16[256,512]{1,0:T(8,128)(2,1)S(1)}, bf16[256,512]{1,0:T(8,128)(2,1)}, u32[]{:S(2)}) copy-start(bf16[256,512]{1,0:T(8,128)(2,1)} %get-tuple-element.12) | copy-start | bytes 786436
  41.6 2.7 %copy-start.10 = (f32[4,16,64]{2,1,0:T(8,128)S(1)}, f32[4,16,64]{2,1,0:T(8,128)}, u32[]{:S(2)}) copy-start(f32[4,16,64]{2,1,0:T(8,128)} %get-tuple-element.19) | copy-start | bytes 49156
  44.3 5.2 %copy-start.13 = (bf16[4,64,512]{2,1,0:T(8,128)(2,1)}, bf16[4,64,512]{2,1,0:T(8,128)(2,1)S(1)}, u32[]{:S(2)}) copy-start(bf16[4,64,512]{2,1,0:T(8,128)(2,1)S(1)} %fusion.23) | copy-start | bytes 786436
  47.1 1.0 copy-start.7
  47.1 0.9 copy-start.9
  48.1 1.4 %copy-start.14 = (bf16[4,64,512]{2,1,0:T(8,128)(2,1)}, bf16[4,64,512]{2,1,0:T(8,128)(2,1)S(1)}, u32[]{:S(2)}) copy-start(bf16[4,64,512]{2,1,0:T(8,128)(2,1)S(1)} %fusion.26) | copy-start | bytes 786436
  49.4 0.7 copy-start.3
  49.4 0.7 copy-start.11
  49.4 0.7 copy-start.12
  51.3 4.3 %copy-start.2 = (bf16[512,256]{0,1:T(8,128)(2,1)S(1)}, bf16[512,256]{0,1:T(8,128)(2,1)}, u32[]{:S(2)}) copy-start(bf16[512,256]{0,1:T(8,128)(2,1)} %get-tuple-element.14) | copy-start | bytes 786436
  51.3 4.4 %copy-start.4 = (bf16[4,64,512]{2,1,0:T(8,128)(2,1)S(1)}, bf16[4,64,512]{2,1,0:T(8,128)(2,1)}, u32[]{:S(2)}) copy-start(bf16[4,64,512]{2,1,0:T(8,128)(2,1)} %copy-done.3) | copy-start | bytes 786436

commit v13 on v7

--- a/solution.py
+++ b/solution.py
@@ -42,7 +42,7 @@
     query_spread = spread(query)
     grad_spread = spread(grad)
     scores = jnp.einsum("wnqc,wkc->wnqk", query_spread, key, preferred_element_type=jnp.float32)
-    peak_score = jnp.max(scores, axis=-1, keepdims=True)
+    peak_score = lax.optimization_barrier(jnp.max(scores, axis=-1, keepdims=True))
     exponent = jnp.exp(scores - peak_score)
     attn_probs = exponent / jnp.sum(exponent, axis=-1, keepdims=True)
     probs_low = attn_probs.astype(jnp.bfloat16)

time: 114 us -> 109 us (0.956)
  matrix products: 16.8 us -> 12.1 us
    sub x1 -> x0, matrix products: 5.13 us -> none  [window_grads(): exponent = jnp.exp(scores - peak_score)]
    dot_general x0 -> x1, matrix products: none -> 2.13 us  [window_grads(): jnp.einsum('wnqc,wkc->wnqk', query_spread, key, preferred_element_type=jn...]
    dot_general x1, matrix products: 2.63 us -> 0.96 us  [window_grads(): jnp.einsum('wnqk,wnqc->wkc', probs_low, grad_spread, preferred_element_ty...]
where the time goes in v13:
time: 109 us
  Pallas kernels  79.2 us (73%)
  matrix products  12.1 us (11%)
  local copies, waits for them, and re-layouts  9.84 us (9%)
  other arithmetic  6.74 us (6%)
    pallas_call x1, Pallas kernels, paired_sum(): pl.pallas_call(functools.partial(paired_sum_kernel, rep_count, tile_count...  51.8 us
    pallas_call x1, Pallas kernels, exchange(): pl.pallas_call(functools.partial(exchange_kernel, tile_count, col_tiles),...  27.5 us
    dot_general x1, matrix products, window_grads(): lax.dot_general(normed, proj_grad, (((0,), (0,)), ((), ())), preferred_el...  2.76 us
    unnamed x23, local copies, waits for them, and re-layouts  2.26 us

profile of v13, /device:TPU:63, one launch (start us, length us, event | category | flops | bytes accessed | tf_op | source)
XLA Modules:
  0.0 108.8 jit_solution(8485265221107354845)
XLA Ops:
  0.6 0.0 copy-start
  0.7 0.6 fusion.43
  1.3 27.5 %shard_map.50 = (bf16[64,4,512]{2,1,0:T(4,128)(2,1)}, bf16[64,4,512]{2,1,0:T(4,128)(2,1)}) custom-call(bf16[1,64,4,512]{3,2,1,0:T(4,128)(2,1)} %tokens_ref.1, bf16[1,64,4,512]{3,2,1,0:T(4,128)(2,1)} %cot_ref.1), custom_call_target="tpu_custom_call" | custom-call | tf_op jit(solution)/shard_map/pallas_call | solution.py:504
  28.8 0.0 copy-start.5
  28.8 1.2 %reshape.238 = f32[1,8,2,4,1,2,2,512]{7,6,5,3,2,1,4,0:T(2,128)S(1)} reshape(bf16[64,4,512]{2,1,0:T(4,128)(2,1)} %get-tuple-element.6) | data formatting | bytes 786432 | tf_op jit(solution)/shard_map/convert_element_type | solution.py:26
  30.0 0.4 fusion.47
  30.4 0.7 div.46
  31.2 0.5 multiply_reduce_fusion.3
  31.7 0.7 rsqrt.13
  32.4 0.0 copy-done.5
  32.4 0.1 reshape_reshape.7
  32.5 0.2 copy.30
  32.8 0.8 mul.106
  33.6 0.3 copy.29
  33.9 0.4 reshape.236
  34.2 0.0 copy-done
  34.2 1.3 %fusion.51 = (bf16[256,1536]{1,0:T(8,128)(2,1)S(1)}, f32[256,1536]{1,0:T(8,128)S(1)}) fusion(bf16[512,1536]{1,0:T(8,128)(2,1)S(1)} %copy-done, f32[256,512]{1,0:T(8,128)S(1)} %reshape.236, f32[256]{0:T(256)} %rsqrt.13, f32[256]{0:T(256)} %div.46), kind=kOutput, calls=%fused_computation.65 | convolution fusion | flops 403439616 | bytes 4458496 | tf_op jit(solution)/shard_map/dot_general | solution.py:28
  35.6 2.1 %fusion.52 = (f32[4,16,64]{2,1,0:T(8,128)S(1)}, f32[4,16,64,64]{2,3,1,0:T(8,128)S(1)}) fusion(bf16[4,64,512,1]{2,1,3,0:T(8,128)(2,1)S(1)} %bitcast.71, bf16[16,512]{1,0:T(8,128)(2,1)S(1)} %get-tuple-element.16, bf16[4,64,512]{2,1,0:T(8,128)(2,1)S(1)} %bitcast.68), kind=kOutput, calls=%fused_computation.66 | convolution fusion | flops 270790656 | bytes 1605632 | tf_op jit(solution)/shard_map/wnqc,wkc->wnqk/dot_general | solution.py:44
  37.8 0.0 copy-start.4
  37.8 0.5 fusion.17
  38.3 0.4 copy-done.4
  38.7 1.0 fusion.24
  39.7 0.0 copy-start.9
  39.7 2.2 %multiply_reduce_fusion.1 = (f32[4,16,64]{2,1,0:T(8,128)S(1)}, f32[4,16,64,64]{2,3,1,0:T(8,128)S(1)}) fusion(f32[4,16,64]{2,1,0:T(8,128)S(1)} %fusion.17, f32[4,16,64,64]{2,3,1,0:T(8,128)S(1)} %get-tuple-element.20, f32[4,16,64]{2,1,0:T(8,128)S(1)} %get-tuple-element.19, bf16[4,64,512,1]{2,1,3,0:T(8,128)(2,1)S(1)} %bitcast.73, ...), kind=kOutput, calls=%fused_computation.11 | convolution fusion | flops 271577088 | bytes 2686976 | tf_op jit(solution)/shard_map/wnqc,wkc->wnqk/dot_general | solution.py:49
  41.9 0.7 multiply_convert_fusion
  42.6 0.0 copy-start.6
  42.6 0.9 fusion.27
  43.5 0.0 copy-done.6
  43.5 0.0 copy-start.10
  43.5 1.3 %multiply_reduce_fusion = f32[4,64,512]{2,1,0:T(8,128)S(1)} fusion(f32[16,512]{1,0:T(8,128)S(1)} %copy-done.6, bf16[4,16,64,64]{2,3,1,0:T(8,128)(2,1)S(1)} %multiply_convert_fusion, bf16[4,64,512,1]{2,1,3,0:T(8,128)(2,1)S(1)} %bitcast.72), kind=kOutput, calls=%fused_computation | convolution fusion | flops 272498688 | bytes 1343488 | tf_op jit(solution)/shard_map/wnqk,wkc->wnqc/dot_general | solution.py:59
  44.9 0.6 fusion.34
  45.5 0.0 copy-done.2
  45.6 0.0 copy-done.7
  45.6 0.0 copy-done.8
  45.6 0.8 fusion.49
  46.4 0.3 reshape.234
  46.8 0.8 div.55
  47.6 0.8 div.53
  48.4 1.5 %fusion.36 = bf16[1,8,2,4,1,2,2,512]{7,5,3,1,6,2,0,4:T(2,128)(2,1)S(1)} fusion(f32[2,2,8,4,2]{4,3,2,1,0:T(4,128)} %div.55, f32[2,2,8,4,2]{4,3,2,1,0:T(4,128)S(1)} %broadcast_multiply_fusion, f32[2,1,2,8,1,4,2,512]{7,6,5,3,2,0,4,1:T(2,128)S(1)} %reshape.234, f32[2,2,8,4,2]{4,3,2,1,0:T(4,128)} %div.53, f32[2,2,8,4,2]{4,3,2,1,0:T(4,128)S(1)} %add_rsqrt_fusion, ...), kind=kLoop, calls=%fused_computation.42 | loop fusion | flops 1179648 | bytes 1576960 | tf_op jit(solution)/shard_map/transpose | solution.py:577
  49.9 0.3 copy.13
  50.2 0.8 reshape_reshape.8.spread_ref
  51.0 0.0 copy-done.1
  51.0 0.1 copy.10
  51.1 0.0 copy-done.3
  51.1 2.8 %convolution_convert_fusion.blocks_ref = bf16[64,8,1536]{2,1,0:T(8,128)(2,1)} fusion(bf16[256,512]{1,0:T(8,128)(2,1)} %bitcast.75, bf16[256,512]{1,0:T(8,128)(2,1)} %bitcast.77, bf16[256,512]{1,0:T(8,128)(2,1)S(1)} %bitcast.67, bf16[512,256]{1,0:T(8,128)(2,1)S(1)} %copy.10), kind=kOutput, calls=%fused_computation.9 | convolution fusion | flops 405798912 | bytes 2621440 | tf_op jit(solution)/shard_map/dot_general | solution.py:77
  53.9 51.8 %shard_map.51 = (f32[8,1536]{1,0:T(8,128)}, bf16[64,4,512]{2,1,0:T(4,128)(2,1)}) custom-call(bf16[64,8,1536]{2,1,0:T(8,128)(2,1)} %convolution_convert_fusion.blocks_ref, bf16[64,4,512]{2,1,0:T(4,128)(2,1)} %reshape_reshape.8.spread_ref), custom_call_target="tpu_custom_call" | custom-call | tf_op jit(solution)/shard_map/pallas_call | solution.py:413
  105.7 1.4 %broadcast_multiply_fusion.1 = f32[8,1536]{1,0:T(8,128)} fusion(f32[8,1536]{1,0:T(8,128)} %get-tuple-element.9), kind=kLoop, calls=%fused_computation.47 | loop fusion | flops 12288 | bytes 98304 | tf_op jit(solution)/shard_map/div | solution.py:588
  107.1 1.7 %copy.32 = bf16[1,64,4,512]{3,2,1,0:T(4,128)(2,1)} copy(bf16[1,64,4,512]{3,2,1,0:T(4,128)(2,1)} %bitcast.70) | data formatting | bytes 524288
  (16 shorter events, 0.2 us)
Async XLA Ops:
  0.6 33.6 %copy-start = (bf16[512,1536]{1,0:T(8,128)(2,1)S(1)}, bf16[512,1536]{1,0:T(8,128)(2,1)}, u32[]{:S(2)}) copy-start(bf16[512,1536]{1,0:T(8,128)(2,1)} %param.4) | copy-start | bytes 4718596
  28.8 3.7 %copy-start.5 = (bf16[64,4,512]{2,1,0:T(4,128)(2,1)S(1)}, bf16[64,4,512]{2,1,0:T(4,128)(2,1)}, u32[]{:S(2)}) copy-start(bf16[64,4,512]{2,1,0:T(4,128)(2,1)} %get-tuple-element.7) | copy-start | bytes 786436
  37.8 1.0 copy-start.4
  39.7 5.2 %copy-start.9 = (bf16[4,64,512]{2,1,0:T(8,128)(2,1)}, bf16[4,64,512]{2,1,0:T(8,128)(2,1)S(1)}, u32[]{:S(2)}) copy-start(bf16[4,64,512]{2,1,0:T(8,128)(2,1)S(1)} %fusion.24) | copy-start | bytes 786436
  42.6 0.9 copy-start.6
  43.5 1.4 %copy-start.10 = (bf16[4,64,512]{2,1,0:T(8,128)(2,1)}, bf16[4,64,512]{2,1,0:T(8,128)(2,1)S(1)}, u32[]{:S(2)}) copy-start(bf16[4,64,512]{2,1,0:T(8,128)(2,1)S(1)} %fusion.27) | copy-start | bytes 786436
  44.9 0.7 copy-start.2
  44.9 0.7 copy-start.7
  44.9 0.7 copy-start.8
  46.7 4.3 %copy-start.1 = (bf16[512,256]{0,1:T(8,128)(2,1)S(1)}, bf16[512,256]{0,1:T(8,128)(2,1)}, u32[]{:S(2)}) copy-start(bf16[512,256]{0,1:T(8,128)(2,1)} %get-tuple-element.14) | copy-start | bytes 786436
  46.7 4.4 %copy-start.3 = (bf16[4,64,512]{2,1,0:T(8,128)(2,1)S(1)}, bf16[4,64,512]{2,1,0:T(8,128)(2,1)}, u32[]{:S(2)}) copy-start(bf16[4,64,512]{2,1,0:T(8,128)(2,1)} %copy-done.2) | copy-start | bytes 786436

commit v14 on v13

--- a/solution.py
+++ b/solution.py
@@ -23,7 +23,7 @@
 
 def window_grads(window_x, window_g, qkv_weight):
     win_count, win_tokens, channels = window_x.shape
-    standard, inv_std = normalize(window_x.astype(jnp.float32))
+    standard, inv_std = lax.optimization_barrier(normalize(window_x.astype(jnp.float32)))
     normed = standard.astype(jnp.bfloat16).reshape(win_count * win_tokens, channels)
     projection = jnp.dot(normed, qkv_weight, preferred_element_type=jnp.float32)
     flat_shape = (win_count, win_tokens, channels)
@@ -563,7 +563,8 @@
             .reshape(win_count, GRID * GRID, channels)
         )
 
-    grad_windows, weight_term = window_grads(to_windows(grid_x), to_windows(grid_g), qkv_weight)
+    window_x, window_g = lax.optimization_barrier((to_windows(grid_x), to_windows(grid_g)))
+    grad_windows, weight_term = window_grads(window_x, window_g, qkv_weight)
     back_shape = (
         fold_rows,
         inner_rows,

time: 109 us -> 102 us (0.936)
  local copies, waits for them, and re-layouts: 9.84 us -> 5.91 us
  other arithmetic: 6.74 us -> 3.61 us
    another operation x2 -> x4, local copies, waits for them, and re-layouts: 0.31 us -> 2.51 us  [to_windows(): values.reshape(token_shape).transpose(2, 4, 6, 1, 0, 3, 5, 7)]
    convert_element_type x3 -> x0, local copies, waits for them, and re-layouts: 1.88 us -> none  [window_grads(): standard, inv_std = normalize(window_x.astype(jnp.float32))]
    transpose x1 -> x0, other arithmetic: 1.54 us -> none  [shards(): grad_windows.reshape(back_shape).transpose(4, 3, 0, 5, 1, 6, 2, 7)]
    div x2 -> x0, local copies, waits for them, and re-layouts: 1.52 us -> none  [the longest x1 0.79 us: window_grads(): jnp.mean(normed_grad * standard, axis=-1, keepdims=True)]
    unnamed x23 -> x9, local copies, waits for them, and re-layouts: 2.26 us -> 1.77 us
where the time goes in v14:
time: 102 us; the launch traced here: 101 us
  Pallas kernels  79.3 us (78%)
  matrix products  11.5 us (11%)
  local copies, waits for them, and re-layouts  5.91 us (6%)
  other arithmetic  3.61 us (4%)
    pallas_call x1, Pallas kernels, paired_sum(): pl.pallas_call(functools.partial(paired_sum_kernel, rep_count, tile_count...  51.7 us
    pallas_call x1, Pallas kernels, exchange(): pl.pallas_call(functools.partial(exchange_kernel, tile_count, col_tiles),...  27.6 us
    dot_general x1, matrix products, window_grads(): lax.dot_general(normed, proj_grad, (((0,), (0,)), ((), ())), preferred_el...  2.84 us
    another operation x4, local copies, waits for them, and re-layouts, to_windows(): values.reshape(token_shape).transpose(2, 4, 6, 1, 0, 3, 5, 7)  2.51 us
    dot_general x1, matrix products, window_grads(): jnp.einsum('wnqc,wkc->wnqk', grad_spread, value, preferred_element_type=j...  2.16 us
    dot_general x1, matrix products, window_grads(): jnp.einsum('wnqc,wkc->wnqk', query_spread, key, preferred_element_type=jn...  2.13 us

profile of v14, /device:TPU:63, one launch (start us, length us, event | category | flops | bytes accessed | tf_op | source)
XLA Modules:
  0.0 101.3 jit_solution(2304196145126169268)
XLA Ops:
  0.6 0.0 copy-start
  0.6 27.6 %shard_map.50 = (bf16[64,4,512]{2,1,0:T(4,128)(2,1)}, bf16[64,4,512]{2,1,0:T(4,128)(2,1)}) custom-call(bf16[1,64,4,512]{3,2,1,0:T(4,128)(2,1)} %tokens_ref.1, bf16[1,64,4,512]{3,2,1,0:T(4,128)(2,1)} %cot_ref.1), custom_call_target="tpu_custom_call" | custom-call | tf_op jit(solution)/shard_map/pallas_call | solution.py:504
  28.2 1.1 %reshape_reshape.9 = bf16[1,8,2,4,1,2,2,512]{7,6,5,3,2,1,4,0:T(2,128)(2,1)S(1)} reshape(bf16[64,4,512]{2,1,0:T(4,128)(2,1)} %get-tuple-element.10) | data formatting | bytes 524288 | tf_op jit(solution)/shard_map/reshape;reshape | solution.py:561
  29.3 0.2 copy.20
  29.5 0.1 reshape.176
  29.6 1.1 %reshape_reshape.10 = bf16[1,8,2,4,1,2,2,512]{7,6,5,3,2,1,4,0:T(2,128)(2,1)S(1)} reshape(bf16[64,4,512]{2,1,0:T(4,128)(2,1)} %get-tuple-element.11) | data formatting | bytes 524288 | tf_op jit(solution)/shard_map/reshape;reshape | solution.py:561
  30.7 0.2 copy.19
  30.9 0.1 reshape.177
  31.0 0.1 convert_reduce_fusion
  31.1 0.2 fusion.34
  31.3 0.1 fusion.32
  31.5 0.0 copy-done
  31.6 0.6 fusion.48
  32.3 2.1 %fusion.49 = (f32[4,16,64]{2,1,0:T(8,128)S(1)}, f32[4,16,64,64]{2,3,1,0:T(8,128)S(1)}) fusion(bf16[4,64,512,1]{2,1,3,0:T(8,128)(2,1)S(1)} %bitcast.73, bf16[16,512]{1,0:T(8,128)(2,1)S(1)} %get-tuple-element.21, bf16[4,64,512]{2,1,0:T(8,128)(2,1)S(1)} %bitcast.70), kind=kOutput, calls=%fused_computation.64 | convolution fusion | flops 270790656 | bytes 1605632 | tf_op jit(solution)/shard_map/wnqc,wkc->wnqk/dot_general | solution.py:44
  34.4 0.5 fusion.17
  34.9 2.2 %multiply_reduce_fusion.1 = (f32[4,16,64]{2,1,0:T(8,128)S(1)}, f32[4,16,64,64]{2,3,1,0:T(8,128)S(1)}) fusion(f32[4,16,64]{2,1,0:T(8,128)S(1)} %fusion.17, f32[4,16,64,64]{2,3,1,0:T(8,128)S(1)} %get-tuple-element.27, f32[4,16,64]{2,1,0:T(8,128)S(1)} %get-tuple-element.26, bf16[4,64,512,1]{2,1,3,0:T(8,128)(2,1)S(1)} %bitcast.75, ...), kind=kOutput, calls=%fused_computation.11 | convolution fusion | flops 271577088 | bytes 2686976 | tf_op jit(solution)/shard_map/wnqc,wkc->wnqk/dot_general | solution.py:49
  37.1 0.7 multiply_convert_fusion
  37.8 1.3 %multiply_reduce_fusion = f32[4,64,512]{2,1,0:T(8,128)S(1)} fusion(f32[16,512]{1,0:T(8,128)S(1)} %get-tuple-element.20, bf16[4,16,64,64]{2,3,1,0:T(8,128)(2,1)S(1)} %multiply_convert_fusion, bf16[4,64,512,1]{2,1,3,0:T(8,128)(2,1)S(1)} %bitcast.74), kind=kOutput, calls=%fused_computation | convolution fusion | flops 272498688 | bytes 1343488 | tf_op jit(solution)/shard_map/wnqk,wkc->wnqc/dot_general | solution.py:59
  39.2 0.0 copy-start.1
  39.2 0.9 fusion.27
  40.1 0.0 copy-start.2
  40.1 1.0 fusion.24
  41.1 0.0 copy-start.3
  41.1 0.0 copy-done.1
  41.1 0.0 copy-done.2
  41.1 0.7 fusion.50
  41.8 0.0 copy-done.3
  41.8 0.1 multiply_reduce_fusion.2
  41.9 0.1 div.48
  42.0 0.2 add_convert_fusion
  42.2 0.1 reshape.184
  42.3 0.3 copy.11
  42.6 0.8 reshape_reshape.11.spread_ref
  43.4 0.1 copy.9
  43.6 2.8 %convolution_convert_fusion.blocks_ref = bf16[64,8,1536]{2,1,0:T(8,128)(2,1)} fusion(bf16[256,512]{1,0:T(8,128)(2,1)} %bitcast.80, bf16[256,512]{1,0:T(8,128)(2,1)} %bitcast.78, bf16[256,512]{1,0:T(8,128)(2,1)} %bitcast.69, bf16[512,256]{1,0:T(8,128)(2,1)S(1)} %copy.9), kind=kOutput, calls=%fused_computation.9 | convolution fusion | flops 405798912 | bytes 2621440 | tf_op jit(solution)/shard_map/dot_general | solution.py:77
  46.4 51.7 %shard_map.51 = (f32[8,1536]{1,0:T(8,128)}, bf16[64,4,512]{2,1,0:T(4,128)(2,1)}) custom-call(bf16[64,8,1536]{2,1,0:T(8,128)(2,1)} %convolution_convert_fusion.blocks_ref, bf16[64,4,512]{2,1,0:T(4,128)(2,1)} %reshape_reshape.11.spread_ref), custom_call_target="tpu_custom_call" | custom-call | tf_op jit(solution)/shard_map/pallas_call | solution.py:413
  98.1 1.4 %broadcast_multiply_fusion = f32[8,1536]{1,0:T(8,128)} fusion(f32[8,1536]{1,0:T(8,128)} %get-tuple-element.17), kind=kLoop, calls=%fused_computation.46 | loop fusion | flops 12288 | bytes 98304 | tf_op jit(solution)/shard_map/div | solution.py:589
  99.6 1.7 %copy.22 = bf16[1,64,4,512]{3,2,1,0:T(4,128)(2,1)} copy(bf16[1,64,4,512]{3,2,1,0:T(4,128)(2,1)} %bitcast.72) | data formatting | bytes 524288
  (11 shorter events, 0.2 us)
Async XLA Ops:
  0.6 30.9 %copy-start = (bf16[512,1536]{1,0:T(8,128)(2,1)S(1)}, bf16[512,1536]{1,0:T(8,128)(2,1)}, u32[]{:S(2)}) copy-start(bf16[512,1536]{1,0:T(8,128)(2,1)} %param.4) | copy-start | bytes 4718596
  39.2 1.9 %copy-start.1 = (bf16[4,64,512]{2,1,0:T(8,128)(2,1)}, bf16[4,64,512]{2,1,0:T(8,128)(2,1)S(1)}, u32[]{:S(2)}) copy-start(bf16[4,64,512]{2,1,0:T(8,128)(2,1)S(1)} %multiply_convert_fusion.1) | copy-start | bytes 786436
  40.1 1.0 copy-start.2
  41.1 0.7 copy-start.3
